TPU v7x, 32 devices: a whole 2x2x4 slice. The times are simulated.
32 devices in a mesh: seq: 16 (over z, y, x), head: 2 (over core).
Axes of the slice: x: 2, y: 2, z: 4, core: 2. Of those that a mesh axis runs over, the one named last changes fastest.
Arguments:
- tokens: bfloat16 [2, 4096, 2048], P(None, 'seq'), may hold values from -6 to 6
- grad_out: bfloat16 [2, 4096, 2048], P(None, 'seq'), may hold values from -6 to 6
- query_weight: bfloat16 [2048, 2048], P('seq', 'head'), may hold values from -0.5 to 0.5
- key_weight: bfloat16 [2048, 2048], P('seq', 'head'), may hold values from -0.5 to 0.5
- value_weight: bfloat16 [2048, 2048], P('seq', 'head'), may hold values from -0.125 to 0.125
- forget_weight: bfloat16 [2048, 256], P('seq', 'head'), may hold values from -0.125 to 0.125
- forget_bias: bfloat16 [4, 64], P('head', 'seq'), as said below
- outgate_weight: bfloat16 [2048, 2048], P('seq', 'head'), may hold values from -0.125 to 0.125
- output_weight: bfloat16 [2048, 2048], P('head', 'seq'), may hold values from -0.125 to 0.125
- slot_gain: bfloat16 [512], P('seq'), may hold values from 0.5 to 1.5
- first_gain: bfloat16 [2048], P('seq'), may hold values from 0.5 to 1.5
- second_gain: bfloat16 [2048], P('seq'), may hold values from 0.5 to 1.5
- gate_weight: bfloat16 [2048, 5632], P('seq', 'head'), may hold values from -0.125 to 0.125
- up_weight: bfloat16 [2048, 5632], P('seq', 'head'), may hold values from -0.125 to 0.125
- down_weight: bfloat16 [5632, 2048], P('head', 'seq'), may hold values from -0.078125 to 0.078125
Outputs:
- output: bfloat16 [2, 4096, 2048], P(None, 'seq')
- input_grad: float32 [2, 4096, 2048], P(None, 'seq')
- query_grad: float32 [2048, 2048], P('seq', 'head')
- key_grad: float32 [2048, 2048], P('seq', 'head')
- value_grad: float32 [2048, 2048], P('seq', 'head')
- forget_grad: float32 [2048, 256], P('seq', 'head')
- forget_bias_grad: float32 [4, 64], P('head', 'seq')
- outgate_grad: float32 [2048, 2048], P('seq', 'head')
- output_grad: float32 [2048, 2048], P('head', 'seq')
- slot_gain_grad: float32 [512], P('seq')
- first_gain_grad: float32 [2048], P('seq')
- second_gain_grad: float32 [2048], P('seq')
- gate_grad: float32 [2048, 5632], P('seq', 'head')
- up_grad: float32 [2048, 5632], P('seq', 'head')
- down_grad: float32 [5632, 2048], P('head', 'seq')
Inputs may be any that keep to these rules, and one draw needn't show every extreme that they name: `forget_bias`: forget gate offsets of the heads and slots, those of per-token decay rates between 0.25 / 4096 and 1 / 30, so about 1 to 9.
All inputs are finite; a program needn't handle non-finite values.
Results may differ from a plain program's by a relative error of at most 0.01655.
Values may be sent and summed in bfloat16 or wider, within the bound.
A program may use at most 320 MiB of HBM per device.

v0:
```python
import jax
import jax.numpy as jnp
from jax import lax
from jax.sharding import PartitionSpec as P

HIGH = lax.Precision.HIGHEST
TAU = 8.0
EPS = 1e-06


def prefix_2(shard, axis, combine, identity):
    size, here = (lax.axis_size(axis), lax.axis_index(axis))
    everything = jax.tree.map(lambda part: lax.all_gather(part, axis), shard)
    start = jax.tree.map(
        lambda part, zero: jnp.broadcast_to(jnp.asarray(zero, part.dtype), part.shape),
        shard,
        identity,
    )

    def prefix_hop(k, before):
        reached = k < here
        new = combine(before, jax.tree.map(lambda part: part[k], everything))
        return jax.tree.map(lambda a, b: jnp.where(reached, a, b), new, before)

    return lax.fori_loop(0, size, prefix_hop, start)


def entering(shard, axis, combine, identity):
    size, here = (lax.axis_size(axis), lax.axis_index(axis))
    everything = jax.tree.map(
        lambda part, kind: lax.all_gather(part.astype(kind), axis),
        shard,
        jax.tree.map(lambda a: jnp.bfloat16 if a.dtype == jnp.float32 else a.dtype, shard),
    )
    start = jax.tree.map(
        lambda part, zero: jnp.broadcast_to(jnp.asarray(zero, part.dtype), part.shape),
        shard,
        identity,
    )

    def entering_hop(k, before):
        at = size - 1 - k
        reached = at > here
        new = combine(
            before, jax.tree.map(lambda part, own: part[at].astype(own.dtype), everything, shard)
        )
        return jax.tree.map(lambda a, b: jnp.where(reached, a, b), new, before)

    return lax.fori_loop(0, size, entering_hop, start)


def rms_scale(values, gain):
    return values * lax.rsqrt(jnp.mean(values * values, axis=-1, keepdims=True) + EPS) * gain


def out_gate(attended, gate, gain):
    return rms_scale(attended, gain) * jax.nn.silu(gate)


def swiglu(ff_gate, ff_up):
    return jax.nn.silu(ff_gate) * ff_up


def silu_slope(values):
    sig = jax.nn.sigmoid(values)
    return sig + values * sig * (1.0 - sig)


def slot_single(query, keys, values, log_decay, keys_in, values_in):
    count = query.shape[0]
    keep = -jnp.expm1(log_decay)
    total = jnp.cumsum(log_decay, axis=0)
    causal = (jnp.arange(count)[:, None] >= jnp.arange(count)[None, :])[:, :, None]
    spread = jnp.where(causal, total[:, None, :] - total[None, :, :], 0.0)
    mixing = jnp.where(causal, jnp.exp(spread), 0.0) * keep[None, :, :]
    scaled = query * query.shape[1] ** (-0.5)
    paired = jnp.dot(scaled, keys.T, precision=HIGH)
    growth = jnp.exp(total)
    scores = jnp.einsum("ts,tsi->ti", paired, mixing, precision=HIGH) + growth * jnp.dot(
        scaled, keys_in.T, precision=HIGH
    )
    probs = jax.nn.softmax(scores, axis=-1)
    weights = jnp.einsum("ti,tsi->ts", probs, mixing, precision=HIGH)
    return jnp.dot(weights, values, precision=HIGH) + jnp.dot(
        probs * growth, values_in, precision=HIGH
    )


def slot_end(keys, values, log_decay):
    total = jnp.cumsum(log_decay, axis=0)
    last = total[-1]
    weight = jnp.exp(last[None, :] - total) * -jnp.expm1(log_decay)
    return (
        jnp.exp(last),
        jnp.dot(weight.T, keys, precision=HIGH),
        jnp.dot(weight.T, values, precision=HIGH),
    )


def heads_attend(query, keys, values, log_decay, keys_in, values_in):

    def one_head(parts):
        return jax.vmap(slot_single)(parts[0], parts[1], parts[2], parts[3], parts[4], parts[5])

    stacked = (
        jnp.moveaxis(query, 2, 0),
        jnp.moveaxis(keys, 2, 0),
        jnp.moveaxis(values, 2, 0),
        jnp.moveaxis(log_decay, 2, 0),
        jnp.moveaxis(keys_in, 1, 0),
        jnp.moveaxis(values_in, 1, 0),
    )
    return jnp.moveaxis(lax.map(jax.checkpoint(one_head), stacked), 0, 2)


def heads_end(keys, values, log_decay):
    inner = jax.vmap(slot_end, in_axes=(1, 1, 1), out_axes=0)
    return jax.vmap(inner, in_axes=(0, 0, 0), out_axes=0)(keys, values, log_decay)


def carry_combine(earlier, later):
    return (
        earlier[0] * later[0],
        later[1] + later[0][..., None] * earlier[1],
        later[2] + later[0][..., None] * earlier[2],
    )


def matmul(left, right):
    return jnp.dot(left, right, preferred_element_type=jnp.float32)


def outer_sum(left, right):
    return jnp.einsum("bti,btj->ij", left, right, preferred_element_type=jnp.float32)


def back_product(grad, weight):
    return jnp.einsum("btj,ij->bti", grad, weight, preferred_element_type=jnp.float32)


def shards(
    tokens,
    grad_out,
    query_weight,
    key_weight,
    value_weight,
    forget_weight,
    forget_bias,
    outgate_weight,
    output_weight,
    slot_gain,
    first_gain,
    second_gain,
    gate_weight,
    up_weight,
    down_weight,
):
    full = (
        lax.all_gather(query_weight, "seq", axis=0, tiled=True),
        lax.all_gather(key_weight, "seq", axis=0, tiled=True),
        lax.all_gather(value_weight, "seq", axis=0, tiled=True),
        lax.all_gather(forget_weight, "seq", axis=0, tiled=True),
        lax.all_gather(forget_bias, "seq", axis=1, tiled=True),
        lax.all_gather(outgate_weight, "seq", axis=0, tiled=True),
        lax.all_gather(output_weight, "seq", axis=1, tiled=True),
        lax.all_gather(slot_gain, "seq", axis=0, tiled=True),
        lax.all_gather(first_gain, "seq", axis=0, tiled=True),
        lax.all_gather(second_gain, "seq", axis=0, tiled=True),
        lax.all_gather(gate_weight, "seq", axis=0, tiled=True),
        lax.all_gather(up_weight, "seq", axis=0, tiled=True),
        lax.all_gather(down_weight, "seq", axis=1, tiled=True),
    )
    query_full = full[0]
    key_full = full[1]
    value_full = full[2]
    forget_full = full[3]
    bias_full = full[4]
    outgate_full = full[5]
    output_full = full[6]
    slot_full = full[7]
    first_full = full[8]
    second_full = full[9]
    gate_full = full[10]
    up_full = full[11]
    down_full = full[12]
    seqs = tokens.shape[0]
    rows = tokens.shape[1]
    heads_here = bias_full.shape[0]
    slots = bias_full.shape[1]
    head_dim = slot_full.shape[0]

    def split_heads(array, inner):
        return array.reshape(seqs, rows, heads_here, inner)

    def join_heads(array):
        return array.reshape(seqs, rows, heads_here * array.shape[3])

    inputs = tokens.astype(jnp.float32)
    normed_one, first_back = jax.vjp(rms_scale, inputs, first_full.astype(jnp.float32))
    normed_one_low = normed_one.astype(jnp.bfloat16)
    query_low = matmul(normed_one_low, query_full).astype(jnp.bfloat16)
    key_low = matmul(normed_one_low, key_full).astype(jnp.bfloat16)
    value_low = matmul(normed_one_low, value_full).astype(jnp.bfloat16)
    forget_logit = matmul(normed_one_low, forget_full) + bias_full.astype(jnp.float32).reshape(
        heads_here * slots
    )
    outgate_pre = matmul(normed_one_low, outgate_full)
    log_decay = split_heads(-jax.nn.softplus(-forget_logit) / TAU, slots)
    query_wide = split_heads(query_low.astype(jnp.float32), head_dim)
    key_wide = split_heads(key_low.astype(jnp.float32), head_dim)
    value_wide = split_heads(value_low.astype(jnp.float32), head_dim)
    query_feat = jax.nn.silu(query_wide)
    key_feat = jax.nn.silu(key_wide)
    decay, local_keys, local_values = heads_end(key_feat, value_wide, log_decay)
    prefix = prefix_2(
        (decay, local_keys, local_values),
        "seq",
        carry_combine,
        (jnp.ones_like(decay), jnp.zeros_like(local_keys), jnp.zeros_like(local_values)),
    )
    keys_in = prefix[1]
    values_in = prefix[2]
    attended, attend_back = jax.vjp(
        heads_attend, query_feat, key_feat, value_wide, log_decay, keys_in, values_in
    )
    gated, gate_back = jax.vjp(
        out_gate, attended, split_heads(outgate_pre, head_dim), slot_full.astype(jnp.float32)
    )
    gated_low = join_heads(gated).astype(jnp.bfloat16)
    mixed = lax.psum(matmul(gated_low, output_full), "head")
    residual = inputs + mixed
    normed_two, second_back = jax.vjp(rms_scale, residual, second_full.astype(jnp.float32))
    normed_two_low = normed_two.astype(jnp.bfloat16)
    ff_gate = matmul(normed_two_low, gate_full)
    ff_up = matmul(normed_two_low, up_full)
    activated_wide, swiglu_back = jax.vjp(swiglu, ff_gate, ff_up)
    activated = activated_wide.astype(jnp.bfloat16)
    ff_out = lax.psum(matmul(activated, down_full).astype(jnp.bfloat16), "head").astype(jnp.float32)
    output = (residual + ff_out).astype(jnp.bfloat16)
    again = (
        lax.all_gather(query_weight, "seq", axis=0, tiled=True),
        lax.all_gather(key_weight, "seq", axis=0, tiled=True),
        lax.all_gather(value_weight, "seq", axis=0, tiled=True),
        lax.all_gather(forget_weight, "seq", axis=0, tiled=True),
        lax.all_gather(forget_bias, "seq", axis=1, tiled=True),
        lax.all_gather(outgate_weight, "seq", axis=0, tiled=True),
        lax.all_gather(output_weight, "seq", axis=1, tiled=True),
        lax.all_gather(slot_gain, "seq", axis=0, tiled=True),
        lax.all_gather(first_gain, "seq", axis=0, tiled=True),
        lax.all_gather(second_gain, "seq", axis=0, tiled=True),
        lax.all_gather(gate_weight, "seq", axis=0, tiled=True),
        lax.all_gather(up_weight, "seq", axis=0, tiled=True),
        lax.all_gather(down_weight, "seq", axis=1, tiled=True),
    )
    query_back = again[0]
    key_back = again[1]
    value_back = again[2]
    forget_back = again[3]
    outgate_back = again[5]
    output_back = again[6]
    gate_back_weight = again[10]
    up_back = again[11]
    down_back = again[12]
    down_grad = outer_sum(activated, grad_out)
    act_grad = back_product(grad_out, down_back)
    gate_wide, up_wide = swiglu_back(act_grad)
    gate_term = gate_wide.astype(jnp.bfloat16)
    up_term = up_wide.astype(jnp.bfloat16)
    gate_grad = outer_sum(normed_two_low, gate_term)
    up_grad = outer_sum(normed_two_low, up_term)
    normed_two_grad = back_product(gate_term, gate_back_weight) + back_product(up_term, up_back)
    normed_two_grad = lax.psum(normed_two_grad.astype(jnp.bfloat16), "head").astype(jnp.float32)
    residual_from_norm, second_gain_grad = second_back(normed_two_grad)
    residual_grad = grad_out.astype(jnp.float32) + residual_from_norm
    residual_low = residual_grad.astype(jnp.bfloat16)
    output_grad = outer_sum(gated_low, residual_low)
    gated_grad = split_heads(back_product(residual_low, output_back), head_dim)
    attended_grad, outgate_wide, slot_gain_grad = gate_back(gated_grad)
    outgate_term = join_heads(outgate_wide).astype(jnp.bfloat16)
    query_part, key_part, value_part, decay_part, keys_in_grad, values_in_grad = attend_back(
        attended_grad
    )
    suffix = entering(
        (decay, keys_in_grad, values_in_grad),
        "seq",
        carry_combine,
        (jnp.ones_like(decay), jnp.zeros_like(keys_in_grad), jnp.zeros_like(values_in_grad)),
    )
    decay_cot = jnp.sum(suffix[1] * keys_in + suffix[2] * values_in, axis=-1)
    ends, end_back = jax.vjp(heads_end, key_feat, value_wide, log_decay)
    key_extra, value_extra, decay_extra = end_back((decay_cot, suffix[1], suffix[2]))
    query_term = join_heads(query_part * silu_slope(query_wide)).astype(jnp.bfloat16)
    key_term = join_heads((key_part + key_extra) * silu_slope(key_wide)).astype(jnp.bfloat16)
    value_term = join_heads(value_part + value_extra).astype(jnp.bfloat16)
    forget_term = (
        join_heads(decay_part + decay_extra) * jax.nn.sigmoid(-forget_logit) / TAU
    ).astype(jnp.bfloat16)
    bias_grad = jnp.sum(forget_term.astype(jnp.float32), axis=(0, 1)).reshape(heads_here, slots)
    query_grad = outer_sum(normed_one_low, query_term)
    key_grad = outer_sum(normed_one_low, key_term)
    value_grad = outer_sum(normed_one_low, value_term)
    forget_grad = outer_sum(normed_one_low, forget_term)
    outgate_grad = outer_sum(normed_one_low, outgate_term)
    normed_one_grad = (
        back_product(query_term, query_back)
        + back_product(key_term, key_back)
        + back_product(value_term, value_back)
        + back_product(forget_term, forget_back)
        + back_product(outgate_term, outgate_back)
    )
    normed_one_grad, slot_gain_grad = (
        lax.psum(normed_one_grad.astype(jnp.bfloat16), "head").astype(jnp.float32),
        lax.psum(slot_gain_grad.astype(jnp.bfloat16), "head").astype(jnp.float32),
    )
    input_from_norm, first_gain_grad = first_back(normed_one_grad)
    input_grad = residual_grad + input_from_norm
    summed = (
        lax.psum_scatter(query_grad, "seq", scatter_dimension=0, tiled=True),
        lax.psum_scatter(key_grad, "seq", scatter_dimension=0, tiled=True),
        lax.psum_scatter(value_grad, "seq", scatter_dimension=0, tiled=True),
        lax.psum_scatter(forget_grad, "seq", scatter_dimension=0, tiled=True),
        lax.psum_scatter(bias_grad, "seq", scatter_dimension=1, tiled=True),
        lax.psum_scatter(outgate_grad, "seq", scatter_dimension=0, tiled=True),
        lax.psum_scatter(output_grad, "seq", scatter_dimension=1, tiled=True),
        lax.psum_scatter(slot_gain_grad, "seq", scatter_dimension=0, tiled=True),
        lax.psum_scatter(first_gain_grad, "seq", scatter_dimension=0, tiled=True),
        lax.psum_scatter(second_gain_grad, "seq", scatter_dimension=0, tiled=True),
        lax.psum_scatter(gate_grad, "seq", scatter_dimension=0, tiled=True),
        lax.psum_scatter(up_grad, "seq", scatter_dimension=0, tiled=True),
        lax.psum_scatter(down_grad, "seq", scatter_dimension=1, tiled=True),
    )
    return (
        output,
        input_grad,
        summed[0],
        summed[1],
        summed[2],
        summed[3],
        summed[4],
        summed[5],
        summed[6],
        summed[7],
        summed[8],
        summed[9],
        summed[10],
        summed[11],
        summed[12],
    )


def solution(mesh):
    return jax.shard_map(
        shards,
        mesh=mesh,
        in_specs=(
            P(None, "seq", None),
            P(None, "seq", None),
            P("seq", "head"),
            P("seq", "head"),
            P("seq", "head"),
            P("seq", "head"),
            P("head", "seq"),
            P("seq", "head"),
            P("head", "seq"),
            P("seq"),
            P("seq"),
            P("seq"),
            P("seq", "head"),
            P("seq", "head"),
            P("head", "seq"),
        ),
        out_specs=(
            P(None, "seq", None),
            P(None, "seq", None),
            P("seq", "head"),
            P("seq", "head"),
            P("seq", "head"),
            P("seq", "head"),
            P("head", "seq"),
            P("seq", "head"),
            P("head", "seq"),
            P("seq"),
            P("seq"),
            P("seq"),
            P("seq", "head"),
            P("seq", "head"),
            P("head", "seq"),
        ),
        check_vma=False,
    )
```

profile of v0, /device:TPU:0, one launch (start us, length us, event | category | flops | bytes accessed | tf_op | source)
XLA Modules:
  0.0 4296.1 jit_solution(4325084734223197280)
XLA Ops:
  9.4 42.4 all-gather.6
  52.7 35.9 all-gather.7
  91.1 41.8 all_gather.83
  144.7 5.9 fusion.188
  158.4 11.9 all-gather.26.cloned.1.call-done
  182.1 39.8 all-reduce.1
  222.5 36.4 all-gather.1
  266.1 5.9 fusion.182
  282.2 81.0 %all-gather.38.cloned.1.call-done = f32[32,2,64,512]{3,2,1,0:T(8,128)} async-done(((f32[2,2,64,512]{3,2,1,0:T(8,128)}), f32[32,2,64,512]{3,2,1,0:T(8,128)}) %all-gather.38.cloned.1.call-update) | async-done | bytes 8388624 | tf_op jit(solution)/shard_map/all_gather | solution.py:13
  363.2 114.2 %all-gather.40.cloned.1.call-done = f32[32,2,64,512]{3,2,1,0:T(8,128)} async-done(((f32[2,2,64,512]{3,2,1,0:T(8,128)}), f32[32,2,64,512]{3,2,1,0:T(8,128)}) %all-gather.40.cloned.1.call-update) | async-done | bytes 8388624 | tf_op jit(solution)/shard_map/all_gather | solution.py:13
  477.5 23.7 while.74
  504.4 167.8 %while.73 = (s32[]{:T(128)}, f32[2,2,256,512]{2,3,0,1:T(8,128)}, f32[2,2,256,512]{3,2,1,0:T(8,128)S(1)}, f32[2,2,256,512]{3,2,1,0:T(8,128)}, f32[2,2,256,64]{2,3...) while((s32[]{:T(128)}, f32[2,2,256,512]{2,3,0,1:T(8,128)}, ...), condition=%wide.region_10.11_spmd.clone.clone, body=%wide.region_5.10_spmd.clone.clone.sunk | while | flops 2287010304 | bytes 27807444 | solution.py:113
  527.2 34.6 fusion.402
  566.1 24.2 fusion.407
  602.0 34.6 fusion.402
  640.8 24.2 fusion.407
  674.0 7.9 multiply_convert_fusion.3
  682.0 7.0 fusion.142
  690.3 37.5 all-gather.8
  727.9 100.7 %all-gather.36.cloned.1.call-done = bf16[2816,2048]{1,0:T(8,128)(2,1)} async-done(((bf16[2816,128]{1,0:T(8,128)(2,1)}), bf16[2816,2048]{1,0:T(8,128)(2,1)}) %all-gather.36.cloned.1.call-update) | async-done | bytes 11534352 | tf_op jit(solution)/shard_map/all_gather | solution.py:171
  828.6 12.7 fusion.112
  841.3 17.0 all-reduce.12.cloned.1.call-done
  865.7 139.0 %all-gather.34.cloned.1.call-done = bf16[2048,2816]{1,0:T(8,128)(2,1)} async-done(((bf16[128,2816]{1,0:T(8,128)(2,1)}), bf16[2048,2816]{1,0:T(8,128)(2,1)}) %all-gather.34.cloned.1.call-update) | async-done | bytes 11534352 | tf_op jit(solution)/shard_map/all_gather | solution.py:170
  1004.7 12.5 fusion.118
  1017.2 131.0 %all-gather.32.cloned.1.call-done = bf16[2048,2816]{1,0:T(8,128)(2,1)} async-done(((bf16[128,2816]{1,0:T(8,128)(2,1)}), bf16[2048,2816]{1,0:T(8,128)(2,1)}) %all-gather.32.cloned.1.call-update) | async-done | bytes 11534352 | tf_op jit(solution)/shard_map/all_gather | solution.py:169
  1148.2 16.6 fusion.126
  1164.8 9.2 fusion.116
  1174.0 12.6 add_convert_fusion.1
  1186.7 19.5 all-reduce.14.cloned.1.call-done
  1230.0 367.7 %while.72 = (s32[]{:T(128)}, f32[2,2,256,512]{2,3,0,1:T(8,128)}, f32[2,2,256,512]{2,3,0,1:T(8,128)}, f32[2,2,256,512]{2,3,0,1:T(8,128)}, f32[2,2,256,64]{2,3,1,0...) while((s32[]{:T(128)}, f32[2,2,256,512]{2,3,0,1:T(8,128)}, ...), condition=%wide.region_29.30_spmd, body=%wide.region_18.29_spmd.sunk | while | flops 5497390080 | bytes 115728032 | solution.py:113
  1250.4 34.8 fusion.380
  1288.9 35.2 fusion.376
  1339.1 27.5 fusion.386
  1370.3 6.4 reduce-window.100
  1379.6 21.3 multiply_reduce_fusion.9
  1430.8 34.8 fusion.380
  1469.4 35.4 fusion.376
  1519.8 27.5 fusion.386
  1551.0 6.4 reduce-window.100
  1560.2 21.0 multiply_reduce_fusion.9
  1598.4 41.4 all-gather.5
  1639.8 10.9 fusion.162
  1663.3 11.9 all-gather.42.cloned.1.call-done
  1679.9 72.6 %all-gather.44.cloned.1.call-done = bf16[32,2,64,512]{3,2,0,1:T(8,128)(2,1)} async-done(((bf16[2,2,64,512]{3,2,0,1:T(8,128)(2,1)}), bf16[32,2,64,512]{3,2,0,1:T(8,128)(2,1)}) %all-gather.44.cloned.1.call-update) | async-done | bytes 4194320 | tf_op jit(solution)/shard_map/all_gather | solution.py:31
  1757.1 21.8 while.75
  1791.1 10.9 reduce-window.80
  1829.4 8.6 convolution_bitcast_fusion.8
  1839.2 6.1 convolution_bitcast_fusion.12
  1846.6 6.0 convolution_bitcast_fusion.9
  1853.8 6.0 convolution_bitcast_fusion.11
  1861.0 5.9 convolution_bitcast_fusion.10
  1867.0 13.0 convolution_bitcast_fusion.7
  1880.1 13.0 convolution_bitcast_fusion.6
  1893.2 13.0 convolution_bitcast_fusion.5
  1914.1 79.1 %all-reduce.6 = (f32[2,64]{1,0:T(2,128)S(1)}, f32[512]{0:T(512)S(1)}, f32[2048]{0:T(1024)S(1)}, f32[2048]{0:T(1024)S(1)}) all-reduce(f32[2,64]{1,0:T(2,128)S(1)} %reshape.331, bf16[512]{0:T(512)(128)(2,1)S(1)} %psum.39, f32[2048]{0:T(1024)S(1)} %get-tuple-element.1070, ...), channel_id=12, replica_groups=mesh['seq'=16,'head'=2] {'seq'}, use_global_device_ids=true, to_apply=%region_43.44.clone | all-reduce | flops 4736 | bytes 36864
  1995.5 7.3 fusion.137
  2002.9 110.5 %reduce-scatter.21.cloned.1.call-done = f32[1024,128]{1,0:T(8,128)} async-done(((f32[1024,2048]{1,0:T(8,128)}), f32[1024,128]{1,0:T(8,128)}) %reduce-scatter.21.cloned.1.call-update) | async-done | bytes 524304 | tf_op jit(solution)/shard_map/reduce_scatter | solution.py:324
  2113.4 182.8 %reduce-scatter.11.cloned.1.call-done = f32[128,1024]{1,0:T(8,128)} async-done(((f32[2048,1024]{1,0:T(8,128)}), f32[128,1024]{1,0:T(8,128)}) %reduce-scatter.11.cloned.1.call-update) | async-done | bytes 524304 | tf_op jit(solution)/shard_map/reduce_scatter | solution.py:318
  2296.2 183.1 %reduce-scatter.19.cloned.1.call-done = f32[128,1024]{1,0:T(8,128)} async-done(((f32[2048,1024]{1,0:T(8,128)}), f32[128,1024]{1,0:T(8,128)}) %reduce-scatter.19.cloned.1.call-update) | async-done | bytes 524304 | tf_op jit(solution)/shard_map/reduce_scatter | solution.py:323
  2479.4 183.0 %reduce-scatter.13.cloned.1.call-done = f32[128,1024]{1,0:T(8,128)} async-done(((f32[2048,1024]{1,0:T(8,128)}), f32[128,1024]{1,0:T(8,128)}) %reduce-scatter.13.cloned.1.call-update) | async-done | bytes 524304 | tf_op jit(solution)/shard_map/reduce_scatter | solution.py:319
  2662.3 183.1 %reduce-scatter.15.cloned.1.call-done = f32[128,1024]{1,0:T(8,128)} async-done(((f32[2048,1024]{1,0:T(8,128)}), f32[128,1024]{1,0:T(8,128)}) %reduce-scatter.15.cloned.1.call-update) | async-done | bytes 524304 | tf_op jit(solution)/shard_map/reduce_scatter | solution.py:320
  2845.5 478.3 %reduce-scatter.23.cloned.1.call-done = f32[128,2816]{1,0:T(8,128)} async-done(((f32[2048,2816]{1,0:T(8,128)}), f32[128,2816]{1,0:T(8,128)}) %reduce-scatter.23.cloned.1.call-update) | async-done | bytes 1441808 | tf_op jit(solution)/shard_map/reduce_scatter | solution.py:328
  3323.8 482.7 %reduce-scatter.25.cloned.1.call-done = f32[128,2816]{1,0:T(8,128)} async-done(((f32[2048,2816]{1,0:T(8,128)}), f32[128,2816]{1,0:T(8,128)}) %reduce-scatter.25.cloned.1.call-update) | async-done | bytes 1441808 | tf_op jit(solution)/shard_map/reduce_scatter | solution.py:329
  3806.5 482.5 %reduce-scatter.27.cloned.1.call-done = f32[2816,128]{1,0:T(8,128)} async-done(((f32[2816,2048]{1,0:T(8,128)}), f32[2816,128]{1,0:T(8,128)}) %reduce-scatter.27.cloned.1.call-update) | async-done | bytes 1441808 | tf_op jit(solution)/shard_map/reduce_scatter | solution.py:330
  (540 shorter events, 352.1 us)
Async XLA Ops:
  7.2 137.5 %all-gather.24.cloned.1.call-start = ((), (), s32[]{:S(2)}) async-start(), calls=%async_computation.10 | async-start | bytes 4456448 | tf_op jit(solution)/shard_map/all_gather | solution.py:160
  7.9 162.4 %all-gather.26.cloned.1.call-start = ((), (), s32[]{:S(2)}) async-start(), calls=%async_computation.11 | async-start | bytes 4456448 | tf_op jit(solution)/shard_map/all_gather | solution.py:161
  8.7 257.4 %all-gather.22.cloned.1.call-start = ((), (), s32[]{:S(2)}) async-start(), calls=%async_computation.9 | async-start | bytes 4456448 | tf_op jit(solution)/shard_map/all_gather | solution.py:159
  9.4 353.8 %all-gather.38.cloned.1.call-start = ((), (), s32[]{:S(2)}) async-start(), calls=%async_computation.28 | async-start | bytes 8912896 | tf_op jit(solution)/shard_map/all_gather | solution.py:13
  51.8 214.3 %copy-start.60 = (f32[16,1,128]{2,1,0:T(1,128)}, f32[16,1,128]{2,1,0:T(1,128)S(1)}, u32[]{:S(2)}) copy-start(f32[16,1,128]{2,1,0:T(1,128)S(1)} %convert_element_type.218) | copy-start | bytes 24580
  91.1 48.3 %copy-start.69 = (f32[2,256]{1,0:T(2,128)}, f32[2,256]{1,0:T(2,128)S(1)}, u32[]{:S(2)}) copy-start(f32[2,256]{1,0:T(2,128)S(1)} %fusion.138) | copy-start | bytes 6148
  91.1 175.0 %copy-start.67 = (f32[2,256]{1,0:T(2,128)}, f32[2,256]{1,0:T(2,128)S(1)}, u32[]{:S(2)}) copy-start(f32[2,256]{1,0:T(2,128)S(1)} %fusion.220) | copy-start | bytes 6148
  136.4 14.2 copy-start.42
  136.4 8.3 copy-start.9
  139.6 11.0 copy-start.24
  139.9 10.7 copy-start.26
  158.3 17.5 copy-start.43
  158.3 22.2 copy-start.72
  158.4 23.5 copy-start.78
  158.4 319.1 %all-gather.40.cloned.1.call-start = ((), (), s32[]{:S(2)}) async-start(), calls=%async_computation.29 | async-start | bytes 8912896 | tf_op jit(solution)/shard_map/all_gather | solution.py:13
  177.4 496.7 %all-gather.28.cloned.1.call-start = ((), (), s32[]{:S(2)}) async-start(), calls=%async_computation.12 | async-start | bytes 4456448 | tf_op jit(solution)/shard_map/all_gather | solution.py:164
  177.9 504.0 %all-gather.30.cloned.1.call-start = ((), (), s32[]{:S(2)}) async-start(), calls=%async_computation.13 | async-start | bytes 4456448 | tf_op jit(solution)/shard_map/all_gather | solution.py:165
  178.7 649.9 %all-gather.36.cloned.1.call-start = ((), (), s32[]{:S(2)}) async-start(), calls=%async_computation.17 | async-start | bytes 12255232 | tf_op jit(solution)/shard_map/all_gather | solution.py:171
  179.4 678.9 %all-reduce.12.cloned.1.call-start = ((), (), s32[]{:S(2)}) async-start(), calls=%async_computation.14 | async-start | bytes 8388608 | tf_op jit(solution)/shard_map/psum | solution.py:230
  504.4 169.6 %copy-start.61 = (f32[16,1,128]{2,1,0:T(1,128)S(1)}, f32[16,1,128]{2,1,0:T(1,128)}, u32[]{:S(2)}) copy-start(f32[16,1,128]{2,1,0:T(1,128)} %copy-done.60) | copy-start | bytes 24580
  527.2 34.6 copy-start.41
  527.2 38.9 copy-start.36
  566.1 26.4 copy-start.4
  602.0 34.6 copy-start.41
  602.0 38.9 copy-start.36
  640.8 26.4 copy-start.4
  682.0 7.0 copy-start.28
  689.0 315.7 %all-gather.34.cloned.1.call-start = ((), (), s32[]{:S(2)}) async-start(), calls=%async_computation.16 | async-start | bytes 12255232 | tf_op jit(solution)/shard_map/all_gather | solution.py:170
  689.6 458.6 %all-gather.32.cloned.1.call-start = ((), (), s32[]{:S(2)}) async-start(), calls=%async_computation.15 | async-start | bytes 12255232 | tf_op jit(solution)/shard_map/all_gather | solution.py:169
  690.3 515.9 %all-reduce.14.cloned.1.call-start = ((), (), s32[]{:S(2)}) async-start(), calls=%async_computation.18 | async-start | bytes 4194304 | tf_op jit(solution)/shard_map/psum | solution.py:272
  1148.2 16.6 copy-start.74
  1164.8 9.2 copy-start.81
  1186.6 488.6 %all-gather.42.cloned.1.call-start = ((), (), s32[]{:S(2)}) async-start(), calls=%async_computation.30 | async-start | bytes 4456448 | tf_op jit(solution)/shard_map/all_gather | solution.py:31
  1206.2 4.9 copy-start.3
  1206.2 4.9 copy-start.32
  1230.4 6.0 copy-start.15
  1325.9 6.7 copy-start.55
  1379.6 21.3 copy-start.33
  1379.6 23.2 copy-start.47
  1410.9 6.0 copy-start.15
  1506.6 6.7 copy-start.55
  1560.2 21.0 copy-start.33
  1560.2 22.9 copy-start.47
  1597.8 154.7 %all-gather.44.cloned.1.call-start = ((), (), s32[]{:S(2)}) async-start(), calls=%async_computation.31 | async-start | bytes 4456448 | tf_op jit(solution)/shard_map/all_gather | solution.py:31
  1598.3 312.5 %all-reduce.16.cloned.1.call-start = ((), (), s32[]{:S(2)}) async-start(), calls=%async_computation.32 | async-start | bytes 8388608 | tf_op jit(solution)/shard_map/psum | solution.py:238
  1639.8 10.9 copy-start.53
  1639.8 11.9 copy-start.23
  1654.2 4.8 copy-start.51
  1803.1 6.8 copy-start.44
  1809.9 4.9 copy-start.35
  1809.9 6.8 copy-start.54
  1809.9 6.8 copy-start.59
  1814.7 5.0 copy-start.79
  1825.8 177.1 %reduce-scatter.17.cloned.1.call-start = ((), (), s32[]{:S(2)}) async-start(), calls=%async_computation.22 | async-start | bytes 1114112 | tf_op jit(solution)/shard_map/reduce_scatter | solution.py:321
  1829.4 284.1 %reduce-scatter.21.cloned.1.call-start = ((), (), s32[]{:S(2)}) async-start(), calls=%async_computation.24 | async-start | bytes 8912896 | tf_op jit(solution)/shard_map/reduce_scatter | solution.py:324
  1838.0 458.2 %reduce-scatter.11.cloned.1.call-start = ((), (), s32[]{:S(2)}) async-start(), calls=%async_computation.19 | async-start | bytes 8912896 | tf_op jit(solution)/shard_map/reduce_scatter | solution.py:318
  1845.4 634.0 %reduce-scatter.19.cloned.1.call-start = ((), (), s32[]{:S(2)}) async-start(), calls=%async_computation.23 | async-start | bytes 8912896 | tf_op jit(solution)/shard_map/reduce_scatter | solution.py:323
  1852.6 809.7 %reduce-scatter.13.cloned.1.call-start = ((), (), s32[]{:S(2)}) async-start(), calls=%async_computation.20 | async-start | bytes 8912896 | tf_op jit(solution)/shard_map/reduce_scatter | solution.py:319
  1859.8 985.7 %reduce-scatter.15.cloned.1.call-start = ((), (), s32[]{:S(2)}) async-start(), calls=%async_computation.21 | async-start | bytes 8912896 | tf_op jit(solution)/shard_map/reduce_scatter | solution.py:320
  1866.9 1456.9 %reduce-scatter.23.cloned.1.call-start = ((), (), s32[]{:S(2)}) async-start(), calls=%async_computation.25 | async-start | bytes 24510464 | tf_op jit(solution)/shard_map/reduce_scatter | solution.py:328
  1880.0 1926.5 %reduce-scatter.25.cloned.1.call-start = ((), (), s32[]{:S(2)}) async-start(), calls=%async_computation.26 | async-start | bytes 24510464 | tf_op jit(solution)/shard_map/reduce_scatter | solution.py:329
  1893.1 2395.9 %reduce-scatter.27.cloned.1.call-start = ((), (), s32[]{:S(2)}) async-start(), calls=%async_computation.27 | async-start | bytes 24510464 | tf_op jit(solution)/shard_map/reduce_scatter | solution.py:330
  1906.2 7.9 copy-start.65
  1906.2 89.3 %copy-start.70 = (f32[2,256]{1,0:T(2,128)S(1)}, f32[2,256]{1,0:T(2,128)}, u32[]{:S(2)}) copy-start(f32[2,256]{1,0:T(2,128)} %copy-done.69) | copy-start | bytes 6148
  (61 other events, 158.5 us)
Sparse Core Ops, SparseCore 0:
  10.8 81.2 all-gather.23
  94.8 75.4 all-gather.25
  173.1 75.3 all-gather.21
  251.7 111.4 all-gather.37
  366.4 111.0 all-gather.39
  480.1 74.2 all-gather.27
  557.2 87.8 all-gather.29
  647.7 180.8 all-gather.35
  831.7 26.6 all-reduce.11
  861.3 143.3 all-gather.33
  1007.8 140.3 all-gather.31
  1186.8 19.3 all-reduce.13
  1597.9 77.2 all-gather.41
  1677.8 74.6 all-gather.43
  1825.9 27.1 all-reduce.15
  1855.9 79.0 reduce-scatter.16
  1937.7 175.7 reduce-scatter.20
  2116.1 180.0 reduce-scatter.10
  2299.1 180.2 reduce-scatter.18
  2482.1 180.2 reduce-scatter.12
  2665.2 180.2 reduce-scatter.14
  2848.4 475.4 reduce-scatter.22
  3326.7 479.7 reduce-scatter.24
  3809.2 479.7 reduce-scatter.26
where the time goes:
time: 4310 us; the launch traced here: 4300 us
  waiting for transfers between devices  2990 us (69%)
  matrix products  532 us (12%)
  blocking collectives  357 us (8%)
  other arithmetic  246 us (6%)
  local copies, waits for them, and re-layouts  123 us (3%)
    reduce_scatter x1, waiting for transfers between devices, shards(): lax.psum_scatter(up_grad, 'seq', scatter_dimension=0, tiled=True)  483 us
    reduce_scatter x1, waiting for transfers between devices, shards(): lax.psum_scatter(down_grad, 'seq', scatter_dimension=1, tiled=True)  483 us
    reduce_scatter x1, waiting for transfers between devices, shards(): lax.psum_scatter(gate_grad, 'seq', scatter_dimension=0, tiled=True)  478 us
    all_gather x2, waiting for transfers between devices, prefix_2(): everything = jax.tree.map(lambda part: lax.all_gather(part, axis), shard)  195 us
    reduce_scatter x1, waiting for transfers between devices, shards(): lax.psum_scatter(value_grad, 'seq', scatter_dimension=0, tiled=True)  183 us
    reduce_scatter x1, waiting for transfers between devices, shards(): lax.psum_scatter(outgate_grad, 'seq', scatter_dimension=0, tiled=True)  183 us
    reduce_scatter x1, waiting for transfers between devices, shards(): lax.psum_scatter(key_grad, 'seq', scatter_dimension=0, tiled=True)  183 us
    reduce_scatter x1, waiting for transfers between devices, shards(): lax.psum_scatter(query_grad, 'seq', scatter_dimension=0, tiled=True)  183 us
  transfers between devices with their start and end apart: 24, of which 18 were waited for; matrix products, arithmetic and copies ran while one was open for 9% of the time, Pallas kernels for 0%

commit v1 on v0

v1 whole, which is shorter than its diff:
```python
import functools

import jax
import jax.numpy as jnp
import numpy as np
from jax import lax
from jax.experimental import pallas as pl
from jax.experimental.pallas import tpu as pltpu
from jax.sharding import PartitionSpec as P

F32, BF16 = jnp.float32, jnp.bfloat16
MESH = pl.DeviceIdType.MESH
HBM = pltpu.HBM
EPS = 1e-06
TAU = 8.0


CHUNK = 256
NT = (((1,), (1,)), ((), ()))
NN = (((1,), (0,)), ((), ()))
TN = (((0,), (0,)), ((), ()))


def decay_tables(count):
    at = np.arange(count)
    paths, masks = [], []
    half = count // 2
    while half >= 1:
        block, second = at // (2 * half), (at // half) % 2 == 1
        edge = block * 2 * half + half - 1
        r, t = at[None, :], at[:, None]
        fore = second[:, None] & (r > edge[:, None]) & (r <= t)
        back = ~second[:, None] & (r > t) & (r <= edge[:, None])
        paths.append(fore | back)
        masks.append((block[:, None] == block[None, :]) & second[:, None] & ~second[None, :])
        half //= 2
    paths.append(at[None, :] <= at[:, None])
    paths.append(at[None, :] > at[:, None])
    return np.concatenate(paths, 0), np.stack(masks)


def bf(x):
    return x.astype(BF16)


def halves(x):
    hi = bf(x)
    return hi, bf(x - hi.astype(F32))


def mm(a, b, dims):
    return lax.dot_general(a, b, dims, preferred_element_type=F32)


def dot3(a, b, dims):
    return mm(a[0], b[0], dims) + (mm(a[0], b[1], dims) + mm(a[1], b[0], dims))


def exact_sums(table, x):
    hi, mid = halves(x)
    low = bf(x - hi.astype(F32) - mid.astype(F32))
    n = x.shape[1]
    both = mm(table, jnp.concatenate([hi, mid, low, jnp.zeros_like(low)], axis=1), NN)
    return both[:, :n] + (both[:, n : 2 * n] + both[:, 2 * n : 3 * n])


def silu(v):
    return v / (1.0 + jnp.exp(-v))


def sigmoid(v):
    return 1.0 / (1.0 + jnp.exp(-v))


def silu_slope(v):
    s = sigmoid(v)
    return s + v * s * (1.0 - s)


def columns_total(x):
    ones = jnp.ones((x.shape[0], 128), BF16)
    hi, mid = halves(x)
    low = bf(x - hi.astype(F32) - mid.astype(F32))
    return mm(hi, ones, TN) + (mm(mid, ones, TN) + mm(low, ones, TN))


def spread(column, width):
    return jnp.concatenate([column] * (width // 128), axis=1)


def ends_kernel(levels, k_ref, v_ref, decay_ref, keep_ref, table_ref, unit_ref, dec_ref, all_ref, alldec_ref):
    count = table_ref.shape[1]
    chunks = k_ref.shape[0] // count
    head = k_ref.shape[1]
    total, total_dec = None, None
    for j in range(chunks):
        rows = pl.ds(j * count, count)
        decay = decay_ref[rows, :]
        weight = jnp.exp(exact_sums(table_ref[...], decay)) * keep_ref[rows, :]
        weight = halves(weight)
        keys = halves(silu(k_ref[rows, :].astype(F32)))
        values = v_ref[rows, :]
        unit_k = dot3(weight, keys, TN)
        unit_v = mm(weight[0], values, TN) + mm(weight[1], values, TN)
        unit = jnp.concatenate([unit_k, unit_v], axis=1)
        dec = jnp.exp(columns_total(decay))
        unit_ref[j] = unit
        dec_ref[j] = dec
        if j == 0:
            total, total_dec = unit, dec
        else:
            total = spread(dec, 2 * head) * total + unit
            total_dec = total_dec * dec
    all_ref[0] = total
    alldec_ref[0] = total_dec


def mix(pair, ratios, keep, masks_ref, own):
    out = own * keep
    for l, ratio in enumerate(ratios):
        left = pair * masks_ref[l].astype(F32)
        out += ratio * dot3(halves(left), halves(ratio * keep), NN)
    return out


def unmix(probs, ratios, keep, masks_ref, diag):
    out = diag * jnp.sum(probs * keep, axis=1, keepdims=True)
    for l, ratio in enumerate(ratios):
        part = dot3(halves(probs * ratio), halves(ratio * keep), NT)
        out += masks_ref[l].astype(F32) * part
    return out


def on_diagonal(count):
    return (
        lax.broadcasted_iota(jnp.int32, (count, count), 0) == lax.broadcasted_iota(jnp.int32, (count, count), 1)
    ).astype(F32)


def attend_kernel(
    levels, q_ref, k_ref, v_ref, gate_ref, decay_ref, keep_ref, start_ref, unit_ref, dec_ref, gain_ref, table_ref, masks_ref,
    gated_ref, attended_ref, probs_ref, scores_ref, weights_ref, states_ref,
):
    count = table_ref.shape[1]
    chunks = k_ref.shape[0] // count
    head = k_ref.shape[1]
    diag = on_diagonal(count)
    states_ref[0] = start_ref[0]

    def chunk(j, carry):
        rows = pl.ds(pl.multiple_of(j * count, count), count)
        keep = keep_ref[rows, :]
        powers = jnp.exp(exact_sums(table_ref[: (levels + 1) * count, :], decay_ref[rows, :]))
        ratios = [powers[l * count : (l + 1) * count] for l in range(levels)]
        growth = powers[levels * count : (levels + 1) * count]
        query = halves(silu(q_ref[rows, :].astype(F32)) * head ** (-0.5))
        keys = halves(silu(k_ref[rows, :].astype(F32)))
        state = states_ref[j]
        pair = dot3(query, keys, NT)
        scores = mix(pair, ratios, keep, masks_ref, jnp.sum(pair * diag, axis=1, keepdims=True))
        scores += growth * dot3(query, halves(state[:, :head]), NT)
        top = jnp.max(scores, axis=1, keepdims=True)
        raised = jnp.exp(scores - top)
        probs = raised / jnp.sum(raised, axis=1, keepdims=True)
        weights = unmix(probs, ratios, keep, masks_ref, diag)
        values = v_ref[rows, :]
        whi, wlo = halves(weights)
        attended = mm(whi, values, NN) + mm(wlo, values, NN)
        attended += dot3(halves(probs * growth), halves(state[:, head:]), NN)
        scale = lax.rsqrt(jnp.mean(attended * attended, axis=1, keepdims=True) + EPS)
        gated = attended * scale * gain_ref[...] * silu(gate_ref[rows, :])
        gated_ref[rows, :] = bf(gated)
        attended_ref[rows, :] = attended
        probs_ref[rows, :] = probs
        scores_ref[rows, :] = scores
        weights_ref[rows, :] = weights
        states_ref[j + 1] = spread(dec_ref[j], 2 * head) * state + unit_ref[j]
        return carry

    lax.fori_loop(0, chunks, chunk, 0)


def back_one_kernel(
    levels, q_ref, v_ref, gate_ref, decay_ref, keep_ref, grad_ref, attended_ref, probs_ref, states_ref, dec_ref, gain_ref,
    table_ref, masks_ref,
    gate_term_ref, gain_grad_ref, attended_grad_ref, dprobs_ref, dscores_ref, unit_ref, all_ref,
):
    count = table_ref.shape[1]
    chunks = q_ref.shape[0] // count
    head = q_ref.shape[1]
    diag = on_diagonal(count)
    gain = gain_ref[...]

    def chunk(n, carry):
        j = chunks - 1 - n
        rows = pl.ds(pl.multiple_of(j * count, count), count)
        gate = gate_ref[rows, :]
        attended = attended_ref[rows, :]
        grad = grad_ref[rows, :]
        scale = lax.rsqrt(jnp.mean(attended * attended, axis=1, keepdims=True) + EPS)
        normed = attended * scale
        weighted = grad * silu(gate)
        gate_term_ref[rows, :] = bf(grad * normed * gain * silu_slope(gate))
        part = jnp.sum(weighted * normed, axis=0, keepdims=True)
        c = weighted * gain
        att_grad = scale * c - attended * (scale * scale * scale) * jnp.mean(c * attended, axis=1, keepdims=True)
        attended_grad_ref[rows, :] = att_grad
        keep = keep_ref[rows, :]
        powers = jnp.exp(exact_sums(table_ref[: (levels + 1) * count, :], decay_ref[rows, :]))
        ratios = [powers[l * count : (l + 1) * count] for l in range(levels)]
        growth = powers[levels * count : (levels + 1) * count]
        ahalf = halves(att_grad)
        values = v_ref[rows, :]
        pair = mm(ahalf[0], values, NT) + mm(ahalf[1], values, NT)
        state = states_ref[j]
        dprobs = mix(pair, ratios, keep, masks_ref, jnp.sum(pair * diag, axis=1, keepdims=True))
        dprobs += growth * dot3(ahalf, halves(state[:, head:]), NT)
        probs = probs_ref[rows, :]
        dscores = probs * (dprobs - jnp.sum(probs * dprobs, axis=1, keepdims=True))
        query = halves(silu(q_ref[rows, :].astype(F32)) * head ** (-0.5))
        unit_k = dot3(halves(growth * dscores), query, TN)
        unit_v = dot3(halves(growth * probs), ahalf, TN)
        unit = jnp.concatenate([unit_k, unit_v], axis=1)
        dprobs_ref[rows, :] = dprobs
        dscores_ref[rows, :] = dscores
        unit_ref[j] = unit
        gsum, total = carry
        return gsum + part, spread(dec_ref[j], 2 * head) * total + unit

    gsum, total = lax.fori_loop(
        0, chunks, chunk, (jnp.zeros((1, head), F32), jnp.zeros((unit_ref.shape[1], 2 * head), F32))
    )
    gain_grad_ref[0] = jnp.broadcast_to(gsum, (8, head))
    all_ref[0] = total


def back_two_kernel(
    levels, q_ref, k_ref, v_ref, decay_ref, keep_ref, probs_ref, scores_ref, weights_ref, states_ref, dec_ref, unit_ref,
    attended_grad_ref, dprobs_ref, dscores_ref, end_ref, table_ref, later_ref, masks_ref,
    term_ref, decay_term_ref,
):
    count = table_ref.shape[1]
    chunks = q_ref.shape[0] // count
    head = q_ref.shape[1]
    diag = on_diagonal(count)
    last = (lax.broadcasted_iota(jnp.int32, (count, 1), 0) == count - 1).astype(F32)

    def chunk(n, adj):
        j = chunks - 1 - n
        rows = pl.ds(pl.multiple_of(j * count, count), count)
        keep = keep_ref[rows, :]
        decay = decay_ref[rows, :]
        powers = jnp.exp(exact_sums(table_ref[...], decay))
        ratios = [powers[l * count : (l + 1) * count] for l in range(levels)]
        growth = powers[levels * count : (levels + 1) * count]
        rest = powers[(levels + 1) * count :]
        qraw = q_ref[rows, :].astype(F32)
        kraw = k_ref[rows, :].astype(F32)
        query = halves(silu(qraw) * head ** (-0.5))
        keys = halves(silu(kraw))
        values = v_ref[rows, :]
        att_grad = halves(attended_grad_ref[rows, :])
        probs, dscores = probs_ref[rows, :], dscores_ref[rows, :]
        state = halves(states_ref[j][:, :head])
        ahalf = halves(adj)
        adj_k, adj_v = (ahalf[0][:, :head], ahalf[1][:, :head]), (ahalf[0][:, head:], ahalf[1][:, head:])
        dweights = halves(unmix(dscores, ratios, keep, masks_ref, diag))
        dquery = dot3(dweights, keys, NN) + dot3(halves(dscores * growth), state, NN)
        term_ref[rows, :head] = bf(silu_slope(qraw) * dquery * head ** (-0.5))
        ending = halves(rest * keep)
        dkey = dot3(dweights, query, TN) + dot3(ending, adj_k, NN)
        term_ref[rows, head : 2 * head] = bf(silu_slope(kraw) * dkey)
        dvalue = dot3(halves(weights_ref[rows, :]), att_grad, TN) + dot3(ending, adj_v, NN)
        term_ref[rows, 2 * head :] = bf(dvalue)
        pair_k = dot3(query, keys, NT)
        pair_v = mm(att_grad[0], values, NT) + mm(att_grad[1], values, NT)
        dkeep = jnp.sum(pair_k * diag, axis=1, keepdims=True) * dscores
        dkeep += jnp.sum(pair_v * diag, axis=1, keepdims=True) * probs
        dkeep += rest * (dot3(keys, adj_k, NT) + mm(values, adj_v[0], NT) + mm(values, adj_v[1], NT))
        for l, ratio in enumerate(ratios):
            mask = masks_ref[l].astype(F32)
            part = dot3(halves(pair_k * mask), halves(dscores * ratio), TN)
            part += dot3(halves(pair_v * mask), halves(probs * ratio), TN)
            dkeep += ratio * part
        dsum = dscores * scores_ref[rows, :] + probs * dprobs_ref[rows, :] - keep * dkeep
        at_end = jnp.sum(adj * states_ref[j + 1], axis=1, keepdims=True)
        at_end = jnp.sum(at_end * on_diagonal(adj.shape[0]), axis=0, keepdims=True)
        dsum += last * at_end
        ddecay = exact_sums(later_ref[...], dsum) - (1.0 - keep) * dkeep
        decay_term_ref[rows, :] = ddecay
        return spread(dec_ref[j], 2 * head) * adj + unit_ref[j]

    lax.fori_loop(0, chunks, chunk, end_ref[0])


def params():
    return pltpu.CompilerParams(vmem_limit_bytes=56 * 2**20)


def call(kernel, grid, ins, outs, name, flops=0):
    return pl.pallas_call(
        kernel,
        grid=grid,
        in_specs=[pl.BlockSpec(block, where) for _, block, where in ins],
        out_specs=[pl.BlockSpec(block, where) for _, _, block, where in outs],
        out_shape=[jax.ShapeDtypeStruct(shape, dtype) for shape, dtype, _, _ in outs],
        compiler_params=params(),
        name=name,
    )(*[array for array, _, _ in ins])


class Slots:
    def __init__(self, seqs, rows, head, slots, chunk):
        self.seqs, self.rows, self.head, self.slots, self.chunk = seqs, rows, head, slots, chunk
        self.chunks = rows // chunk
        paths, masks = decay_tables(chunk)
        self.levels = masks.shape[0]
        self.paths = jnp.asarray(paths, BF16)
        self.masks = jnp.asarray(masks, BF16)

    def row(self, array, width=None, place=0):
        width = array.shape[1] if width is None else width
        return (array, (self.rows, width), lambda b: (b, place))

    def whole(self, array):
        return (array, array.shape, lambda b: (0,) * array.ndim)

    def per(self, array, count):
        return (array, (count,) + array.shape[1:], lambda b: (b,) + (0,) * (array.ndim - 1))

    def out_row(self, width, dtype):
        return ((self.seqs * self.rows, width), dtype, (self.rows, width), lambda b: (b, 0))

    def out_per(self, count, shape, dtype=F32):
        return ((self.seqs * count,) + shape, dtype, (count,) + shape, lambda b: (b,) + (0,) * len(shape))

    def ends(self, qkv, decay, keep):
        m, w = self.slots, 2 * self.head
        tail = self.paths[-self.chunk :]
        return call(
            functools.partial(ends_kernel, self.levels), (self.seqs,),
            [self.row(qkv, self.head, 1), self.row(qkv, self.head, 2), self.row(decay), self.row(keep), self.whole(tail)],
            [self.out_per(self.chunks, (m, w)), self.out_per(self.chunks, (m, 128)), self.out_per(1, (m, w)), self.out_per(1, (m, 128))],
            "slot_ends",
        )

    def attend(self, qkv, gate, decay, keep, start, unit, dec, gain):
        h, m = self.head, self.slots
        return call(
            functools.partial(attend_kernel, self.levels), (self.seqs,),
            [self.row(qkv, h, 0), self.row(qkv, h, 1), self.row(qkv, h, 2), self.row(gate, h, 0), self.row(decay), self.row(keep),
             self.per(start, 1), self.per(unit, self.chunks), self.per(dec, self.chunks), self.whole(gain), self.whole(self.paths),
             self.whole(self.masks)],
            [self.out_row(h, BF16), self.out_row(h, F32), self.out_row(m, F32), self.out_row(m, F32), self.out_row(self.chunk, F32),
             self.out_per(self.chunks + 1, (m, 2 * h))],
            "slot_attend",
        )

    def back_one(self, qkv, gate, decay, keep, grad, attended, probs, states, dec, gain):
        h, m = self.head, self.slots
        return call(
            functools.partial(back_one_kernel, self.levels), (self.seqs,),
            [self.row(qkv, h, 0), self.row(qkv, h, 2), self.row(gate, h, 0), self.row(decay), self.row(keep), self.row(grad),
             self.row(attended), self.row(probs), self.per(states, self.chunks + 1), self.per(dec, self.chunks), self.whole(gain),
             self.whole(self.paths), self.whole(self.masks)],
            [self.out_row(h, BF16), self.out_per(1, (8, h)), self.out_row(h, F32), self.out_row(m, F32), self.out_row(m, F32),
             self.out_per(self.chunks, (m, 2 * h)), self.out_per(1, (m, 2 * h))],
            "slot_back_one",
        )

    def back_two(self, qkv, decay, keep, probs, scores, weights, states, dec, unit, attended_grad, dprobs, dscores, end):
        h, m = self.head, self.slots
        later = self.paths[-2 * self.chunk : -self.chunk].T
        return call(
            functools.partial(back_two_kernel, self.levels), (self.seqs,),
            [self.row(qkv, h, 0), self.row(qkv, h, 1), self.row(qkv, h, 2), self.row(decay), self.row(keep), self.row(probs),
             self.row(scores), self.row(weights), self.per(states, self.chunks + 1), self.per(dec, self.chunks),
             self.per(unit, self.chunks), self.row(attended_grad), self.row(dprobs), self.row(dscores), self.per(end, 1),
             self.whole(self.paths), self.whole(later), self.whole(self.masks)],
            [self.out_row(3 * h, BF16), self.out_row(m, F32)],
            "slot_back_two",
        )

class Place:
    def __init__(self, size):
        self.size = size
        self.line = size // 4
        s = lax.axis_index("seq")
        self.c = lax.axis_index("head")
        self.s = s
        self.x = lax.rem(s, 2)
        self.b = lax.rem(s // 2, 2)
        self.a = s // 4

    def at(self, a, b, x):
        return (a * 2 + b) * 2 + x

    def partner(self):
        return (self.at(self.a, self.b, 1 - self.x), self.c)

    def across(self):
        return (self.at(self.a, 1 - self.b, self.x), self.c)

    def up(self):
        return (self.at(jnp.minimum(self.a + 1, self.line - 1), self.b, self.x), self.c)

    def down(self):
        return (self.at(jnp.maximum(self.a - 1, 0), self.b, self.x), self.c)

    def sibling(self):
        return (self.s, 1 - self.c)

    def has_up(self):
        return self.a < self.line - 1

    def has_down(self):
        return self.a > 0


def signal(sem, device):
    pl.semaphore_signal(sem, inc=1, device_id=device, device_id_type=MESH)


def greet(place, partner=True, across=True, line=True, sibling=False):
    barrier = pltpu.get_barrier_semaphore()
    count = jnp.int32(0)
    if partner:
        signal(barrier, place.partner())
        count = count + 1
    if sibling:
        signal(barrier, place.sibling())
        count = count + 1
    if across:
        signal(barrier, place.across())
        count = count + 1
    if line:
        pl.when(place.has_up())(lambda: signal(barrier, place.up()))
        pl.when(place.has_down())(lambda: signal(barrier, place.down()))
        count = count + place.has_up().astype(jnp.int32) + place.has_down().astype(jnp.int32)
    pl.semaphore_wait(barrier, count)


def remote(src, dst, send, recv, device):
    return pltpu.make_async_remote_copy(
        src_ref=src, dst_ref=dst, send_sem=send, recv_sem=recv, device_id=device, device_id_type=MESH
    )


class Gather:
    def __init__(self, place, shard, full, unit, offset, width, sems, late):
        self.pl, self.shard, self.full = place, shard, full
        self.unit, self.offset, self.width, self.late = unit, offset, width, late
        self.x_sem, self.b_sem, self.up_sem, self.down_sem = sems

    def part(self, start, count):
        rows = pl.ds(start * self.unit, count * self.unit)
        if self.width == self.full.shape[1]:
            return self.full.at[rows]
        return self.full.at[rows, pl.ds(self.offset, self.width)]

    def mine(self, x):
        if self.shard.shape[1] == self.width:
            return self.shard
        return self.shard.at[:, pl.ds(x * self.width, self.width)]

    def x_copy(self):
        p = self.pl
        return remote(self.mine(1 - p.x), self.part(p.s, 1), self.x_sem.at[0], self.x_sem.at[1], p.partner())

    def own_copy(self):
        return pltpu.make_async_copy(self.mine(self.pl.x), self.part(self.pl.s, 1), self.x_sem.at[2])

    def block(self, a):
        p = self.pl
        if self.late:
            return self.part(4 * a, 4)
        return self.part(4 * a + 2 * p.b, 2)

    def b_copy(self, i, a):
        p = self.pl
        return remote(
            self.part(4 * a + 2 * p.b, 2), self.part(4 * a + 2 * p.b, 2),
            self.b_sem.at[0, i], self.b_sem.at[1, i], p.across(),
        )

    def line_copy(self, way, h):
        p = self.pl
        if way == "up":
            blk = self.block(jnp.maximum(p.a - (h - 1), 0))
            return remote(blk, blk, self.up_sem.at[0, h - 1], self.up_sem.at[1, h - 1], p.up())
        blk = self.block(jnp.minimum(p.a + (h - 1), p.line - 1))
        return remote(blk, blk, self.down_sem.at[0, h - 1], self.down_sem.at[1, h - 1], p.down())

    def sends(self, way, h):
        p = self.pl
        if way == "up":
            return jnp.logical_and(p.has_up(), p.a - (h - 1) >= 0)
        return jnp.logical_and(p.has_down(), p.a + (h - 1) <= p.line - 1)

    def gets(self, way, h):
        p = self.pl
        if way == "up":
            return p.a - h >= 0
        return p.a + h <= p.line - 1

    def got(self, way, h):
        p = self.pl
        if way == "up":
            return jnp.maximum(p.a - h, 0)
        return jnp.minimum(p.a + h, p.line - 1)

    def slot(self, way, h):
        return h if way == "up" else self.pl.line - 1 + h

    def start_x(self):
        self.x_copy().start()
        self.own_copy().start()

    def stage(self, h):
        p = self.pl
        if h == 0:
            self.own_copy().wait()
            self.x_copy().wait_recv()
            if self.late:
                self.b_copy(0, p.a).start()
            else:
                for way in ("up", "down"):
                    pl.when(self.sends(way, 1))(lambda way=way: self.line_copy(way, 1).start())
                self.b_copy(0, p.a).start()
            return
        if self.late:
            if h == 1:
                self.b_copy(0, p.a).wait_recv()
                for way in ("up", "down"):
                    pl.when(self.sends(way, 1))(lambda way=way: self.line_copy(way, 1).start())
                return
            h = h - 1
        for way in ("up", "down"):

            def go(way=way):
                self.line_copy(way, h).wait_recv()
                if not self.late:
                    self.b_copy(self.slot(way, h), self.got(way, h)).start()

            def on(way=way):
                self.line_copy(way, h + 1).start()

            pl.when(self.gets(way, h))(go)
            if h + 1 <= p.line - 1:
                pl.when(self.sends(way, h + 1))(on)

    def stages(self):
        return self.pl.line + (1 if self.late else 0)

    def finish(self):
        p = self.pl
        self.x_copy().wait_send()
        self.b_copy(0, p.a).wait_send()
        if not self.late:
            self.b_copy(0, p.a).wait_recv()
        for way in ("up", "down"):
            for h in range(1, p.line):
                pl.when(self.sends(way, h))(lambda way=way, h=h: self.line_copy(way, h).wait_send())
                if not self.late:

                    def both(way=way, h=h):
                        cp = self.b_copy(self.slot(way, h), self.got(way, h))
                        cp.wait_send()
                        cp.wait_recv()

                    pl.when(self.gets(way, h))(both)


def gather_sems(line):
    return [
        pltpu.SemaphoreType.DMA((3,)),
        pltpu.SemaphoreType.DMA((2, 2 * line - 1)),
        pltpu.SemaphoreType.DMA((2, line - 1)),
        pltpu.SemaphoreType.DMA((2, line - 1)),
    ]


def gather_ops(gathers, ahead):
    steps = []
    n = len(gathers)
    for k in range(min(ahead, n)):
        steps.append(gathers[k].start_x)
    steps.append(functools.partial(gathers[0].stage, 0))
    for k in range(n):
        if k + ahead < n:
            steps.append(gathers[k + ahead].start_x)
        if k + 1 < n:
            steps.append(functools.partial(gathers[k + 1].stage, 0))
        for h in range(1, gathers[k].stages()):
            steps.append(functools.partial(gathers[k].stage, h))
    for g in gathers:
        steps.append(g.finish)
    return steps

def prefix_kernel(size, back, own_ref, dec_ref, start_ref, peer, peer_dec, line, out, p_sem, d_sem, l_sem):
    p = Place(size)
    greet(p, partner=False)
    seqs, slots, width = own_ref.shape
    half = width // 2
    pieces = [(b, h) for b in range(seqs) for h in range(2)]

    def cut(ref, piece):
        return ref.at[piece[0], :, pl.ds(piece[1] * half, half)]

    def peer_copy(i, piece):
        return remote(cut(own_ref, piece), cut(peer, piece), p_sem.at[0, i], p_sem.at[1, i], p.across())

    if back:
        has_prev, has_next, after = p.has_up(), p.has_down(), p.down()
    else:
        has_prev, has_next, after = p.has_down(), p.has_up(), p.up()

    def line_copy(i, piece):
        return remote(cut(out, piece), cut(line, piece), l_sem.at[0, i], l_sem.at[1, i], after)

    dec_copy = remote(dec_ref, peer_dec, d_sem.at[0], d_sem.at[1], p.across())
    dec_copy.start()
    for i, piece in enumerate(pieces):
        peer_copy(i, piece).start()
    own_first = (p.b == 1) if back else (p.b == 0)
    first = own_first.astype(F32)
    dec_copy.wait_recv()
    for i, piece in enumerate(pieces):
        peer_copy(i, piece).wait_recv()
        dec_own = spread(dec_ref[piece[0]], half)
        dec_peer = spread(peer_dec[piece[0]], half)
        own, other = cut(own_ref, piece)[...], cut(peer, piece)[...]
        both = first * (dec_peer * own + other) + (1.0 - first) * (dec_own * other + own)
        here = cut(out, piece)

        def go_on():
            line_copy(i, piece).wait_recv()
            came = cut(line, piece)[...]
            here[...] = dec_own * dec_peer * came + both
            cut(start_ref, piece)[...] = first * came + (1.0 - first) * (dec_peer * came + other)

        def begin():
            here[...] = both
            cut(start_ref, piece)[...] = (1.0 - first) * other

        pl.when(has_prev)(go_on)
        pl.when(jnp.logical_not(has_prev))(begin)
        pl.when(has_next)(lambda i=i, piece=piece: line_copy(i, piece).start())
    dec_copy.wait_send()
    for i, piece in enumerate(pieces):
        peer_copy(i, piece).wait_send()
        pl.when(has_next)(lambda i=i, piece=piece: line_copy(i, piece).wait_send())


VM = pl.BlockSpec(memory_space=pltpu.VMEM)
ANY = pl.BlockSpec(memory_space=HBM)


def remote_params(number, mib=56):
    return pltpu.CompilerParams(collective_id=number, has_side_effects=True, vmem_limit_bytes=mib * 2**20)


def prefix(size, number, own, dec, back):
    shape = own.shape
    count = 2 * shape[0]
    return pl.pallas_call(
        functools.partial(prefix_kernel, size, back),
        out_shape=jax.ShapeDtypeStruct(shape, F32),
        in_specs=[VM, VM],
        out_specs=VM,
        scratch_shapes=[
            pltpu.VMEM(shape, F32), pltpu.VMEM(dec.shape, F32), pltpu.VMEM(shape, F32), pltpu.VMEM(shape, F32),
            pltpu.SemaphoreType.DMA((2, count)), pltpu.SemaphoreType.DMA((2,)), pltpu.SemaphoreType.DMA((2, count)),
        ],
        compiler_params=remote_params(number),
        name="slot_suffix" if back else "slot_prefix",
    )(own, dec)


STRIPS = 4


class Fold:
    def __init__(self, place, part, sib, sent, came, sems):
        self.p, self.part, self.sib, self.sent, self.came = place, part, sib, sent, came
        self.s_sem, self.x_sem = sems
        self.rows = part.shape[2] // STRIPS

    def strip(self, r):
        return pl.ds(r * self.rows, self.rows)

    def sib_copy(self, far, r):
        p = self.p
        x = 1 - p.x if far else p.x
        i = (0 if far else STRIPS) + r
        return remote(
            self.part.at[1 - p.c, x, self.strip(r)], self.sib.at[1 if far else 0, self.strip(r)],
            self.s_sem.at[0, i], self.s_sem.at[1, i], p.sibling(),
        )

    def x_copy(self, r):
        return remote(
            self.sent.at[self.strip(r)], self.came.at[self.strip(r)], self.x_sem.at[0, r], self.x_sem.at[1, r], self.p.partner()
        )

    def start(self):
        for r in range(STRIPS):
            self.sib_copy(True, r).start()
        for r in range(STRIPS):
            self.sib_copy(False, r).start()

    def cross(self, r):
        p = self.p
        self.sib_copy(True, r).wait_recv()
        own = self.part[p.c, 1 - p.x, self.strip(r)].astype(F32)
        self.sent[self.strip(r)] = bf(own + self.sib[1, self.strip(r)].astype(F32))
        self.x_copy(r).start()

    def total(self, r):
        p = self.p
        self.sib_copy(False, r).wait_recv()
        self.x_copy(r).wait_recv()
        own = self.part[p.c, p.x, self.strip(r)].astype(F32) + self.sib[0, self.strip(r)].astype(F32)
        return own + self.came[self.strip(r)].astype(F32)

    def finish(self):
        for r in range(STRIPS):
            self.sib_copy(True, r).wait_send()
            self.sib_copy(False, r).wait_send()
            self.x_copy(r).wait_send()


def fold_scratch(rows, width):
    return [
        pltpu.VMEM((2, rows, width), BF16), pltpu.VMEM((rows, width), BF16), pltpu.VMEM((rows, width), BF16),
        pltpu.SemaphoreType.DMA((2, 2 * STRIPS)), pltpu.SemaphoreType.DMA((2, STRIPS)),
    ]


class Share:
    def __init__(self, place, out, sems):
        self.p, self.out = place, out
        self.x_sem, self.s_sem = sems
        self.rows = out.shape[2] // STRIPS

    def strip(self, r):
        return pl.ds(r * self.rows, self.rows)

    def x_copy(self, r):
        p = self.p
        block = self.out.at[p.c, p.x, self.strip(r)]
        return remote(block, block, self.x_sem.at[0, r], self.x_sem.at[1, r], p.partner())

    def s_copy(self, far, r):
        p = self.p
        block = self.out.at[p.c, 1 - p.x if far else p.x, self.strip(r)]
        i = (0 if far else STRIPS) + r
        return remote(block, block, self.s_sem.at[0, i], self.s_sem.at[1, i], p.sibling())

    def put(self, r, value):
        self.out[self.p.c, self.p.x, self.strip(r)] = value
        self.x_copy(r).start()
        self.s_copy(False, r).start()

    def forward(self, r):
        self.x_copy(r).wait_recv()
        self.s_copy(True, r).start()

    def finish(self):
        for r in range(STRIPS):
            self.x_copy(r).wait_send()
            for far in (False, True):
                self.s_copy(far, r).wait_send()
                self.s_copy(far, r).wait_recv()


SHARE_SEMS = [pltpu.SemaphoreType.DMA((2, STRIPS)), pltpu.SemaphoreType.DMA((2, 2 * STRIPS))]


def inverse_rms(values):
    return lax.rsqrt(jnp.mean(values * values, axis=-1, keepdims=True) + EPS)


def norm_back(grad, values, gain):
    scale = inverse_rms(values)
    u = grad * gain
    down = scale * u - values * (scale * scale * scale) * jnp.mean(u * values, axis=-1, keepdims=True)
    return down, jnp.sum(grad * values * scale, axis=0, keepdims=True)


def blend_kernel(size, part, tokens, gain, residual, normed, sib, sent, came, s1, s2, s3, s4):
    p = Place(size)
    greet(p, across=False, line=False, sibling=True)
    fold = Fold(p, part, sib, sent, came, (s1, s2))
    share = Share(p, normed, (s3, s4))
    fold.start()
    for r in range(STRIPS):
        fold.cross(r)
    for r in range(STRIPS):
        value = tokens[p.c, fold.strip(r)].astype(F32) + fold.total(r)
        residual[fold.strip(r)] = value
        share.put(r, bf(value * inverse_rms(value) * gain[...]))
    for r in range(STRIPS):
        share.forward(r)
    share.finish()
    fold.finish()


def blend(size, number, part, tokens, gain):
    _, _, rows, width = part.shape
    return pl.pallas_call(
        functools.partial(blend_kernel, size),
        out_shape=[jax.ShapeDtypeStruct((rows, width), F32), jax.ShapeDtypeStruct(part.shape, BF16)],
        in_specs=[VM] * 3,
        out_specs=[VM] * 2,
        scratch_shapes=fold_scratch(rows, width) + SHARE_SEMS,
        compiler_params=remote_params(number),
        name="blend",
    )(part, tokens, gain)


def blend_back_kernel(size, part, grad_out, residual, gain, residual_grad, low, gain_grad, sib, sent, came, s1, s2, s3, s4):
    p = Place(size)
    greet(p, across=False, line=False, sibling=True)
    fold = Fold(p, part, sib, sent, came, (s1, s2))
    share = Share(p, low, (s3, s4))
    fold.start()
    for r in range(STRIPS):
        fold.cross(r)
    gains = jnp.zeros((1, part.shape[3]), F32)
    for r in range(STRIPS):
        down, more = norm_back(fold.total(r), residual[fold.strip(r)], gain[...])
        value = grad_out[p.c, fold.strip(r)].astype(F32) + down
        gains += more
        residual_grad[fold.strip(r)] = value
        share.put(r, bf(value))
    gain_grad[...] = gains
    for r in range(STRIPS):
        share.forward(r)
    share.finish()
    fold.finish()


def blend_back(size, number, part, grad_out, residual, gain):
    _, _, rows, width = part.shape
    return pl.pallas_call(
        functools.partial(blend_back_kernel, size),
        out_shape=[
            jax.ShapeDtypeStruct((rows, width), F32), jax.ShapeDtypeStruct(part.shape, BF16), jax.ShapeDtypeStruct((1, width), F32)
        ],
        in_specs=[VM] * 4,
        out_specs=[VM] * 3,
        scratch_shapes=fold_scratch(rows, width) + SHARE_SEMS,
        compiler_params=remote_params(number),
        name="blend_back",
    )(part, grad_out, residual, gain)


def finish_kernel(
    size, part, ff_part, tokens, residual, residual_grad, gain, input_grad, output, gain_grad,
    sib, sent, came, s1, s2, sib2, sent2, came2, t1, t2, out_sem,
):
    p = Place(size)
    greet(p, across=False, line=False, sibling=True)
    fold = Fold(p, part, sib, sent, came, (s1, s2))
    ff = Fold(p, ff_part, sib2, sent2, came2, (t1, t2))
    ff.start()
    fold.start()
    for r in range(STRIPS):
        ff.cross(r)
        fold.cross(r)
    gains = jnp.zeros((1, part.shape[3]), F32)

    def out_copy(ref, k, r):
        block = ref.at[p.c, fold.strip(r)]
        return remote(block, block, out_sem.at[0, k * STRIPS + r], out_sem.at[1, k * STRIPS + r], p.sibling())

    for r in range(STRIPS):
        output[p.c, fold.strip(r)] = bf(residual[fold.strip(r)] + ff.total(r))
        out_copy(output, 0, r).start()
        down, more = norm_back(fold.total(r), tokens[p.c, fold.strip(r)].astype(F32), gain[...])
        gains += more
        input_grad[p.c, fold.strip(r)] = residual_grad[fold.strip(r)] + down
        out_copy(input_grad, 1, r).start()
    gain_grad[...] = gains
    for r in range(STRIPS):
        out_copy(output, 0, r).wait()
        out_copy(input_grad, 1, r).wait()
    ff.finish()
    fold.finish()


def finish(size, number, part, ff_part, tokens, residual, residual_grad, gain):
    _, _, rows, width = part.shape
    return pl.pallas_call(
        functools.partial(finish_kernel, size),
        out_shape=[
            jax.ShapeDtypeStruct((2, rows, width), F32), jax.ShapeDtypeStruct((2, rows, width), BF16),
            jax.ShapeDtypeStruct((1, width), F32),
        ],
        in_specs=[VM] * 6,
        out_specs=[VM] * 3,
        scratch_shapes=fold_scratch(rows, width) * 2 + [pltpu.SemaphoreType.DMA((2, 2 * STRIPS))],
        compiler_params=remote_params(number),
        name="finish",
    )(part, ff_part, tokens, residual, residual_grad, gain)


class Scatter:
    def __init__(self, place, grad, out, unit, offset, width, bufs, sems):
        self.p, self.grad, self.out = place, grad, out
        self.unit, self.offset, self.width = unit, offset, width
        self.whole = out.shape[-1] == width
        self.own, self.peer, self.line, self.total = bufs
        self.o_sem, self.b_sem, self.l_sem, self.x_sem = sems

    def block(self, a, b):
        rows = pl.ds((4 * a + 2 * b) * self.unit, 2 * self.unit)
        if self.width == self.grad.shape[1]:
            return self.grad.at[rows]
        return self.grad.at[rows, pl.ds(self.offset, self.width)]

    def own_copy(self, a):
        return pltpu.make_async_copy(self.block(a, self.p.b), self.own.at[a], self.o_sem.at[a])

    def b_copy(self, a):
        return remote(self.block(a, 1 - self.p.b), self.peer.at[a], self.b_sem.at[0, a], self.b_sem.at[1, a], self.p.across())

    def send_line(self, d, way):
        p = self.p
        if way == "up":
            return remote(self.own.at[d], self.line.at[d], self.l_sem.at[0, d], self.l_sem.at[1, d], p.up())
        slot = jnp.where(p.a - 1 == d, p.line, d)
        return remote(self.own.at[d], self.line.at[slot], self.l_sem.at[0, d], self.l_sem.at[1, slot], p.down())

    def wait_line(self, d, slot):
        p = self.p
        remote(self.own.at[d], self.line.at[slot], self.l_sem.at[0, d], self.l_sem.at[1, slot], p.across()).wait_recv()

    def start(self):
        lines = self.p.line
        for a in sorted(range(lines), key=lambda a: -abs(2 * a - lines + 1)):
            self.b_copy(a).start()
            self.own_copy(a).start()

    def strips(self, do):
        rows, width = self.own.shape[1], self.own.shape[2]
        step = max(r for r in (16, 32, 64, 128) if rows % r == 0 and (r == 16 or r * width <= 64 * 1024))

        def one(i, carry):
            do(pl.ds(pl.multiple_of(i * step, step), step))
            return carry

        lax.fori_loop(0, rows // step, one, 0)

    def ready(self, d):
        self.own_copy(d).wait()
        self.b_copy(d).wait_recv()

    def add(self, d, lines):
        def do(rows):
            value = self.own[d, rows].astype(F32) + self.peer[d, rows].astype(F32)
            for slot in lines:
                value += self.line[slot, rows].astype(F32)
            self.own[d, rows] = bf(value)

        self.strips(do)

    def hop(self, j):
        p = self.p

        def go(d, way, has_prev):
            self.ready(d)

            def more():
                self.wait_line(d, d)
                self.add(d, [d])

            pl.when(has_prev)(more)
            pl.when(jnp.logical_not(has_prev))(lambda: self.add(d, []))
            self.send_line(d, way).start()

        up = p.line - 1 - j
        pl.when(up > p.a)(lambda: go(up, "up", p.has_down()))
        pl.when(j < p.a)(lambda: go(j, "down", p.has_up()))

    def last(self):
        p = self.p
        lines = p.line
        for a in range(lines):

            def here(a=a):
                self.ready(a)
                slots = []
                if a > 0:
                    self.wait_line(a, a)
                    slots.append(a)
                if a < lines - 1:
                    self.wait_line(a, lines)
                    slots.append(lines)

                def do(rows):
                    value = self.own[a, rows].astype(F32) + self.peer[a, rows].astype(F32)
                    for slot in slots:
                        value += self.line[slot, rows].astype(F32)
                    self.total[rows] = value

                self.strips(do)

            pl.when(p.a == a)(here)
        self.x_copy().start()
        if not self.whole:
            self.out_copy().start()

    def half(self, x):
        return self.total.at[pl.ds(x * self.unit, self.unit)]

    def place(self):
        return self.out.at[:, pl.ds(self.p.x * self.width, self.width)]

    def x_copy(self):
        p = self.p
        where = self.out.at[1] if self.whole else self.place()
        return remote(self.half(1 - p.x), where, self.x_sem.at[0], self.x_sem.at[1], p.partner())

    def out_copy(self):
        return pltpu.make_async_copy(self.half(self.p.x), self.place(), self.x_sem.at[2])

    def finish(self):
        p = self.p
        self.x_copy().wait()
        if self.whole:
            self.out[0] = self.out[1] + self.half(p.x)[...]
        else:
            self.out_copy().wait()
        for a in range(p.line):
            self.b_copy(a).wait_send()
            pl.when(a > p.a)(lambda a=a: self.send_line(a, "up").wait_send())
            pl.when(a < p.a)(lambda a=a: self.send_line(a, "down").wait_send())


def scatter_scratch(line, block):
    return [
        pltpu.VMEM((line,) + block, BF16), pltpu.VMEM((line,) + block, BF16), pltpu.VMEM((line + 1,) + block, BF16),
        pltpu.VMEM(block, F32),
        pltpu.SemaphoreType.DMA((line,)), pltpu.SemaphoreType.DMA((2, line)), pltpu.SemaphoreType.DMA((2, line + 1)),
        pltpu.SemaphoreType.DMA((3,)),
    ]


def greet_all(place):
    barrier = pltpu.get_barrier_semaphore()

    def one(i, carry):
        signal(barrier, (lax.rem(place.s + i // 2, place.size), lax.rem(place.c + lax.rem(i, 2), 2)))
        return carry

    lax.fori_loop(1, 2 * place.size, one, 0)
    pl.semaphore_wait(barrier, 2 * place.size - 1)


class Smalls:
    def __init__(self, place, pack, out, came, sems):
        self.p, self.pack, self.out, self.came, self.sems = place, pack, out, came, sems

    def copy(self, i):
        p = self.p
        s = lax.rem(p.s + i // 2, p.size)
        return remote(
            self.pack.at[s], self.came.at[i], self.sems.at[0, i], self.sems.at[1, i], (s, lax.rem(p.c + lax.rem(i, 2), 2))
        )

    def start(self):
        lax.fori_loop(1, 2 * self.p.size, lambda i, c: (self.copy(i).start(), c)[1], 0)

    def finish(self):
        def one(i, total):
            self.copy(i).wait()
            return total + self.came[i]

        self.out[...] = lax.fori_loop(1, 2 * self.p.size, one, self.pack[self.p.s])


def scatter_kernel(size, plan, *refs):
    p = Place(size)
    grads = max(i for i, _, _, _ in plan) + 1
    outs = len(plan)
    ins, refs = refs[: grads + 1], refs[grads + 1 :]
    out_refs, refs = refs[: outs + 1], refs[outs + 1 :]
    came, s_sem = refs[:2]
    refs = refs[2:]
    greet_all(p)
    smalls = Smalls(p, ins[grads], out_refs[outs], came, s_sem)
    work = []
    for n, (i, unit, offset, width) in enumerate(plan):
        mine = refs[8 * n : 8 * n + 8]
        work.append(Scatter(p, ins[i], out_refs[n], unit, offset, width, mine[:4], mine[4:]))
    work[0].start()
    smalls.start()
    for n, chunk in enumerate(work):
        if n + 1 < len(work):
            work[n + 1].start()
        for j in range(p.line - 1):
            chunk.hop(j)
        chunk.last()
    smalls.finish()
    for chunk in work:
        chunk.finish()


def scatter(size, number, plan, grads, pack):
    line = size // 4
    shapes, specs, scratch = [], [], []
    for i, unit, offset, width, whole in plan:
        shapes.append(jax.ShapeDtypeStruct((2, unit, width) if whole else (unit, 2 * width), F32))
        specs.append(VM if whole else ANY)
        scratch += scatter_scratch(line, (2 * unit, width))
    return pl.pallas_call(
        functools.partial(scatter_kernel, size, [entry[:4] for entry in plan]),
        out_shape=shapes + [jax.ShapeDtypeStruct(pack.shape[1:], F32)],
        in_specs=[ANY] * len(grads) + [VM],
        out_specs=specs + [VM],
        scratch_shapes=[pltpu.VMEM((2 * size,) + pack.shape[1:], F32), pltpu.SemaphoreType.DMA((2, 2 * size))] + scratch,
        compiler_params=remote_params(number, 60),
        name="scatter",
    )(*grads, pack)


class Swap:
    def __init__(self, place, own, both, sems):
        self.p, self.own, self.both, self.sems = place, own, both, sems

    def start(self):
        p = self.p
        self.cross = remote(self.own, self.both.at[:, p.x], self.sems.at[0], self.sems.at[1], p.partner())
        self.keep = pltpu.make_async_copy(self.own, self.both.at[:, p.x], self.sems.at[2])
        self.cross.start()
        self.keep.start()

    def finish(self):
        self.keep.wait()
        self.cross.wait()


def gather_kernel(size, plan, swaps, *refs):
    p = Place(size)
    shards = len(plan)
    fulls = max(i for i, _, _, _, _ in plan) + 1
    ins, refs = refs[: shards + swaps], refs[shards + swaps :]
    outs, refs = refs[: fulls + swaps], refs[fulls + swaps :]
    greet(p)
    work = []
    for n, (i, unit, offset, width, late) in enumerate(plan):
        work.append(Gather(p, ins[n], outs[i], unit, offset, width, refs[4 * n : 4 * n + 4], late))
    moves = [Swap(p, ins[shards + n], outs[fulls + n], refs[4 * shards + n]) for n in range(swaps)]
    steps = gather_ops(work, 3)
    for step in steps[: -len(work)]:
        step()
    for move in moves:
        move.start()
    for step in steps[-len(work) :]:
        step()
    for move in moves:
        move.finish()


def gather(size, number, plan, shards, fulls, tokens):
    line = size // 4
    scratch = []
    for _ in plan:
        scratch += gather_sems(line)
    shapes = [jax.ShapeDtypeStruct(shape, BF16) for shape in fulls]
    for array in tokens:
        shapes.append(jax.ShapeDtypeStruct((array.shape[0], 2) + array.shape[1:], BF16))
        scratch.append(pltpu.SemaphoreType.DMA((3,)))
    return pl.pallas_call(
        functools.partial(gather_kernel, size, plan, len(tokens)),
        out_shape=shapes,
        in_specs=[ANY] * (len(shards) + len(tokens)),
        out_specs=[ANY] * len(shapes),
        scratch_shapes=scratch,
        compiler_params=remote_params(number, 16),
        name="gather",
    )(*shards, *tokens)


def dot(left, right, dims, dtype=F32):
    return lax.dot_general(left, right, dims, preferred_element_type=F32).astype(dtype)


def lanes(row):
    return jnp.pad(row.reshape(-1), (0, 128 - row.size))


def shards(
    tokens, grad_out, query_weight, key_weight, value_weight, forget_weight, forget_bias, outgate_weight, output_weight,
    slot_gain, first_gain, second_gain, gate_weight, up_weight, down_weight,
):
    size = lax.axis_size("seq")
    x = lax.rem(lax.axis_index("seq"), 2)
    c = lax.axis_index("head")
    seqs, block, width = tokens.shape
    heads_here, slot_part = forget_bias.shape
    slots = slot_part * size
    head = slot_gain.shape[0] * size
    unit = first_gain.shape[0]
    hidden = gate_weight.shape[1] // 2
    rows = seqs * 2 * block
    pack = jnp.stack([lanes(first_gain), lanes(second_gain), lanes(slot_gain), lanes(forget_bias)] + [jnp.zeros(128, BF16)] * 12)
    plan = [
        (0, unit, 0, head, False), (0, unit, head, head, False), (0, unit, 2 * head, head, False),
        (1, unit, 0, head, False), (1, unit, head, 2 * slots, False), (2, unit, 0, head, False),
        (3, 16, 0, 128, False),
        (4, unit, 0, hidden, False), (4, unit, hidden, hidden, False), (5, unit, 0, hidden, False),
    ]
    fulls = [
        (width, 3 * head), (width, head + 2 * slots), (width, head), (16 * size, 128), (width, 2 * hidden), (width, hidden),
    ]
    qkv_full, gate_full, out_full, small_full, ff_full, down_full, tok, gout = gather(
        size, 0, plan,
        (query_weight, key_weight, value_weight, outgate_weight, forget_weight, output_weight.T, pack, gate_weight, up_weight,
         down_weight.T),
        fulls, (tokens, grad_out),
    )
    small = small_full.reshape(size, 16, 128).astype(F32)
    first_full = small[:, 0, :unit].reshape(1, width)
    second_full = small[:, 1, :unit].reshape(1, width)
    slot_full = small[:, 2, : head // size].reshape(1, head)
    bias_full = small[:, 3, : heads_here * slot_part].reshape(size, heads_here, slot_part)
    bias_full = jnp.moveaxis(bias_full, 1, 0).reshape(heads_here, slots)

    def own_head(array, axis):
        return jnp.where(x == 0, *jnp.split(array, 2, axis=axis))

    inputs = tok.reshape(rows, width).astype(F32)
    normed_one = (inputs * inverse_rms(inputs) * first_full).astype(BF16)
    qkv = dot(normed_one, qkv_full, NN, BF16)
    gates = dot(normed_one, gate_full, NN)
    logit = own_head(gates[:, head:], 1) + own_head(bias_full, 0)
    decay = -jax.nn.softplus(-logit) / TAU
    keep = -jnp.expm1(decay)
    chunk = min(CHUNK, 2 * block)
    slot = Slots(seqs, 2 * block, head, slots, chunk)
    units, decs, ends, end_decs = slot.ends(qkv, decay, keep)
    start = prefix(size, 1, ends, end_decs, False)
    gated, attended, probs, scores, weights, states = slot.attend(qkv, gates, decay, keep, start, units, decs, slot_full)
    shape = (seqs, 2, block, width)
    mixed = dot(gated, out_full, NT, BF16).reshape(shape)
    residual, normed_two = blend(size, 2, mixed, tokens, second_full)
    normed_two = normed_two.reshape(rows, width)
    ff = dot(normed_two, ff_full, NN)
    ff_gate, ff_up = ff[:, :hidden], ff[:, hidden:]
    sig = jax.nn.sigmoid(ff_gate)
    activated = (ff_gate * sig * ff_up).astype(BF16)
    ff_part = dot(activated, down_full, NT, BF16).reshape(shape)
    gout = gout.reshape(rows, width)
    act_grad = dot(gout, down_full, NN)
    ff_term = jnp.concatenate(
        [act_grad * ff_up * (sig + ff_gate * sig * (1.0 - sig)), act_grad * ff_gate * sig], axis=1
    ).astype(BF16)
    down_grad = dot(gout, activated, TN, BF16)
    ff_grad = dot(normed_two, ff_term, TN, BF16)
    normed_two_grad = dot(ff_term, ff_full, NT, BF16).reshape(shape)
    residual_grad, low, second_part = blend_back(size, 3, normed_two_grad, grad_out, residual, second_full)
    low = low.reshape(rows, width)
    gated_grad = dot(low, out_full, NN)
    out_grad = dot(low, gated, TN, BF16)
    gate_term, slot_part_grad, att_grad, dprobs, dscores, back_units, back_ends = slot.back_one(
        qkv, gates, decay, keep, gated_grad, attended, probs, states, decs, slot_full
    )
    finals = prefix(size, 4, back_ends, end_decs, True)
    qkv_term, decay_term = slot.back_two(
        qkv, decay, keep, probs, scores, weights, states, decs, back_units, att_grad, dprobs, dscores, finals
    )
    forget_term = (decay_term * jax.nn.sigmoid(-logit) / TAU).astype(BF16)
    none = jnp.zeros_like(forget_term)
    gates_term = jnp.concatenate(
        [gate_term, jnp.where(x == 0, forget_term, none), jnp.where(x == 0, none, forget_term)], axis=1
    )
    qkv_grad = dot(normed_one, qkv_term, TN, BF16)
    gates_grad = dot(normed_one, gates_term, TN, BF16)
    normed_one_grad = (dot(qkv_term, qkv_full, NT) + dot(gates_term, gate_full, NT)).astype(BF16).reshape(shape)
    input_grad, output, first_part = finish(size, 5, normed_one_grad, ff_part, tokens, residual, residual_grad, first_full)
    bias_part = jnp.sum(forget_term.astype(F32), axis=0)
    which = jnp.arange(2 * heads_here) == heads_here * c + x
    bias_part = jnp.where(which[:, None], bias_part[None, :], 0.0).reshape(2 * heads_here, size, slot_part)
    slot_part_sum = jnp.sum(slot_part_grad[:, 0], axis=0)

    def rows_of(array):
        array = array.reshape(size, -1)
        return jnp.pad(array, ((0, 0), (0, 128 - array.shape[1])))

    zero = jnp.zeros((size, 128), F32)
    packed = jnp.stack(
        [rows_of(first_part), rows_of(second_part), rows_of(slot_part_sum), rows_of(jnp.moveaxis(bias_part, 1, 0))] + [zero] * 4, axis=1
    )
    grads = (ff_grad, down_grad, out_grad, qkv_grad, gates_grad)
    plan = [
        (0, unit, 0, hidden, False), (0, unit, hidden, hidden, False), (1, unit, 0, hidden, False), (2, unit, 0, head, False),
        (3, unit, 0, head, False), (3, unit, head, head, False), (3, unit, 2 * head, head, False), (4, unit, 0, head, False),
        (4, unit, head, 2 * slots, True),
    ]
    gate_grad, up_grad, down_grad, output_grad, query_grad, key_grad, value_grad, outgate_grad, forget_grad, sums = scatter(
        size, 6, plan, grads, packed
    )
    bias_grad = sums[3, : 2 * heads_here * slot_part].reshape(2, heads_here, slot_part)
    bias_grad = jnp.where(c == 0, bias_grad[0], bias_grad[1])
    return (
        output, input_grad, query_grad, key_grad, value_grad, forget_grad[0], bias_grad, outgate_grad, output_grad.T,
        sums[2, : head // size], sums[0, :unit], sums[1, :unit], gate_grad, up_grad, down_grad.T,
    )


def solution(mesh):
    row, column, vector, token = P("seq", "head"), P("head", "seq"), P("seq"), P(None, "seq", None)
    return jax.shard_map(
        shards,
        mesh=mesh,
        in_specs=(token, token, row, row, row, row, column, row, column, vector, vector, vector, row, row, column),
        out_specs=(token, token, row, row, row, row, column, row, column, vector, vector, vector, row, row, column),
        check_vma=False,
    )
```

time: 4310 us -> 1200 us (0.28)
  waiting for transfers between devices: 2990 us -> 0 us
  Pallas kernels: 0 us -> 997 us
  matrix products: 532 us -> 144 us
  blocking collectives: 357 us -> 0 us
  other arithmetic: 246 us -> 8.06 us
  local copies, waits for them, and re-layouts: 123 us -> 44.6 us
    reduce_scatter x9 -> x0, waiting for transfers between devices: 2290 us -> none  [the longest x1 483 us: shards(): lax.psum_scatter(up_grad, 'seq', scatter_dimension=0, tiled=True)]
    pallas_call x0 -> x11, Pallas kernels: none -> 997 us  [the longest x1 364 us: scatter(): pl.pallas_call(functools.partial(scatter_kernel, size, [entry[:4] for ent...]
    all_gather x12 -> x0, waiting for transfers between devices: 662 us -> none  [the longest x2 195 us: prefix_2(): everything = jax.tree.map(lambda part: lax.all_gather(part, axis), shard)]
    dot_general x67 -> x15, matrix products: 521 us -> 144 us  [dot(): lax.dot_general(left, right, dims, preferred_element_type=F32).astype(dtype)]
    all_gather x6 -> x0, blocking collectives: 235 us -> none  [the longest x1 42.4 us: shards(): lax.all_gather(first_gain, 'seq', axis=0, tiled=True)]
    unnamed x2 -> x0, blocking collectives: 119 us -> none
    reduce_sum x13 -> x3, other arithmetic: 74.3 us -> 3.35 us  [the longest x1 1.68 us: shards(): bias_part = jnp.sum(forget_term.astype(F32), axis=0)]
  transfers between devices with their start and end apart: 24 -> 0, of which waited for: 18 -> 0; matrix products, arithmetic and copies ran while one was open for 9% -> 0% of each run, Pallas kernels for 0% -> 0%
where the time goes in v1:
time: 1200 us; the launch traced here: 1190 us
  Pallas kernels  997 us (83%)
  matrix products  144 us (12%)
  local copies, waits for them, and re-layouts  44.6 us (4%)
    pallas_call x1, Pallas kernels, scatter(): pl.pallas_call(functools.partial(scatter_kernel, size, [entry[:4] for ent...  364 us
    pallas_call x1, Pallas kernels, gather(): pl.pallas_call(functools.partial(gather_kernel, size, plan, len(tokens)),...  326 us
    dot_general x15, matrix products, dot(): lax.dot_general(left, right, dims, preferred_element_type=F32).astype(dtype)  144 us
    pallas_call x4, Pallas kernels, call(): pl.pallas_call(kernel, grid=grid, in_specs=[pl.BlockSpec(block, where) fo...  77.2 us
    pallas_call x1, Pallas kernels, finish(): pl.pallas_call(functools.partial(finish_kernel, size), out_shape=[jax.Sha...  58.9 us
    pallas_call x1, Pallas kernels, blend_back(): pl.pallas_call(functools.partial(blend_back_kernel, size), out_shape=[jax...  57.1 us
    pallas_call x1, Pallas kernels, blend(): pl.pallas_call(functools.partial(blend_kernel, size), out_shape=[jax.Shap...  56.6 us
    pallas_call x2, Pallas kernels, prefix(): pl.pallas_call(functools.partial(prefix_kernel, size, back), out_shape=ja...  56.2 us

profile of v1, /device:TPU:0, one launch (start us, length us, event | category | flops | bytes accessed | tf_op | source)
XLA Modules:
  0.0 1194.6 jit_solution(12619384160098568507)
XLA Ops:
  0.6 0.7 reshape.127
  2.1 0.7 stack.45.refs_6_
  2.8 1.4 copy.46
  4.1 1.1 copy.45
  5.3 1.6 copy-done
  6.8 1.6 copy-done.1
  8.4 1.1 copy-done.2
  9.5 1.1 copy-done.3
  10.7 0.9 copy-done.4
  11.6 0.9 copy-done.5
  12.6 0.9 copy-done.6
  13.5 0.9 copy-done.7
  14.5 0.8 copy-done.8
  15.2 326.4 %gather.1 = (bf16[2048,1536]{1,0:T(8,128)(2,1)S(1)}, bf16[2048,640]{1,0:T(8,128)(2,1)S(1)}, bf16[2048,512]{1,0:T(8,128)(2,1)S(1)}, bf16[256,128]{1,0:T(8,128)(2,...) custom-call(bf16[128,1024]{1,0:T(8,128)(2,1)S(1)} %copy-done.4, ...), custom_call_target="tpu_custom_call" | custom-call | tf_op jit(solution)/shard_map/gather/pallas_call | solution.py:1176
  341.6 2.7 copy-done.9
  344.3 2.4 copy-done.10
  346.7 2.0 copy-done.11
  348.7 0.9 multiply_reduce_fusion
  349.6 1.0 fusion.1
  350.7 4.9 fusion.11.gate_ref
  355.9 2.8 exponential-minus-one_negate_fusion
  358.7 11.3 convolution_convert_fusion.4.k_ref.v_ref.q_ref
  370.0 5.7 slot_ends.1
  375.6 14.8 %slot_prefix.1.start_ref = f32[2,64,1024]{2,1,0:T(8,128)} custom-call(f32[2,64,1024]{2,1,0:T(8,128)} %get-tuple-element.64.own_ref, f32[2,64,128]{2,1,0:T(8,128)} %get-tuple-element.65.dec_ref), custom_call_target="tpu_custom_call" | custom-call | tf_op jit(solution)/shard_map/slot_prefix/pallas_call | solution.py:666
  390.5 0.7 reshape_squeeze.14.gain_ref
  391.2 22.3 %slot_attend.1 = (bf16[1024,512]{1,0:T(8,128)(2,1)}, f32[1024,512]{1,0:T(8,128)}, f32[1024,64]{1,0:T(8,128)}, f32[1024,64]{1,0:T(8,128)}, f32[1024,256]{1,0:T(8,128)}, /*index=5*/f32[6,64,1024]{2,1,0:T(8,128)}) custom-call(bf16[1024,1536]{1,0:T(8,128)(2,1)} %convolution_convert_fusion.4.k_ref.v_ref.q_ref, ...), custom_call_target="tpu_custom_call" | custom-call | tf_op jit(solution)/shard_map/slot_attend/pallas_call | solution.py:301
  413.5 5.5 convolution_convert_fusion.6
  419.7 56.6 %blend.1 = (f32[256,2048]{1,0:T(8,128)}, bf16[2,2,256,2048]{3,2,1,0:T(8,128)(2,1)}) custom-call(bf16[2,2,256,2048]{3,2,1,0:T(8,128)(2,1)} %bitcast.98, bf16[2,256,2048]{2,1,0:T(8,128)(2,1)} %tokens.3, f32[1,2048]{1,0:T(1,128)} %get-tuple-element.145.gain), custom_call_target="tpu_custom_call" | custom-call | tf_op jit(solution)/shard_map/blend/pallas_call | solution.py:811
  476.3 18.8 %fusion.12 = f32[1024,2816]{1,0:T(8,128)} fusion(bf16[1024,2048]{1,0:T(8,128)(2,1)} %bitcast.112, bf16[2048,2816]{1,0:T(8,128)(2,1)} %get-tuple-element.77), kind=kOutput, calls=%fused_computation.51 | convolution fusion | flops 11811160064 | bytes 27262976 | tf_op jit(solution)/shard_map/dot_general | solution.py:1188
  495.2 12.8 %multiply_convert_fusion.2 = (bf16[1024,1408]{1,0:T(8,128)(2,1)S(1)}, bf16[1024,1408]{1,0:T(8,128)(2,1)}, bf16[1024,1408]{1,0:T(8,128)(2,1)S(1)}) fusion(f32[1024,2816]{1,0:T(8,128)} %fusion.12, bf16[1024,2048]{1,0:T(8,128)(2,1)S(1)} %bitcast.93, bf16[2048,1408]{1,0:T(8,128)(2,1)S(1)} %bitcast.92), kind=kOutput, calls=%fused_computation.11 | convolution fusion | flops 5927206912 | bytes 30146560 | tf_op jit(solution)/shard_map/dot_general | solution.py:1188
  508.0 8.3 convolution_convert_fusion.5
  516.3 17.3 %convolution_convert_fusion.3 = bf16[1024,2048]{1,0:T(8,128)(2,1)} fusion(bf16[2048,2816]{1,0:T(8,128)(2,1)} %get-tuple-element.77, bf16[1024,1408]{1,0:T(8,128)(2,1)} %get-tuple-element.140, bf16[1024,1408]{1,0:T(8,128)(2,1)S(1)} %get-tuple-element.139), kind=kOutput, calls=%fused_computation.14 | convolution fusion | flops 11824791552 | bytes 21495808 | tf_op jit(solution)/shard_map/dot_general | solution.py:1188
  533.6 57.1 %blend_back.1 = (f32[256,2048]{1,0:T(8,128)}, bf16[2,2,256,2048]{3,2,1,0:T(8,128)(2,1)}, f32[1,2048]{1,0:T(1,128)}) custom-call(bf16[2,2,256,2048]{3,2,1,0:T(8,128)(2,1)} %bitcast.97, bf16[2,256,2048]{2,1,0:T(8,128)(2,1)} %grad_out.1, f32[256,2048]{1,0:T(8,128)} %get-tuple-element.78.residual, f32[1,2048]{1,0:T(1,128)} %get-tuple-element.145.gain), custom_call_target="tpu_custom_call" | custom-call | tf_op jit(solution)/shard_map/blend_back/pallas_call | solution.py:846
  590.7 5.8 fusion.13.grad_ref
  596.6 18.7 %slot_back_one.1 = (bf16[1024,512]{1,0:T(8,128)(2,1)}, f32[2,8,512]{2,1,0:T(8,128)}, f32[1024,512]{1,0:T(8,128)}, f32[1024,64]{1,0:T(8,128)}, f32[1024,64]{1,0:T...) custom-call(bf16[1024,1536]{1,0:T(8,128)(2,1)} %convolution_convert_fusion.4.k_ref.v_ref.q_ref, ...), custom_call_target="tpu_custom_call" | custom-call | tf_op jit(solution)/shard_map/slot_back_one/pallas_call | solution.py:301
  615.3 41.4 %slot_suffix.1.end_ref = f32[2,64,1024]{2,1,0:T(8,128)} custom-call(f32[2,64,1024]{2,1,0:T(8,128)} %get-tuple-element.85.own_ref, f32[2,64,128]{2,1,0:T(8,128)} %get-tuple-element.65.dec_ref), custom_call_target="tpu_custom_call" | custom-call | tf_op jit(solution)/shard_map/slot_suffix/pallas_call | solution.py:666
  656.7 30.4 %slot_back_two.1 = (bf16[1024,1536]{1,0:T(8,128)(2,1)}, f32[1024,64]{1,0:T(8,128)}) custom-call(bf16[1024,1536]{1,0:T(8,128)(2,1)} %convolution_convert_fusion.4.k_ref.v_ref.q_ref, bf16[1024,1536]{1,0:T(8,128)(2,1)} %convolution_convert_fusion.4.k_ref.v_ref.q_ref, bf16[1024,1536]{1,0:T(8,128)(2,1)} %convolution_convert_fusion.4.k_ref.v_ref.q_ref, ...), custom_call_target="tpu_custom_call" | custom-call | tf_op jit(solution)/shard_map/slot_back_two/pallas_call | solution.py:301
  687.1 1.7 convert_reduce_fusion
  688.9 8.7 fusion.14
  697.6 5.5 add_convert_fusion
  703.1 58.9 %finish.1 = (f32[2,256,2048]{2,1,0:T(8,128)}, bf16[2,256,2048]{2,1,0:T(8,128)(2,1)}, f32[1,2048]{1,0:T(1,128)}) custom-call(bf16[2,2,256,2048]{3,2,1,0:T(8,128)(2,1)} %bitcast.96, bf16[2,2,256,2048]{3,2,1,0:T(8,128)(2,1)} %bitcast.95, bf16[2,256,2048]{2,1,0:T(8,128)(2,1)} %tokens.3, f32[256,2048]{1,0:T(8,128)} %get-tuple-element.78.residual, ...), custom_call_target="tpu_custom_call" | custom-call | tf_op jit(solution)/shard_map/finish/pallas_call | solution.py:895
  762.4 0.8 slice_reduce_fusion
  763.3 1.4 stack.51.refs_5_
  764.7 7.4 convolution_convert_fusion.7.refs_4_
  772.1 9.0 convolution_convert_fusion.1.refs_3_
  781.2 3.8 convolution_convert_fusion.8.refs_2_
  784.9 0.9 copy-done.34
  785.8 14.5 %convolution_convert_fusion.refs_0_ = bf16[2048,2816]{1,0:T(8,128)(2,1)} fusion(bf16[1024,2048]{1,0:T(8,128)(2,1)S(1)} %bitcast.113, bf16[1024,1408]{1,0:T(8,128)(2,1)S(1)} %copy-done.34, bf16[1024,1408]{1,0:T(8,128)(2,1)S(1)} %copy-done.33), kind=kOutput, calls=%fused_computation | convolution fusion | flops 11828461568 | bytes 21495808 | tf_op jit(solution)/shard_map/dot_general | solution.py:1188
  800.3 10.4 convolution_convert_fusion.2.refs_1_
  810.7 364.2 %scatter.1 = (f32[128,2816]{1,0:T(8,128)}, f32[128,2816]{1,0:T(8,128)}, f32[128,2816]{1,0:T(8,128)}, f32[128,1024]{1,0:T(8,128)}, f32[128,1024]{1,0:T(8,128)}, /...) custom-call(bf16[2048,2816]{1,0:T(8,128)(2,1)} %convolution_convert_, ...), custom_call_target="tpu_custom_call" | custom-call | tf_op jit(solution)/shard_map/scatter/pallas_call | solution.py:1118
  1174.9 3.0 copy.59
  1178.0 2.0 copy.58
  1180.0 1.5 slice_bitcast_fusion
  1181.5 0.8 fusion.5
  1183.0 1.3 slice_bitcast_fusion.2
  1184.3 1.2 slice_bitcast_fusion.4
  1185.5 1.3 copy.74
  1186.8 2.1 copy.75
  1189.0 0.8 copy.76
  1189.8 0.8 copy.77
  1190.6 0.8 copy.78
  1191.4 0.8 copy.79
  1192.2 1.1 copy.80
  1193.3 1.1 copy.81
  (97 shorter events, 2.9 us)
Async XLA Ops:
  5.2 1.6 copy-start
  6.8 1.6 copy-start.1
  8.4 1.1 copy-start.2
  9.5 1.1 copy-start.3
  10.6 0.9 copy-start.4
  11.6 0.9 copy-start.5
  12.5 0.9 copy-start.6
  13.5 0.9 copy-start.7
  14.4 0.8 copy-start.8
  341.6 2.7 copy-start.9
  344.3 2.4 copy-start.10
  346.7 2.0 copy-start.11
  348.7 2.0 copy-start.14
  350.7 5.0 copy-start.16
  419.7 75.5 %slice-start.2 = ((s8[5767168]{0:T(1024)(128)(4,1)}), s8[1572864]{0:T(1024)(128)(4,1)S(1)}, s32[]{:S(2)}) async-start(s8[5767168]{0:T(1024)(128)(4,1)} %bitcast.91), calls=%async_computation.2 | async-start | bytes 3145728
  476.3 18.9 %slice-start.3 = ((s8[5767168]{0:T(1024)(128)(4,1)}), s8[4194304]{0:T(1024)(128)(4,1)S(1)}, s32[]{:S(2)}) async-start(s8[5767168]{0:T(1024)(128)(4,1)} %bitcast.91), calls=%async_computation.3 | async-start | bytes 8388608
  476.3 18.9 %copy-start.12 = (bf16[2,2,256,2048]{3,2,1,0:T(8,128)(2,1)S(1)}, bf16[2,2,256,2048]{3,2,1,0:T(8,128)(2,1)}, u32[]{:S(2)}) copy-start(bf16[2,2,256,2048]{3,2,1,0:T(8,128)(2,1)} %copy-done.11) | copy-start | bytes 12582916
  507.9 8.3 copy-start.35
  507.9 8.3 copy-start.32
  596.6 92.3 %slice-start = ((s8[6291456]{0:T(1024)(128)(4,1)}), s8[4194304]{0:T(1024)(128)(4,1)S(1)}, s32[]{:S(2)}) async-start(s8[6291456]{0:T(1024)(128)(4,1)} %bitcast.89), calls=%async_computation | async-start | bytes 8388608
  656.7 32.2 %slice-start.1 = ((s8[6291456]{0:T(1024)(128)(4,1)}), s8[2097152]{0:T(1024)(128)(4,1)S(1)}, s32[]{:S(2)}) async-start(s8[6291456]{0:T(1024)(128)(4,1)} %bitcast.89), calls=%async_computation.1 | async-start | bytes 4194304
  688.8 8.7 copy-start.15
  688.9 8.7 copy-start.31
  703.1 60.2 %copy-start.26 = (f32[1,2048]{1,0:T(1,128)S(1)}, f32[1,2048]{1,0:T(1,128)}, u32[]{:S(2)}) copy-start(f32[1,2048]{1,0:T(1,128)} %get-tuple-element.93) | copy-start | bytes 24580
  764.7 7.4 copy-start.17
  764.7 7.4 copy-start.29
  772.1 9.0 copy-start.28
  772.1 9.0 copy-start.30
  781.1 3.8 copy-start.27
  781.1 3.8 copy-start.33
  781.1 4.7 copy-start.34
  785.8 14.5 %copy-start.13 = (bf16[2,2,256,2048]{3,2,1,0:T(8,128)(2,1)S(1)}, bf16[2,2,256,2048]{3,2,1,0:T(8,128)(2,1)}, u32[]{:S(2)}) copy-start(bf16[2,2,256,2048]{3,2,1,0:T(8,128)(2,1)} %copy-done.11) | copy-start | bytes 12582916
  1174.9 10.6 copy-start.19
  1183.0 3.9 copy-start.18
  1186.8 2.1 copy-start.25
  1186.8 2.9 copy-start.24
  1186.8 3.7 copy-start.23
  1186.8 4.5 copy-start.22
  1189.0 3.2 copy-start.21
  1189.0 4.3 copy-start.20

commit v2 on v1

--- a/solution.py
+++ b/solution.py
@@ -709,6 +709,10 @@
         for r in range(STRIPS):
             self.sib_copy(False, r).start()
 
+    def sib_all(self, far):
+        for r in range(STRIPS):
+            self.sib_copy(far, r).start()
+
     def cross(self, r):
         p = self.p
         self.sib_copy(True, r).wait_recv()
@@ -905,6 +909,244 @@
         name="finish",
     )(part, ff_part, tokens, residual, residual_grad, gain)
 
+
+def ends_chunk(k, v, decay, keep, tail):
+    weight = halves(jnp.exp(exact_sums(tail, decay)) * keep)
+    unit_k = dot3(weight, halves(silu(k.astype(F32))), TN)
+    unit_v = mm(weight[0], v, TN) + mm(weight[1], v, TN)
+    return jnp.concatenate([unit_k, unit_v], axis=1), jnp.exp(columns_total(decay))
+
+
+def powers_of(table, count, levels, decay):
+    powers = jnp.exp(exact_sums(table, decay))
+    return [powers[l * count : (l + 1) * count] for l in range(levels)], [
+        powers[l * count : (l + 1) * count] for l in range(levels, table.shape[0] // count)
+    ]
+
+
+class Prefix:
+    def __init__(self, place, back, own, dec, start, peer, peer_dec, line, out, sems):
+        p = self.p = place
+        self.own, self.dec, self.start_ref, self.peer, self.peer_dec = own, dec, start, peer, peer_dec
+        self.line, self.out = line, out
+        self.p_sem, self.d_sem, self.l_sem = sems
+        seqs, slots, width = own.shape
+        self.half = width // 2
+        self.pieces = [(b, h) for b in range(seqs) for h in range(2)]
+        if back:
+            self.has_prev, self.has_next, self.after = p.has_up(), p.has_down(), p.down()
+        else:
+            self.has_prev, self.has_next, self.after = p.has_down(), p.has_up(), p.up()
+        self.first = ((p.b == 1) if back else (p.b == 0)).astype(F32)
+
+    def cut(self, ref, i):
+        b, h = self.pieces[i]
+        return ref.at[b, :, pl.ds(h * self.half, self.half)]
+
+    def peer_copy(self, i):
+        return remote(self.cut(self.own, i), self.cut(self.peer, i), self.p_sem.at[0, i], self.p_sem.at[1, i], self.p.across())
+
+    def line_copy(self, i):
+        return remote(self.cut(self.out, i), self.cut(self.line, i), self.l_sem.at[0, i], self.l_sem.at[1, i], self.after)
+
+    def dec_copy(self):
+        return remote(self.dec, self.peer_dec, self.d_sem.at[0], self.d_sem.at[1], self.p.across())
+
+    def start(self):
+        self.dec_copy().start()
+        for i in range(len(self.pieces)):
+            self.peer_copy(i).start()
+
+    def run(self):
+        self.dec_copy().wait_recv()
+        for i, (b, _) in enumerate(self.pieces):
+            self.peer_copy(i).wait_recv()
+            dec_own = spread(self.dec[b], self.half)
+            dec_peer = spread(self.peer_dec[b], self.half)
+            own, other = self.cut(self.own, i)[...], self.cut(self.peer, i)[...]
+            first = self.first
+            both = first * (dec_peer * own + other) + (1.0 - first) * (dec_own * other + own)
+            here, result = self.cut(self.out, i), self.cut(self.start_ref, i)
+
+            def go_on(i=i):
+                self.line_copy(i).wait_recv()
+                came = self.cut(self.line, i)[...]
+                here[...] = dec_own * dec_peer * came + both
+                result[...] = first * came + (1.0 - first) * (dec_peer * came + other)
+
+            def begin():
+                here[...] = both
+                result[...] = (1.0 - first) * other
+
+            pl.when(self.has_prev)(go_on)
+            pl.when(jnp.logical_not(self.has_prev))(begin)
+            pl.when(self.has_next)(lambda i=i: self.line_copy(i).start())
+
+    def finish(self):
+        self.dec_copy().wait_send()
+        for i in range(len(self.pieces)):
+            self.peer_copy(i).wait_send()
+            pl.when(self.has_next)(lambda i=i: self.line_copy(i).wait_send())
+
+
+def prefix_scratch(seqs, slots, width):
+    count = 2 * seqs
+    return [
+        pltpu.VMEM((seqs, slots, width), F32), pltpu.VMEM((seqs, slots, width), F32), pltpu.VMEM((seqs, slots, 128), F32),
+        pltpu.VMEM((seqs, slots, width), F32), pltpu.VMEM((seqs, slots, width), F32),
+        pltpu.SemaphoreType.DMA((2, count)), pltpu.SemaphoreType.DMA((2,)), pltpu.SemaphoreType.DMA((2, count)),
+    ]
+
+
+def take(refs, count):
+    return refs[:count], refs[count:]
+
+
+class Weave:
+    def __init__(self, steps):
+        self.steps = list(steps)
+
+    def run(self, count):
+        for step in self.steps[:count]:
+            step()
+        self.steps = self.steps[count:]
+
+    def rest(self):
+        self.run(len(self.steps))
+
+
+def blocks_in_order(p, seqs):
+    def block(i):
+        b = jnp.where(i < 2, 1 - p.c, p.c)
+        x = jnp.where(lax.rem(i, 2) == 0, 1 - p.x, p.x)
+        return b, x
+
+    return block
+
+
+def forward_kernel(size, plan, levels, *refs):
+    p = Place(size)
+    (qkv, gates, decay, keep, gain, out_w, tokens, gain2, paths, masks), refs = take(refs, 10)
+    shard_refs, refs = take(refs, len(plan))
+    (gated, attended, probs, scores, weights, states, decs, end_dec, residual, normed), refs = take(refs, 10)
+    fulls, refs = take(refs, max(i for i, _, _, _, _ in plan) + 1)
+    (units, part, total), refs = take(refs, 3)
+    (start, *prefix_refs), refs = take(refs, 8)
+    fold_refs, refs = take(refs, 5)
+    share_sems, refs = take(refs, 2)
+    count = paths.shape[1]
+    head = gated.shape[1]
+    seqs = tokens.shape[0]
+    slots = keep.shape[1]
+    greet(p, sibling=True)
+    work = []
+    for n, (i, unit, offset, width, late) in enumerate(plan):
+        work.append(Gather(p, shard_refs[n], fulls[i], unit, offset, width, refs[4 * n : 4 * n + 4], late))
+    weave = Weave(gather_ops(work, 3))
+    weave.run(3)
+    tail = paths[(levels + 1) * count :, :]
+
+    def ends(b):
+        for j in range(2):
+            rows = pl.ds((b * 2 + j) * count, count)
+            unit, dec = ends_chunk(
+                qkv[rows, head : 2 * head], qkv[rows, 2 * head :], decay[rows, :], keep[rows, :], tail
+            )
+            units[b, j] = unit
+            decs[b, j] = dec
+        total[b] = spread(dec, 2 * head) * units[b, 0] + unit
+        end_dec[b] = decs[b, 0] * dec
+
+    for b in range(seqs):
+        ends(b)
+    carry = Prefix(p, False, total, end_dec, start, *prefix_refs[:4], prefix_refs[4:])
+    carry.start()
+    weave.run(1)
+    carry.run()
+    for b in range(seqs):
+        states[3 * b] = start[b]
+        for j in range(2):
+            states[3 * b + j + 1] = spread(decs[b, j], 2 * head) * states[3 * b + j] + units[b, j]
+    weave.run(1)
+    diag = on_diagonal(count)
+    order = blocks_in_order(p, seqs)
+    fold = Fold(p, part, *fold_refs[:3], fold_refs[3:])
+    share = Share(p, normed, share_sems)
+
+    def attend(i, nothing):
+        b, j = order(i)
+        rows = pl.ds(pl.multiple_of((b * 2 + j) * count, count), count)
+        here = keep[rows, :]
+        ratios, (growth,) = powers_of(paths[: (levels + 1) * count, :], count, levels, decay[rows, :])
+        query = halves(silu(qkv[rows, :head].astype(F32)) * head ** (-0.5))
+        keys = halves(silu(qkv[rows, head : 2 * head].astype(F32)))
+        state = states[3 * b + j]
+        pair = dot3(query, keys, NT)
+        score = mix(pair, ratios, here, masks, jnp.sum(pair * diag, axis=1, keepdims=True))
+        score += growth * dot3(query, halves(state[:, :head]), NT)
+        raised = jnp.exp(score - jnp.max(score, axis=1, keepdims=True))
+        prob = raised / jnp.sum(raised, axis=1, keepdims=True)
+        weight = unmix(prob, ratios, here, masks, diag)
+        values = qkv[rows, 2 * head :]
+        whi, wlo = halves(weight)
+        result = mm(whi, values, NN) + mm(wlo, values, NN)
+        result += dot3(halves(prob * growth), halves(state[:, head:]), NN)
+        scale = lax.rsqrt(jnp.mean(result * result, axis=1, keepdims=True) + EPS)
+        low = bf(result * scale * gain[...] * silu(gates[rows, :head]))
+        gated[rows, :] = low
+        attended[rows, :] = result
+        probs[rows, :] = prob
+        scores[rows, :] = score
+        weights[rows, :] = weight
+        part[b, j] = bf(mm(low, out_w[...], NT))
+        pl.when(i == 0)(lambda: fold.sib_all(True))
+        pl.when(i == 1)(lambda: fold.sib_all(False))
+        return nothing
+
+    lax.fori_loop(0, 2, attend, 0)
+    weave.run(1)
+    lax.fori_loop(2, 3, attend, 0)
+    for r in range(STRIPS):
+        fold.cross(r)
+    lax.fori_loop(3, 4, attend, 0)
+    weave.run(1)
+    for r in range(STRIPS):
+        value = tokens[p.c, fold.strip(r)].astype(F32) + fold.total(r)
+        residual[fold.strip(r)] = value
+        share.put(r, bf(value * inverse_rms(value) * gain2[...]))
+    weave.run(2)
+    for r in range(STRIPS):
+        share.forward(r)
+    weave.rest()
+    share.finish()
+    fold.finish()
+    carry.finish()
+
+
+def forward(size, number, slot, plan, fulls, qkv, gates, decay, keep, gain, out_w, tokens, gain2, shards):
+    seqs, block, width = tokens.shape
+    h, m, n, rows = slot.head, slot.slots, slot.chunks, slot.seqs * slot.rows
+    shape = jax.ShapeDtypeStruct
+    outs = [
+        shape((rows, h), BF16), shape((rows, h), F32), shape((rows, m), F32), shape((rows, m), F32), shape((rows, slot.chunk), F32),
+        shape((seqs * (n + 1), m, 2 * h), F32), shape((seqs, n, m, 128), F32), shape((seqs, m, 128), F32),
+        shape((block, width), F32), shape((seqs, 2, block, width), BF16),
+    ]
+    scratch = [
+        pltpu.VMEM((seqs, n, m, 2 * h), F32), pltpu.VMEM((seqs, 2, block, width), BF16), pltpu.VMEM((seqs, m, 2 * h), F32),
+    ]
+    scratch += prefix_scratch(seqs, m, 2 * h) + fold_scratch(block, width) + SHARE_SEMS
+    for _ in plan:
+        scratch += gather_sems(size // 4)
+    return pl.pallas_call(
+        functools.partial(forward_kernel, size, plan, slot.levels),
+        out_shape=outs + [shape(full, BF16) for full in fulls],
+        in_specs=[VM] * 10 + [ANY] * len(shards),
+        out_specs=[VM] * 10 + [ANY] * len(fulls),
+        scratch_shapes=scratch,
+        compiler_params=remote_params(number, 60),
+        name="attend_forward",
+    )(qkv, gates, decay, keep, gain, out_w, tokens, gain2, slot.paths, slot.masks, *shards)
 
 class Scatter:
     def __init__(self, place, grad, out, unit, offset, width, bufs, sems):
@@ -1128,18 +1370,24 @@
 
 class Swap:
     def __init__(self, place, own, both, sems):
-        self.p, self.own, self.both, self.sems = place, own, both, sems
+        p = self.p = place
+        self.keep = pltpu.make_async_copy(own, both.at[:, p.x], sems.at[0])
+        self.cross = remote(own.at[p.c], both.at[p.c, p.x], sems.at[1], sems.at[2], p.partner())
+        came = both.at[p.c, 1 - p.x]
+        self.hand = remote(came, came, sems.at[3], sems.at[4], p.sibling())
 
     def start(self):
-        p = self.p
-        self.cross = remote(self.own, self.both.at[:, p.x], self.sems.at[0], self.sems.at[1], p.partner())
-        self.keep = pltpu.make_async_copy(self.own, self.both.at[:, p.x], self.sems.at[2])
         self.cross.start()
         self.keep.start()
 
+    def forward(self):
+        self.cross.wait_recv()
+        self.hand.start()
+
     def finish(self):
         self.keep.wait()
-        self.cross.wait()
+        self.cross.wait_send()
+        self.hand.wait()
 
 
 def gather_kernel(size, plan, swaps, *refs):
@@ -1148,18 +1396,19 @@
     fulls = max(i for i, _, _, _, _ in plan) + 1
     ins, refs = refs[: shards + swaps], refs[shards + swaps :]
     outs, refs = refs[: fulls + swaps], refs[fulls + swaps :]
-    greet(p)
+    greet(p, sibling=True)
     work = []
     for n, (i, unit, offset, width, late) in enumerate(plan):
         work.append(Gather(p, ins[n], outs[i], unit, offset, width, refs[4 * n : 4 * n + 4], late))
     moves = [Swap(p, ins[shards + n], outs[fulls + n], refs[4 * shards + n]) for n in range(swaps)]
-    steps = gather_ops(work, 3)
-    for step in steps[: -len(work)]:
-        step()
+    weave = Weave(gather_ops(work, len(work)))
+    weave.run(len(work))
     for move in moves:
         move.start()
-    for step in steps[-len(work) :]:
-        step()
+    weave.run(len(weave.steps) - len(work))
+    for move in moves:
+        move.forward()
+    weave.rest()
     for move in moves:
         move.finish()
 
@@ -1172,14 +1421,14 @@
     shapes = [jax.ShapeDtypeStruct(shape, BF16) for shape in fulls]
     for array in tokens:
         shapes.append(jax.ShapeDtypeStruct((array.shape[0], 2) + array.shape[1:], BF16))
-        scratch.append(pltpu.SemaphoreType.DMA((3,)))
+        scratch.append(pltpu.SemaphoreType.DMA((5,)))
     return pl.pallas_call(
         functools.partial(gather_kernel, size, plan, len(tokens)),
         out_shape=shapes,
         in_specs=[ANY] * (len(shards) + len(tokens)),
         out_specs=[ANY] * len(shapes),
         scratch_shapes=scratch,
-        compiler_params=remote_params(number, 16),
+        compiler_params=remote_params(number, 60),
         name="gather",
     )(*shards, *tokens)
 
@@ -1211,15 +1460,11 @@
         (0, unit, 0, head, False), (0, unit, head, head, False), (0, unit, 2 * head, head, False),
         (1, unit, 0, head, False), (1, unit, head, 2 * slots, False), (2, unit, 0, head, False),
         (3, 16, 0, 128, False),
-        (4, unit, 0, hidden, False), (4, unit, hidden, hidden, False), (5, unit, 0, hidden, False),
     ]
-    fulls = [
-        (width, 3 * head), (width, head + 2 * slots), (width, head), (16 * size, 128), (width, 2 * hidden), (width, hidden),
-    ]
-    qkv_full, gate_full, out_full, small_full, ff_full, down_full, tok, gout = gather(
+    fulls = [(width, 3 * head), (width, head + 2 * slots), (width, head), (16 * size, 128)]
+    qkv_full, gate_full, out_full, small_full, tok, gout = gather(
         size, 0, plan,
-        (query_weight, key_weight, value_weight, outgate_weight, forget_weight, output_weight.T, pack, gate_weight, up_weight,
-         down_weight.T),
+        (query_weight, key_weight, value_weight, outgate_weight, forget_weight, output_weight.T, pack),
         fulls, (tokens, grad_out),
     )
     small = small_full.reshape(size, 16, 128).astype(F32)
@@ -1241,12 +1486,13 @@
     keep = -jnp.expm1(decay)
     chunk = min(CHUNK, 2 * block)
     slot = Slots(seqs, 2 * block, head, slots, chunk)
-    units, decs, ends, end_decs = slot.ends(qkv, decay, keep)
-    start = prefix(size, 1, ends, end_decs, False)
-    gated, attended, probs, scores, weights, states = slot.attend(qkv, gates, decay, keep, start, units, decs, slot_full)
+    ff_plan = [(0, unit, 0, hidden, False), (0, unit, hidden, hidden, False), (1, unit, 0, hidden, False)]
+    (gated, attended, probs, scores, weights, states, decs, end_decs, residual, normed_two, ff_full, down_full) = forward(
+        size, 1, slot, ff_plan, [(width, 2 * hidden), (width, hidden)], qkv, gates, decay, keep, slot_full, out_full, tokens,
+        second_full, (gate_weight, up_weight, down_weight.T),
+    )
+    decs = decs.reshape(seqs * slot.chunks, slots, 128)
     shape = (seqs, 2, block, width)
-    mixed = dot(gated, out_full, NT, BF16).reshape(shape)
-    residual, normed_two = blend(size, 2, mixed, tokens, second_full)
     normed_two = normed_two.reshape(rows, width)
     ff = dot(normed_two, ff_full, NN)
     ff_gate, ff_up = ff[:, :hidden], ff[:, hidden:]

time: 1200 us -> 1140 us (0.950)
  Pallas kernels: 997 us -> 950 us
  local copies, waits for them, and re-layouts: 44.6 us -> 30.7 us
    pallas_call x1, Pallas kernels: 326 us -> 154 us  [gather(): pl.pallas_call(functools.partial(gather_kernel, size, plan, len(tokens)),...]
    pallas_call x1, Pallas kernels: 56.6 us -> 225 us  [forward(): pl.pallas_call(functools.partial(forward_kernel, size, plan, slot.levels)...]
    pallas_call x4 -> x2, Pallas kernels: 77.2 us -> 49.1 us  [call(): pl.pallas_call(kernel, grid=grid, in_specs=[pl.BlockSpec(block, where) fo...]
    unnamed x94 -> x78, local copies, waits for them, and re-layouts: 34.4 us -> 17.7 us
    pallas_call x2 -> x1, Pallas kernels: 56.2 us -> 39.9 us  [prefix(): pl.pallas_call(functools.partial(prefix_kernel, size, back), out_shape=ja...]
    dot_general x15 -> x14, matrix products: 144 us -> 138 us  [dot(): lax.dot_general(left, right, dims, preferred_element_type=F32).astype(dtype)]
where the time goes in v2:
time: 1140 us; the launch traced here: 1130 us
  Pallas kernels  950 us (83%)
  matrix products  138 us (12%)
  local copies, waits for them, and re-layouts  30.7 us (3%)
    pallas_call x1, Pallas kernels, scatter(): pl.pallas_call(functools.partial(scatter_kernel, size, [entry[:4] for ent...  365 us
    pallas_call x1, Pallas kernels, forward(): pl.pallas_call(functools.partial(forward_kernel, size, plan, slot.levels)...  225 us
    pallas_call x1, Pallas kernels, gather(): pl.pallas_call(functools.partial(gather_kernel, size, plan, len(tokens)),...  154 us
    dot_general x14, matrix products, dot(): lax.dot_general(left, right, dims, preferred_element_type=F32).astype(dtype)  138 us
    pallas_call x1, Pallas kernels, finish(): pl.pallas_call(functools.partial(finish_kernel, size), out_shape=[jax.Sha...  60 us
    pallas_call x1, Pallas kernels, blend_back(): pl.pallas_call(functools.partial(blend_back_kernel, size), out_shape=[jax...  57.3 us
    pallas_call x2, Pallas kernels, call(): pl.pallas_call(kernel, grid=grid, in_specs=[pl.BlockSpec(block, where) fo...  49.1 us
    pallas_call x1, Pallas kernels, prefix(): pl.pallas_call(functools.partial(prefix_kernel, size, back), out_shape=ja...  39.9 us

profile of v2, /device:TPU:0, one launch (start us, length us, event | category | flops | bytes accessed | tf_op | source)
XLA Modules:
  0.0 1129.4 jit_solution(15918308271078615714)
XLA Ops:
  0.7 0.7 reshape.127
  1.4 0.7 pad_bitcast_fusion
  2.1 1.9 stack.45.refs_6_
  3.9 1.8 copy.45
  5.7 154.1 %gather.1 = (bf16[2048,1536]{1,0:T(8,128)(2,1)}, bf16[2048,640]{1,0:T(8,128)(2,1)}, bf16[2048,512]{1,0:T(8,128)(2,1)}, bf16[256,128]{1,0:T(8,128)(2,1)}, bf16[2,...) custom-call(bf16[128,1024]{1,0:T(8,128)(2,1)} %refs_0_.1, bf16[128,1024]{1,0:T(8,128)(2,1)} %refs_1_.1, ...), custom_call_target="tpu_custom_call" | custom-call | tf_op jit(solution)/shard_map/gather/pallas_call | solution.py:1425
  159.8 0.8 slice.67
  160.5 0.1 copy.62
  160.6 0.1 copy.50
  160.7 0.1 select_n.60
  160.8 0.9 slice.66
  161.7 3.3 multiply_reduce_fusion
  165.1 1.0 fusion.1
  166.1 0.7 copy-done.22
  166.8 3.4 fusion.11.refs_1_.gate_ref
  170.3 1.8 exponential-minus-one_negate_fusion
  172.1 0.0 copy-start.9
  172.1 8.1 convolution_convert_fusion.4.refs_0_.q_ref.v_ref.k_ref
  180.2 0.6 slice_bitcast_fusion.5
  180.9 0.7 reshape_squeeze.14.refs_4_.gain_ref
  181.5 1.1 copy.53
  182.7 224.8 %attend_forward.1 = (bf16[1024,512]{1,0:T(8,128)(2,1)}, f32[1024,512]{1,0:T(8,128)}, f32[1024,64]{1,0:T(8,128)}, f32[1024,64]{1,0:T(8,128)}, f32[1024,256]{1,0:T...) custom-call(bf16[1024,1536]{1,0:T(8,128)(2,1)} %convolution_convert_, ...), custom_call_target="tpu_custom_call" | custom-call | tf_op jit(solution)/shard_map/attend_forward/pallas_call | solution.py:1141
  407.5 19.1 %fusion.12 = f32[1024,2816]{1,0:T(8,128)} fusion(bf16[1024,2048]{1,0:T(8,128)(2,1)} %bitcast.109, bf16[2048,2816]{1,0:T(8,128)(2,1)} %get-tuple-element.71), kind=kOutput, calls=%fused_computation.50 | convolution fusion | flops 11811160064 | bytes 27262976 | tf_op jit(solution)/shard_map/dot_general | solution.py:1437
  426.6 12.3 %multiply_convert_fusion.2 = (bf16[1024,1408]{1,0:T(8,128)(2,1)S(1)}, bf16[1024,1408]{1,0:T(8,128)(2,1)S(1)}, bf16[1024,1408]{1,0:T(8,128)(2,1)}) fusion(f32[1024,2816]{1,0:T(8,128)} %fusion.12, bf16[1024,2048]{1,0:T(8,128)(2,1)S(1)} %bitcast.107, bf16[2048,1408]{1,0:T(8,128)(2,1)S(1)} %copy-done.16), kind=kOutput, calls=%fused_computation.11 | convolution fusion | flops 5927206912 | bytes 30146560 | tf_op jit(solution)/shard_map/dot_general | solution.py:1437
  438.9 12.2 %convolution_convert_fusion.5 = bf16[1024,2048]{1,0:T(8,128)(2,1)} fusion(bf16[1024,1408]{1,0:T(8,128)(2,1)} %get-tuple-element.137, bf16[2048,1408]{1,0:T(8,128)(2,1)S(1)} %copy-done.16), kind=kOutput, calls=%fused_computation.16 | convolution fusion | flops 5907677184 | bytes 12845056 | tf_op jit(solution)/shard_map/dot_general | solution.py:1437
  451.1 16.5 %convolution_convert_fusion.3 = bf16[1024,2048]{1,0:T(8,128)(2,1)} fusion(bf16[2048,2816]{1,0:T(8,128)(2,1)} %get-tuple-element.71, bf16[1024,1408]{1,0:T(8,128)(2,1)S(1)} %get-tuple-element.136, bf16[1024,1408]{1,0:T(8,128)(2,1)S(1)} %get-tuple-element.135), kind=kOutput, calls=%fused_computation.14 | convolution fusion | flops 11824791552 | bytes 21495808 | tf_op jit(solution)/shard_map/dot_general | solution.py:1437
  467.5 57.3 %blend_back.1 = (f32[256,2048]{1,0:T(8,128)}, bf16[2,2,256,2048]{3,2,1,0:T(8,128)(2,1)}, f32[1,2048]{1,0:T(1,128)}) custom-call(bf16[2,2,256,2048]{3,2,1,0:T(8,128)(2,1)} %bitcast.83, bf16[2,256,2048]{2,1,0:T(8,128)(2,1)} %grad_out.1, f32[256,2048]{1,0:T(8,128)} %get-tuple-element.72.residual, f32[1,2048]{1,0:T(1,128)} %get-tuple-element.141.refs_7_.gain), custom_call_target="tpu_custom_call" | custom-call | tf_op jit(solution)/shard_map/blend_back/pallas_call | solution.py:850
  524.8 5.8 fusion.13.grad_ref
  530.7 18.6 %slot_back_one.1 = (bf16[1024,512]{1,0:T(8,128)(2,1)}, f32[2,8,512]{2,1,0:T(8,128)}, f32[1024,512]{1,0:T(8,128)}, f32[1024,64]{1,0:T(8,128)}, f32[1024,64]{1,0:T...) custom-call(bf16[1024,1536]{1,0:T(8,128)(2,1)} %convolution_convert_fusion.4.refs_0_.q_ref.v_ref.k_ref, ...), custom_call_target="tpu_custom_call" | custom-call | tf_op jit(solution)/shard_map/slot_back_one/pallas_call | solution.py:301
  549.3 39.9 %slot_suffix.1.end_ref = f32[2,64,1024]{2,1,0:T(8,128)} custom-call(f32[2,64,1024]{2,1,0:T(8,128)} %get-tuple-element.79.own_ref, f32[2,64,128]{2,1,0:T(8,128)} %get-tuple-element.80.dec_ref), custom_call_target="tpu_custom_call" | custom-call | tf_op jit(solution)/shard_map/slot_suffix/pallas_call | solution.py:666
  589.2 30.5 %slot_back_two.1 = (bf16[1024,1536]{1,0:T(8,128)(2,1)}, f32[1024,64]{1,0:T(8,128)}) custom-call(bf16[1024,1536]{1,0:T(8,128)(2,1)} %convolution_convert_fusion.4.refs_0_.q_ref.v_ref.k_ref, bf16[1024,1536]{1,0:T(8,128)(2,1)} %convolution_convert_fusion.4.refs_0_.q_ref.v_ref.k_ref, bf16[1024,1536]{1,0:T(8,128)(2,1)} %convolution_convert_fusion.4.refs_0_.q_ref.v_ref.k_ref, ...), custom_call_target="tpu_custom_call" | custom-call | tf_op jit(solution)/shard_map/slot_back_two/pallas_call | solution.py:301
  619.7 1.7 convert_reduce_fusion
  621.4 0.0 copy-start.24
  621.4 9.8 fusion.14
  631.3 5.2 add_convert_fusion
  636.5 60.0 %finish.1 = (f32[2,256,2048]{2,1,0:T(8,128)}, bf16[2,256,2048]{2,1,0:T(8,128)(2,1)}, f32[1,2048]{1,0:T(1,128)}) custom-call(bf16[2,2,256,2048]{3,2,1,0:T(8,128)(2,1)} %bitcast.82, bf16[2,2,256,2048]{3,2,1,0:T(8,128)(2,1)} %bitcast.81, bf16[2,256,2048]{2,1,0:T(8,128)(2,1)} %tokens.1, f32[256,2048]{1,0:T(8,128)} %get-tuple-element.72.residual, ...), custom_call_target="tpu_custom_call" | custom-call | tf_op jit(solution)/shard_map/finish/pallas_call | solution.py:899
  696.5 0.1 broadcast_in_dim.38
  696.5 0.1 copy.56
  696.6 0.1 copy.57
  696.7 0.1 broadcast_in_dim.35
  696.8 0.1 broadcast_in_dim.36
  696.9 0.8 slice_reduce_fusion
  697.7 0.1 reshape.135
  697.8 1.4 stack.51.refs_5_
  699.2 7.4 convolution_convert_fusion.6.refs_4_
  706.6 3.7 convolution_convert_fusion.7.refs_2_
  710.3 16.7 %convolution_convert_fusion.refs_0_ = bf16[2048,2816]{1,0:T(8,128)(2,1)} fusion(bf16[1024,2048]{1,0:T(8,128)(2,1)S(1)} %bitcast.110, bf16[1024,1408]{1,0:T(8,128)(2,1)} %copy-done.28, bf16[1024,1408]{1,0:T(8,128)(2,1)S(1)} %copy-done.27), kind=kOutput, calls=%fused_computation | convolution fusion | flops 11828461568 | bytes 21495808 | tf_op jit(solution)/shard_map/dot_general | solution.py:1437
  727.0 8.6 convolution_convert_fusion.1.refs_3_
  735.6 8.6 convolution_convert_fusion.2.refs_1_
  744.3 365.2 %scatter.1 = (f32[128,2816]{1,0:T(8,128)}, f32[128,2816]{1,0:T(8,128)}, f32[128,2816]{1,0:T(8,128)}, f32[128,1024]{1,0:T(8,128)}, f32[128,1024]{1,0:T(8,128)}, /...) custom-call(bf16[2048,2816]{1,0:T(8,128)(2,1)} %convolution_convert_, ...), custom_call_target="tpu_custom_call" | custom-call | tf_op jit(solution)/shard_map/scatter/pallas_call | solution.py:1360
  1109.5 3.0 copy.59
  1112.6 2.0 copy.58
  1114.6 1.5 slice_bitcast_fusion
  1116.1 0.8 fusion.5
  1116.9 0.6 select_n.67
  1117.5 1.3 slice_bitcast_fusion.2
  1118.9 1.2 slice_bitcast_fusion.4
  1120.1 1.3 copy.74
  1121.4 2.1 copy.75
  1123.5 0.8 copy.76
  1124.3 0.8 copy.77
  1125.1 0.8 copy.78
  1125.9 0.8 copy.79
  1126.7 1.1 copy.80
  1127.8 1.1 copy.81
  (76 shorter events, 0.3 us)
Async XLA Ops:
  160.8 4.3 copy-start.1
  165.1 1.7 copy-start.22
  165.1 7.0 slice-start
  166.1 6.0 copy-start.2
  166.8 5.3 slice-start.1
  170.2 10.0 copy-start
  172.1 8.1 copy-start.14
  172.1 9.4 copy-start.9
  407.4 19.1 %copy-start.16 = (bf16[2048,1408]{1,0:T(8,128)(2,1)S(1)}, bf16[2048,1408]{1,0:T(8,128)(2,1)}, u32[]{:S(2)}) copy-start(bf16[2048,1408]{1,0:T(8,128)(2,1)} %get-tuple-element.69) | copy-start | bytes 17301508
  407.5 19.1 %copy-start.17 = (bf16[2,2,256,2048]{3,2,1,0:T(8,128)(2,1)S(1)}, bf16[2,2,256,2048]{3,2,1,0:T(8,128)(2,1)}, u32[]{:S(2)}) copy-start(bf16[2,2,256,2048]{3,2,1,0:T(8,128)(2,1)} %get-tuple-element.68) | copy-start | bytes 12582916
  438.9 12.2 %copy-start.26 = (bf16[1024,1408]{1,0:T(8,128)(2,1)}, bf16[1024,1408]{1,0:T(8,128)(2,1)S(1)}, u32[]{:S(2)}) copy-start(bf16[1024,1408]{1,0:T(8,128)(2,1)S(1)} %get-tuple-element.135) | copy-start | bytes 8650756
  438.9 12.2 %copy-start.28 = (bf16[1024,1408]{1,0:T(8,128)(2,1)}, bf16[1024,1408]{1,0:T(8,128)(2,1)S(1)}, u32[]{:S(2)}) copy-start(bf16[1024,1408]{1,0:T(8,128)(2,1)S(1)} %get-tuple-element.136) | copy-start | bytes 8650756
  467.5 57.3 %copy-start.6 = (bf16[2048,512]{1,0:T(8,128)(2,1)S(1)}, bf16[2048,512]{1,0:T(8,128)(2,1)}, u32[]{:S(2)}) copy-start(bf16[2048,512]{1,0:T(8,128)(2,1)} %get-tuple-element.62.refs_5_) | copy-start | bytes 6291460
  621.4 9.9 copy-start.24
  636.5 61.3 %copy-start.15 = (f32[1,2048]{1,0:T(1,128)S(1)}, f32[1,2048]{1,0:T(1,128)}, u32[]{:S(2)}) copy-start(f32[1,2048]{1,0:T(1,128)} %get-tuple-element.89) | copy-start | bytes 24580
  636.5 62.7 %copy-start.25 = (bf16[1024,512]{1,0:T(8,128)(2,1)S(1)}, bf16[1024,512]{1,0:T(8,128)(2,1)}, u32[]{:S(2)}) copy-start(bf16[1024,512]{1,0:T(8,128)(2,1)} %get-tuple-element.82) | copy-start | bytes 3145732
  699.2 7.4 copy-start.20
  699.2 7.4 copy-start.23
  706.6 3.7 copy-start.19
  706.6 3.7 copy-start.27
  710.3 16.7 %copy-start.3 = (bf16[1024,2048]{1,0:T(8,128)(2,1)S(1)}, bf16[1024,2048]{1,0:T(8,128)(2,1)}, u32[]{:S(2)}) copy-start(bf16[1024,2048]{1,0:T(8,128)(2,1)} %copy-done.2) | copy-start | bytes 12582916
  710.3 16.7 %copy-start.21 = (bf16[1024,1536]{1,0:T(8,128)(2,1)S(1)}, bf16[1024,1536]{1,0:T(8,128)(2,1)}, u32[]{:S(2)}) copy-start(bf16[1024,1536]{1,0:T(8,128)(2,1)} %get-tuple-element.81) | copy-start | bytes 9437188
  727.0 8.6 copy-start.18
  727.0 8.6 copy-start.29
  1109.5 10.6 copy-start.5
  1117.5 3.9 copy-start.4
  1121.4 2.1 copy-start.13
  1121.4 2.9 copy-start.12
  1121.4 3.7 copy-start.11
  1121.4 4.5 copy-start.10
  1123.5 3.2 copy-start.8
  1123.5 4.3 copy-start.7

commit v3 on v2

v3 whole, which is shorter than its diff:
```python
import functools

import jax
import jax.numpy as jnp
import numpy as np
from jax import lax
from jax.experimental import pallas as pl
from jax.experimental.pallas import tpu as pltpu
from jax.sharding import PartitionSpec as P

F32, BF16 = jnp.float32, jnp.bfloat16
MESH = pl.DeviceIdType.MESH
HBM = pltpu.HBM
EPS = 1e-06
TAU = 8.0


CHUNK = 256
NT = (((1,), (1,)), ((), ()))
NN = (((1,), (0,)), ((), ()))
TN = (((0,), (0,)), ((), ()))


def decay_tables(count):
    at = np.arange(count)
    paths, masks = [], []
    half = count // 2
    while half >= 1:
        block, second = at // (2 * half), (at // half) % 2 == 1
        edge = block * 2 * half + half - 1
        r, t = at[None, :], at[:, None]
        fore = second[:, None] & (r > edge[:, None]) & (r <= t)
        back = ~second[:, None] & (r > t) & (r <= edge[:, None])
        paths.append(fore | back)
        masks.append((block[:, None] == block[None, :]) & second[:, None] & ~second[None, :])
        half //= 2
    paths.append(at[None, :] <= at[:, None])
    paths.append(at[None, :] > at[:, None])
    return np.concatenate(paths, 0), np.stack(masks)


def bf(x):
    return x.astype(BF16)


def halves(x):
    hi = bf(x)
    return hi, bf(x - hi.astype(F32))


def mm(a, b, dims):
    return lax.dot_general(a, b, dims, preferred_element_type=F32)


def dot3(a, b, dims):
    return mm(a[0], b[0], dims) + (mm(a[0], b[1], dims) + mm(a[1], b[0], dims))


def exact_sums(table, x):
    hi, mid = halves(x)
    low = bf(x - hi.astype(F32) - mid.astype(F32))
    n = x.shape[1]
    both = mm(table, jnp.concatenate([hi, mid, low, jnp.zeros_like(low)], axis=1), NN)
    return both[:, :n] + (both[:, n : 2 * n] + both[:, 2 * n : 3 * n])


def silu(v):
    return v / (1.0 + jnp.exp(-v))


def sigmoid(v):
    return 1.0 / (1.0 + jnp.exp(-v))


def silu_slope(v):
    s = sigmoid(v)
    return s + v * s * (1.0 - s)


def columns_total(x):
    ones = jnp.ones((x.shape[0], 128), BF16)
    hi, mid = halves(x)
    low = bf(x - hi.astype(F32) - mid.astype(F32))
    return mm(hi, ones, TN) + (mm(mid, ones, TN) + mm(low, ones, TN))


def spread(column, width):
    return jnp.concatenate([column] * (width // 128), axis=1)


def mix(pair, ratios, keep, masks_ref, own):
    out = own * keep
    for l, ratio in enumerate(ratios):
        left = pair * masks_ref[l].astype(F32)
        out += ratio * dot3(halves(left), halves(ratio * keep), NN)
    return out


def unmix(probs, ratios, keep, masks_ref, diag):
    out = diag * jnp.sum(probs * keep, axis=1, keepdims=True)
    for l, ratio in enumerate(ratios):
        part = dot3(halves(probs * ratio), halves(ratio * keep), NT)
        out += masks_ref[l].astype(F32) * part
    return out


def on_diagonal(count):
    return (
        lax.broadcasted_iota(jnp.int32, (count, count), 0) == lax.broadcasted_iota(jnp.int32, (count, count), 1)
    ).astype(F32)


class Slots:
    def __init__(self, seqs, rows, head, slots, chunk):
        self.seqs, self.rows, self.head, self.slots, self.chunk = seqs, rows, head, slots, chunk
        self.chunks = rows // chunk
        paths, masks = decay_tables(chunk)
        self.levels = masks.shape[0]
        self.paths = jnp.asarray(paths, BF16)
        self.masks = jnp.asarray(masks, BF16)

class Place:
    def __init__(self, size):
        self.size = size
        self.line = size // 4
        s = lax.axis_index("seq")
        self.c = lax.axis_index("head")
        self.s = s
        self.x = lax.rem(s, 2)
        self.b = lax.rem(s // 2, 2)
        self.a = s // 4

    def at(self, a, b, x):
        return (a * 2 + b) * 2 + x

    def partner(self):
        return (self.at(self.a, self.b, 1 - self.x), self.c)

    def across(self):
        return (self.at(self.a, 1 - self.b, self.x), self.c)

    def up(self):
        return (self.at(jnp.minimum(self.a + 1, self.line - 1), self.b, self.x), self.c)

    def down(self):
        return (self.at(jnp.maximum(self.a - 1, 0), self.b, self.x), self.c)

    def sibling(self):
        return (self.s, 1 - self.c)

    def has_up(self):
        return self.a < self.line - 1

    def has_down(self):
        return self.a > 0


def signal(sem, device):
    pl.semaphore_signal(sem, inc=1, device_id=device, device_id_type=MESH)


def greet(place, partner=True, across=True, line=True, sibling=False):
    barrier = pltpu.get_barrier_semaphore()
    count = jnp.int32(0)
    if partner:
        signal(barrier, place.partner())
        count = count + 1
    if sibling:
        signal(barrier, place.sibling())
        count = count + 1
    if across:
        signal(barrier, place.across())
        count = count + 1
    if line:
        pl.when(place.has_up())(lambda: signal(barrier, place.up()))
        pl.when(place.has_down())(lambda: signal(barrier, place.down()))
        count = count + place.has_up().astype(jnp.int32) + place.has_down().astype(jnp.int32)
    pl.semaphore_wait(barrier, count)


def remote(src, dst, send, recv, device):
    return pltpu.make_async_remote_copy(
        src_ref=src, dst_ref=dst, send_sem=send, recv_sem=recv, device_id=device, device_id_type=MESH
    )


class Gather:
    def __init__(self, place, shard, full, unit, offset, width, sems, late):
        self.pl, self.shard, self.full = place, shard, full
        self.unit, self.offset, self.width, self.late = unit, offset, width, late
        self.x_sem, self.b_sem, self.up_sem, self.down_sem = sems

    def part(self, start, count):
        rows = pl.ds(start * self.unit, count * self.unit)
        if self.width == self.full.shape[1]:
            return self.full.at[rows]
        return self.full.at[rows, pl.ds(self.offset, self.width)]

    def mine(self, x):
        if self.shard.shape[1] == self.width:
            return self.shard
        return self.shard.at[:, pl.ds(x * self.width, self.width)]

    def x_copy(self):
        p = self.pl
        return remote(self.mine(1 - p.x), self.part(p.s, 1), self.x_sem.at[0], self.x_sem.at[1], p.partner())

    def own_copy(self):
        return pltpu.make_async_copy(self.mine(self.pl.x), self.part(self.pl.s, 1), self.x_sem.at[2])

    def block(self, a):
        p = self.pl
        if self.late:
            return self.part(4 * a, 4)
        return self.part(4 * a + 2 * p.b, 2)

    def b_copy(self, i, a):
        p = self.pl
        return remote(
            self.part(4 * a + 2 * p.b, 2), self.part(4 * a + 2 * p.b, 2),
            self.b_sem.at[0, i], self.b_sem.at[1, i], p.across(),
        )

    def line_copy(self, way, h):
        p = self.pl
        if way == "up":
            blk = self.block(jnp.maximum(p.a - (h - 1), 0))
            return remote(blk, blk, self.up_sem.at[0, h - 1], self.up_sem.at[1, h - 1], p.up())
        blk = self.block(jnp.minimum(p.a + (h - 1), p.line - 1))
        return remote(blk, blk, self.down_sem.at[0, h - 1], self.down_sem.at[1, h - 1], p.down())

    def sends(self, way, h):
        p = self.pl
        if way == "up":
            return jnp.logical_and(p.has_up(), p.a - (h - 1) >= 0)
        return jnp.logical_and(p.has_down(), p.a + (h - 1) <= p.line - 1)

    def gets(self, way, h):
        p = self.pl
        if way == "up":
            return p.a - h >= 0
        return p.a + h <= p.line - 1

    def got(self, way, h):
        p = self.pl
        if way == "up":
            return jnp.maximum(p.a - h, 0)
        return jnp.minimum(p.a + h, p.line - 1)

    def slot(self, way, h):
        return h if way == "up" else self.pl.line - 1 + h

    def start_x(self):
        self.x_copy().start()
        self.own_copy().start()

    def stage(self, h):
        p = self.pl
        if h == 0:
            self.own_copy().wait()
            self.x_copy().wait_recv()
            if self.late:
                self.b_copy(0, p.a).start()
            else:
                for way in ("up", "down"):
                    pl.when(self.sends(way, 1))(lambda way=way: self.line_copy(way, 1).start())
                self.b_copy(0, p.a).start()
            return
        if self.late:
            if h == 1:
                self.b_copy(0, p.a).wait_recv()
                for way in ("up", "down"):
                    pl.when(self.sends(way, 1))(lambda way=way: self.line_copy(way, 1).start())
                return
            h = h - 1
        for way in ("up", "down"):

            def go(way=way):
                self.line_copy(way, h).wait_recv()
                if not self.late:
                    self.b_copy(self.slot(way, h), self.got(way, h)).start()

            def on(way=way):
                self.line_copy(way, h + 1).start()

            pl.when(self.gets(way, h))(go)
            if h + 1 <= p.line - 1:
                pl.when(self.sends(way, h + 1))(on)

    def stages(self):
        return self.pl.line + (1 if self.late else 0)

    def finish(self):
        p = self.pl
        self.x_copy().wait_send()
        self.b_copy(0, p.a).wait_send()
        if not self.late:
            self.b_copy(0, p.a).wait_recv()
        for way in ("up", "down"):
            for h in range(1, p.line):
                pl.when(self.sends(way, h))(lambda way=way, h=h: self.line_copy(way, h).wait_send())
                if not self.late:

                    def both(way=way, h=h):
                        cp = self.b_copy(self.slot(way, h), self.got(way, h))
                        cp.wait_send()
                        cp.wait_recv()

                    pl.when(self.gets(way, h))(both)


def gather_sems(line):
    return [
        pltpu.SemaphoreType.DMA((3,)),
        pltpu.SemaphoreType.DMA((2, 2 * line - 1)),
        pltpu.SemaphoreType.DMA((2, line - 1)),
        pltpu.SemaphoreType.DMA((2, line - 1)),
    ]


def gather_ops(gathers, ahead):
    steps = []
    n = len(gathers)
    for k in range(min(ahead, n)):
        steps.append(gathers[k].start_x)
    steps.append(functools.partial(gathers[0].stage, 0))
    for k in range(n):
        if k + ahead < n:
            steps.append(gathers[k + ahead].start_x)
        if k + 1 < n:
            steps.append(functools.partial(gathers[k + 1].stage, 0))
        for h in range(1, gathers[k].stages()):
            steps.append(functools.partial(gathers[k].stage, h))
    for g in gathers:
        steps.append(g.finish)
    return steps

VM = pl.BlockSpec(memory_space=pltpu.VMEM)
ANY = pl.BlockSpec(memory_space=HBM)


def remote_params(number, mib=56):
    return pltpu.CompilerParams(collective_id=number, has_side_effects=True, vmem_limit_bytes=mib * 2**20)


STRIPS = 4


class Fold:
    def __init__(self, place, part, sib, sent, came, sems, own=None):
        self.p, self.part, self.sib, self.sent, self.came = place, part, sib, sent, came
        self.own = part.at[place.c] if own is None else own
        self.s_sem, self.x_sem = sems
        self.rows = part.shape[2] // STRIPS

    def strip(self, r):
        return pl.ds(r * self.rows, self.rows)

    def sib_copy(self, far, r):
        p = self.p
        x = 1 - p.x if far else p.x
        i = (0 if far else STRIPS) + r
        return remote(
            self.part.at[1 - p.c, x, self.strip(r)], self.sib.at[1 if far else 0, self.strip(r)],
            self.s_sem.at[0, i], self.s_sem.at[1, i], p.sibling(),
        )

    def x_copy(self, r):
        return remote(
            self.sent.at[self.strip(r)], self.came.at[self.strip(r)], self.x_sem.at[0, r], self.x_sem.at[1, r], self.p.partner()
        )

    def start(self):
        for r in range(STRIPS):
            self.sib_copy(True, r).start()
        for r in range(STRIPS):
            self.sib_copy(False, r).start()

    def sib_all(self, far):
        for r in range(STRIPS):
            self.sib_copy(far, r).start()

    def cross(self, r):
        p = self.p
        self.sib_copy(True, r).wait_recv()
        own = self.own[1 - p.x, self.strip(r)].astype(F32)
        self.sent[self.strip(r)] = bf(own + self.sib[1, self.strip(r)].astype(F32))
        self.x_copy(r).start()

    def total(self, r):
        p = self.p
        self.sib_copy(False, r).wait_recv()
        self.x_copy(r).wait_recv()
        own = self.own[p.x, self.strip(r)].astype(F32) + self.sib[0, self.strip(r)].astype(F32)
        return own + self.came[self.strip(r)].astype(F32)

    def finish(self):
        for r in range(STRIPS):
            self.sib_copy(True, r).wait_send()
            self.sib_copy(False, r).wait_send()
            self.x_copy(r).wait_send()


def fold_scratch(rows, width):
    return [
        pltpu.VMEM((2, rows, width), BF16), pltpu.VMEM((rows, width), BF16), pltpu.VMEM((rows, width), BF16),
        pltpu.SemaphoreType.DMA((2, 2 * STRIPS)), pltpu.SemaphoreType.DMA((2, STRIPS)),
    ]


class Share:
    def __init__(self, place, out, sems):
        self.p, self.out = place, out
        self.x_sem, self.s_sem = sems
        self.rows = out.shape[2] // STRIPS

    def strip(self, r):
        return pl.ds(r * self.rows, self.rows)

    def x_copy(self, r):
        p = self.p
        block = self.out.at[p.c, p.x, self.strip(r)]
        return remote(block, block, self.x_sem.at[0, r], self.x_sem.at[1, r], p.partner())

    def s_copy(self, far, r):
        p = self.p
        block = self.out.at[p.c, 1 - p.x if far else p.x, self.strip(r)]
        i = (0 if far else STRIPS) + r
        return remote(block, block, self.s_sem.at[0, i], self.s_sem.at[1, i], p.sibling())

    def put(self, r, value):
        self.out[self.p.c, self.p.x, self.strip(r)] = value
        self.x_copy(r).start()
        self.s_copy(False, r).start()

    def forward(self, r):
        self.x_copy(r).wait_recv()
        self.s_copy(True, r).start()

    def wait_sibling(self, far):
        for r in range(STRIPS):
            self.s_copy(far, r).wait_recv()

    def finish(self, receive=True):
        for r in range(STRIPS):
            self.x_copy(r).wait_send()
            for far in (False, True):
                self.s_copy(far, r).wait_send()
                if receive:
                    self.s_copy(far, r).wait_recv()


SHARE_SEMS = [pltpu.SemaphoreType.DMA((2, STRIPS)), pltpu.SemaphoreType.DMA((2, 2 * STRIPS))]


def inverse_rms(values):
    return lax.rsqrt(jnp.mean(values * values, axis=-1, keepdims=True) + EPS)


def norm_back(grad, values, gain):
    scale = inverse_rms(values)
    u = grad * gain
    down = scale * u - values * (scale * scale * scale) * jnp.mean(u * values, axis=-1, keepdims=True)
    return down, jnp.sum(grad * values * scale, axis=0, keepdims=True)


def ends_chunk(k, v, decay, keep, tail):
    weight = halves(jnp.exp(exact_sums(tail, decay)) * keep)
    unit_k = dot3(weight, halves(silu(k.astype(F32))), TN)
    unit_v = mm(weight[0], v, TN) + mm(weight[1], v, TN)
    return jnp.concatenate([unit_k, unit_v], axis=1), jnp.exp(columns_total(decay))


def powers_of(table, count, levels, decay):
    powers = jnp.exp(exact_sums(table, decay))
    return [powers[l * count : (l + 1) * count] for l in range(levels)], [
        powers[l * count : (l + 1) * count] for l in range(levels, table.shape[0] // count)
    ]


class Prefix:
    def __init__(self, place, back, own, dec, start, peer, peer_dec, line, out, sems):
        p = self.p = place
        self.own, self.dec, self.start_ref, self.peer, self.peer_dec = own, dec, start, peer, peer_dec
        self.line, self.out = line, out
        self.p_sem, self.d_sem, self.l_sem = sems
        seqs, slots, width = own.shape
        self.half = width // 2
        self.pieces = [(b, h) for b in range(seqs) for h in range(2)]
        if back:
            self.has_prev, self.has_next, self.after = p.has_up(), p.has_down(), p.down()
        else:
            self.has_prev, self.has_next, self.after = p.has_down(), p.has_up(), p.up()
        self.first = ((p.b == 1) if back else (p.b == 0)).astype(F32)

    def cut(self, ref, i):
        b, h = self.pieces[i]
        return ref.at[b, :, pl.ds(h * self.half, self.half)]

    def peer_copy(self, i):
        return remote(self.cut(self.own, i), self.cut(self.peer, i), self.p_sem.at[0, i], self.p_sem.at[1, i], self.p.across())

    def line_copy(self, i):
        return remote(self.cut(self.out, i), self.cut(self.line, i), self.l_sem.at[0, i], self.l_sem.at[1, i], self.after)

    def dec_copy(self):
        return remote(self.dec, self.peer_dec, self.d_sem.at[0], self.d_sem.at[1], self.p.across())

    def start(self):
        self.dec_copy().start()
        for i in range(len(self.pieces)):
            self.peer_copy(i).start()

    def run(self):
        self.dec_copy().wait_recv()
        for i, (b, _) in enumerate(self.pieces):
            self.peer_copy(i).wait_recv()
            dec_own = spread(self.dec[b], self.half)
            dec_peer = spread(self.peer_dec[b], self.half)
            own, other = self.cut(self.own, i)[...], self.cut(self.peer, i)[...]
            first = self.first
            both = first * (dec_peer * own + other) + (1.0 - first) * (dec_own * other + own)
            here, result = self.cut(self.out, i), self.cut(self.start_ref, i)

            def go_on(i=i):
                self.line_copy(i).wait_recv()
                came = self.cut(self.line, i)[...]
                here[...] = dec_own * dec_peer * came + both
                result[...] = first * came + (1.0 - first) * (dec_peer * came + other)

            def begin():
                here[...] = both
                result[...] = (1.0 - first) * other

            pl.when(self.has_prev)(go_on)
            pl.when(jnp.logical_not(self.has_prev))(begin)
            pl.when(self.has_next)(lambda i=i: self.line_copy(i).start())

    def finish(self):
        self.dec_copy().wait_send()
        for i in range(len(self.pieces)):
            self.peer_copy(i).wait_send()
            pl.when(self.has_next)(lambda i=i: self.line_copy(i).wait_send())


def prefix_scratch(seqs, slots, width):
    count = 2 * seqs
    return [
        pltpu.VMEM((seqs, slots, width), F32), pltpu.VMEM((seqs, slots, width), F32), pltpu.VMEM((seqs, slots, 128), F32),
        pltpu.VMEM((seqs, slots, width), F32), pltpu.VMEM((seqs, slots, width), F32),
        pltpu.SemaphoreType.DMA((2, count)), pltpu.SemaphoreType.DMA((2,)), pltpu.SemaphoreType.DMA((2, count)),
    ]


def take(refs, count):
    return refs[:count], refs[count:]


class Weave:
    def __init__(self, steps):
        self.steps = list(steps)

    def run(self, count):
        for step in self.steps[:count]:
            step()
        self.steps = self.steps[count:]

    def rest(self):
        self.run(len(self.steps))


def blocks_in_order(p, seqs):
    def block(i):
        b = jnp.where(i < 2, 1 - p.c, p.c)
        x = jnp.where(lax.rem(i, 2) == 0, 1 - p.x, p.x)
        return b, x

    return block


def forward_kernel(size, plan, levels, *refs):
    p = Place(size)
    (qkv, gates, decay, keep, gain, out_w, tokens, gain2, paths, masks), refs = take(refs, 10)
    shard_refs, refs = take(refs, len(plan))
    (gated, attended, probs, scores, weights, states, decs, end_dec, residual, normed), refs = take(refs, 10)
    fulls, refs = take(refs, max(i for i, _, _, _, _ in plan) + 1)
    (units, part, total), refs = take(refs, 3)
    (start, *prefix_refs), refs = take(refs, 8)
    fold_refs, refs = take(refs, 5)
    share_sems, refs = take(refs, 2)
    count = paths.shape[1]
    head = gated.shape[1]
    seqs = tokens.shape[0]
    slots = keep.shape[1]
    greet(p, sibling=True)
    work = []
    for n, (i, unit, offset, width, late) in enumerate(plan):
        work.append(Gather(p, shard_refs[n], fulls[i], unit, offset, width, refs[4 * n : 4 * n + 4], late))
    weave = Weave(gather_ops(work, 3))
    weave.run(3)
    tail = paths[(levels + 1) * count :, :]

    def ends(b):
        for j in range(2):
            rows = pl.ds((b * 2 + j) * count, count)
            unit, dec = ends_chunk(
                qkv[rows, head : 2 * head], qkv[rows, 2 * head :], decay[rows, :], keep[rows, :], tail
            )
            units[b, j] = unit
            decs[b, j] = dec
        total[b] = spread(dec, 2 * head) * units[b, 0] + unit
        end_dec[b] = decs[b, 0] * dec

    for b in range(seqs):
        ends(b)
    carry = Prefix(p, False, total, end_dec, start, *prefix_refs[:4], prefix_refs[4:])
    carry.start()
    weave.run(1)
    carry.run()
    for b in range(seqs):
        states[3 * b] = start[b]
        for j in range(2):
            states[3 * b + j + 1] = spread(decs[b, j], 2 * head) * states[3 * b + j] + units[b, j]
    weave.run(1)
    diag = on_diagonal(count)
    order = blocks_in_order(p, seqs)
    fold = Fold(p, part, *fold_refs[:3], fold_refs[3:])
    share = Share(p, normed, share_sems)

    def attend(i, nothing):
        b, j = order(i)
        rows = pl.ds(pl.multiple_of((b * 2 + j) * count, count), count)
        here = keep[rows, :]
        ratios, (growth,) = powers_of(paths[: (levels + 1) * count, :], count, levels, decay[rows, :])
        query = halves(silu(qkv[rows, :head].astype(F32)) * head ** (-0.5))
        keys = halves(silu(qkv[rows, head : 2 * head].astype(F32)))
        state = states[3 * b + j]
        pair = dot3(query, keys, NT)
        score = mix(pair, ratios, here, masks, jnp.sum(pair * diag, axis=1, keepdims=True))
        score += growth * dot3(query, halves(state[:, :head]), NT)
        raised = jnp.exp(score - jnp.max(score, axis=1, keepdims=True))
        prob = raised / jnp.sum(raised, axis=1, keepdims=True)
        weight = unmix(prob, ratios, here, masks, diag)
        values = qkv[rows, 2 * head :]
        whi, wlo = halves(weight)
        result = mm(whi, values, NN) + mm(wlo, values, NN)
        result += dot3(halves(prob * growth), halves(state[:, head:]), NN)
        scale = lax.rsqrt(jnp.mean(result * result, axis=1, keepdims=True) + EPS)
        low = bf(result * scale * gain[...] * silu(gates[rows, :head]))
        gated[rows, :] = low
        attended[rows, :] = result
        probs[rows, :] = prob
        scores[rows, :] = score
        weights[rows, :] = weight
        part[b, j] = bf(mm(low, out_w[...], NT))
        pl.when(i == 0)(lambda: fold.sib_all(True))
        pl.when(i == 1)(lambda: fold.sib_all(False))
        return nothing

    lax.fori_loop(0, 2, attend, 0)
    weave.run(1)
    lax.fori_loop(2, 3, attend, 0)
    for r in range(STRIPS):
        fold.cross(r)
    lax.fori_loop(3, 4, attend, 0)
    weave.run(1)
    for r in range(STRIPS):
        value = tokens[p.c, fold.strip(r)].astype(F32) + fold.total(r)
        residual[fold.strip(r)] = value
        share.put(r, bf(value * inverse_rms(value) * gain2[...]))
    weave.run(2)
    for r in range(STRIPS):
        share.forward(r)
    weave.rest()
    share.finish()
    fold.finish()
    carry.finish()


def forward(size, number, slot, plan, fulls, qkv, gates, decay, keep, gain, out_w, tokens, gain2, shards):
    seqs, block, width = tokens.shape
    h, m, n, rows = slot.head, slot.slots, slot.chunks, slot.seqs * slot.rows
    shape = jax.ShapeDtypeStruct
    outs = [
        shape((rows, h), BF16), shape((rows, h), F32), shape((rows, m), F32), shape((rows, m), F32), shape((rows, slot.chunk), F32),
        shape((seqs * (n + 1), m, 2 * h), F32), shape((seqs, n, m, 128), F32), shape((seqs, m, 128), F32),
        shape((block, width), F32), shape((seqs, 2, block, width), BF16),
    ]
    scratch = [
        pltpu.VMEM((seqs, n, m, 2 * h), F32), pltpu.VMEM((seqs, 2, block, width), BF16), pltpu.VMEM((seqs, m, 2 * h), F32),
    ]
    scratch += prefix_scratch(seqs, m, 2 * h) + fold_scratch(block, width) + SHARE_SEMS
    for _ in plan:
        scratch += gather_sems(size // 4)
    return pl.pallas_call(
        functools.partial(forward_kernel, size, plan, slot.levels),
        out_shape=outs + [shape(full, BF16) for full in fulls],
        in_specs=[VM] * 10 + [ANY] * len(shards),
        out_specs=[VM] * 10 + [ANY] * len(fulls),
        scratch_shapes=scratch,
        compiler_params=remote_params(number, 60),
        name="attend_forward",
    )(qkv, gates, decay, keep, gain, out_w, tokens, gain2, slot.paths, slot.masks, *shards)

class Pool:
    def __init__(self, refs):
        self.loads, self.extra, self.sends, self.totals, self.sems = refs

    def slot(self, which, slot):
        return self.extra if slot == 3 else self.loads.at[which, slot]


POOL_SENDS = 2


def pool_scratch(rows, width):
    return [
        pltpu.VMEM((2, 3, rows, width), BF16), pltpu.VMEM((rows, width), BF16), pltpu.VMEM((POOL_SENDS, rows, width), BF16),
        pltpu.VMEM((rows, width), F32),
        pltpu.SemaphoreType.DMA((2, 4)),
    ]


class Scatter:
    def __init__(self, place, grad, out, peer, line, unit, offset, width, sems):
        self.p, self.grad, self.out, self.peer, self.line = place, grad, out, peer, line
        self.unit, self.offset, self.width = unit, offset, width
        self.whole = out.shape[-1] == width
        self.b_sem, self.l_sem, self.x_sem = sems

    def goal(self, n):
        p = self.p
        low, high = p.a, p.line - 1 - p.a
        more, less = jnp.maximum(low, high), jnp.minimum(low, high)
        alone = more - less
        up_more = jnp.where(high >= low, 1, -1)
        m = n - alone
        early = n < alone
        reach = jnp.where(early, more - n, less - m // 2)
        side = jnp.where(early, up_more, jnp.where(lax.rem(jnp.maximum(m, 0), 2) == 0, 1, -1))
        return p.a + side * reach

    def block(self, a, b):
        rows = pl.ds((4 * a + 2 * b) * self.unit, 2 * self.unit)
        if self.width == self.grad.shape[1]:
            return self.grad.at[rows]
        return self.grad.at[rows, pl.ds(self.offset, self.width)]

    def b_copy(self, a):
        return remote(self.block(a, 1 - self.p.b), self.peer.at[a], self.b_sem.at[0, a], self.b_sem.at[1, a], self.p.across())

    def start(self):
        for n in range(self.p.line):
            self.b_copy(self.goal(n)).start()

    def cut(self, ref):
        return ref if self.width == ref.shape[1] else ref.at[:, pl.ds(0, self.width)]

    def load(self, pool, which, slot, source):
        return pltpu.make_async_copy(source, self.cut(pool.slot(which, slot)), pool.sems.at[which, slot])

    def prepare(self, pool, which, n):
        d = self.goal(n)
        self.b_copy(d).wait_recv()
        self.load(pool, which, 0, self.block(d, self.p.b)).start()
        self.load(pool, which, 1, self.peer.at[d]).start()

    def loaded(self, pool, which, n):
        d = self.goal(n)
        self.load(pool, which, 0, self.block(d, self.p.b)).wait()
        self.load(pool, which, 1, self.peer.at[d]).wait()

    def strips(self, do):
        rows = 2 * self.unit
        step = max(r for r in (16, 32, 64, 128) if rows % r == 0 and (r == 16 or r * self.width <= 64 * 1024))

        def one(i, carry):
            do(pl.ds(pl.multiple_of(i * step, step), step))
            return carry

        lax.fori_loop(0, rows // step, one, 0)

    def bring(self, pool, which, slot, place):
        remote(self.line.at[place], self.line.at[place], self.l_sem.at[0, 0], self.l_sem.at[1, place], self.p.across()).wait_recv()
        self.load(pool, which, slot, self.line.at[place]).start()

    def send(self, pool, out, n):
        p = self.p
        d = self.goal(n)
        up = d > p.a
        to = jnp.clip(p.a + jnp.where(up, 1, -1), 0, p.line - 1)
        slot = jnp.where(jnp.logical_and(jnp.logical_not(up), d == p.a - 1), p.line, d)
        return remote(
            self.cut(pool.sends.at[out]), self.line.at[slot], self.l_sem.at[0, n], self.l_sem.at[1, slot], (p.at(to, p.b, p.x), p.c)
        )

    def hop(self, pool, which, n, out):
        p = self.p
        d = self.goal(n)
        behind = jnp.logical_or(jnp.logical_and(d > p.a, p.has_down()), jnp.logical_and(d < p.a, p.has_up()))
        pl.when(behind)(lambda: self.bring(pool, which, 2, d))
        self.loaded(pool, which, n)
        a, b, c = (self.cut(pool.slot(which, i)) for i in range(3))
        to = self.cut(pool.sends.at[out])

        def with_line():
            self.load(pool, which, 2, self.line.at[d]).wait()

            def do(rows):
                to[rows] = bf(a[rows].astype(F32) + b[rows].astype(F32) + c[rows].astype(F32))

            self.strips(do)

        def without():
            def do(rows):
                to[rows] = bf(a[rows].astype(F32) + b[rows].astype(F32))

            self.strips(do)

        pl.when(behind)(with_line)
        pl.when(jnp.logical_not(behind))(without)
        self.send(pool, out, n).start()

    def last(self, pool, which):
        p = self.p
        n = p.line - 1
        pl.when(p.has_down())(lambda: self.bring(pool, which, 2, p.a))
        pl.when(p.has_up())(lambda: self.bring(pool, which, 3, p.line))
        self.loaded(pool, which, n)
        a, b, c, d = (self.cut(pool.slot(which, i)) for i in range(4))
        to = self.total = self.cut(pool.totals)

        def first(rows):
            to[rows] = a[rows].astype(F32) + b[rows].astype(F32)

        self.strips(first)

        def more(slot, place, ref):
            def go():
                self.load(pool, which, slot, self.line.at[place]).wait()

                def do(rows):
                    to[rows] = to[rows] + ref[rows].astype(F32)

                self.strips(do)

            return go

        pl.when(p.has_down())(more(2, p.a, c))
        pl.when(p.has_up())(more(3, p.line, d))
        self.x_copy().start()
        if not self.whole:
            self.out_copy().start()

    def half(self, x):
        return self.total.at[pl.ds(x * self.unit, self.unit)]

    def place(self):
        return self.out.at[:, pl.ds(self.p.x * self.width, self.width)]

    def x_copy(self):
        p = self.p
        where = self.out.at[1] if self.whole else self.place()
        return remote(self.half(1 - p.x), where, self.x_sem.at[0], self.x_sem.at[1], p.partner())

    def out_copy(self):
        return pltpu.make_async_copy(self.half(self.p.x), self.place(), self.x_sem.at[2])

    def sent(self):
        self.x_copy().wait_send()
        if not self.whole:
            self.out_copy().wait()

    def finish(self):
        p = self.p
        self.x_copy().wait_recv()
        if self.whole:
            self.out[0] = self.out[1] + self.half(p.x)[...]
        for n in range(p.line):
            self.b_copy(self.goal(n)).wait_send()


def scatter_sems(line):
    return [pltpu.SemaphoreType.DMA((2, line)), pltpu.SemaphoreType.DMA((2, line + 1)), pltpu.SemaphoreType.DMA((3,))]


def scatter_ops(work, pool):
    lines = work[0].p.line
    jobs = [(k, n) for k in range(len(work)) for n in range(lines)]
    steps = [work[0].start]
    if len(work) > 1:
        steps.append(work[1].start)
    sends, totals = [], []

    def job(i):
        k, n = jobs[i]

        def step():
            work[k].prepare(pool, i % 2, n)
            if n == 0 and 0 < k < len(work) - 1:
                work[k + 1].start()
            if n < lines - 1:
                out = len(sends) % POOL_SENDS
                if len(sends) >= POOL_SENDS:
                    ok, on, oo = sends[-POOL_SENDS]
                    work[ok].send(pool, oo, on).wait_send()
                work[k].hop(pool, i % 2, n, out)
                sends.append((k, n, out))
            else:
                if totals:
                    work[totals[-1]].sent()
                work[k].last(pool, i % 2)
                totals.append(k)

        return step

    steps += [job(i) for i in range(len(jobs))]

    def finish():
        for ok, on, oo in sends[-POOL_SENDS:]:
            work[ok].send(pool, oo, on).wait_send()
        work[totals[-1]].sent()
        for chunk in work:
            chunk.finish()

    steps.append(finish)
    return steps

SECOND_JOBS = ((0, 1), (1, 1), (2, 1), (3, 1))


def backward_kernel(size, plan, levels, *refs):
    p = Place(size)
    (grad_out_all, gates_all, attended, grad_part), refs = take(refs, 4)
    (residual, gain2, out_w, qkv, decay, keep, gain, probs, scores, weights, states, decs,
     end_dec, paths, later, masks), refs = take(refs, 16)
    grads = max(i for i, _, _, _, _ in plan) + 1
    grad_refs, refs = take(refs, grads)
    (residual_grad, low, second_part, gate_term, gain_part, term, decay_term), refs = take(refs, 7)
    outs, refs = take(refs, len(plan))
    spaces, refs = take(refs, 2 * len(plan))
    (grad_out, gates, own_part, own_sem, att_grad, dprobs, dscores, units, adjoints, total), refs = take(refs, 10)
    (ending, *prefix_refs), refs = take(refs, 8)
    fold_refs, refs = take(refs, 5)
    share_sems, refs = take(refs, 2)
    pool_refs, refs = take(refs, 5)
    count = paths.shape[1]
    head = gate_term.shape[1]
    seqs = grad_out_all.shape[0]
    own = [
        pltpu.make_async_copy(grad_out_all.at[p.c], grad_out, own_sem.at[0]),
        pltpu.make_async_copy(gates_all.at[:, pl.ds(0, head)], gates, own_sem.at[1]),
        pltpu.make_async_copy(attended, att_grad, own_sem.at[2]),
        pltpu.make_async_copy(grad_part.at[p.c], own_part, own_sem.at[3]),
    ]
    for copy in own:
        copy.start()
    greet(p, sibling=True)
    pool = Pool(pool_refs)
    work = []
    for n, (i, unit, offset, width, _) in enumerate(plan):
        work.append(
            Scatter(p, grad_refs[i], outs[n], spaces[2 * n], spaces[2 * n + 1], unit, offset, width, refs[3 * n : 3 * n + 3])
        )
    weave = Weave(scatter_ops(work, pool))
    fold = Fold(p, grad_part, *fold_refs[:3], fold_refs[3:], own_part)
    share = Share(p, low, share_sems)
    fold.start()
    weave.run(2)
    own[3].wait()
    for r in range(STRIPS):
        fold.cross(r)
    own[0].wait()
    gains = jnp.zeros((1, grad_part.shape[3]), F32)
    for r in range(STRIPS):
        down, more = norm_back(fold.total(r), residual[fold.strip(r)], gain2[...])
        value = grad_out[fold.strip(r)].astype(F32) + down
        gains += more
        residual_grad[fold.strip(r)] = value
        share.put(r, bf(value))
        if r == 1:
            weave.run(1)
    second_part[...] = gains
    weave.run(1)
    diag = on_diagonal(count)
    gain_part[...] = jnp.zeros_like(gain_part)

    def place(i):
        b = jnp.where(lax.rem(i, 2) == 0, p.c, 1 - p.c)
        x = jnp.where(i < 2, p.x, 1 - p.x)
        return b, x

    def first(i, nothing):
        b, j = place(i)
        rows = pl.ds(pl.multiple_of((b * 2 + j) * count, count), count)
        grad = mm(low[b, j], out_w[...], NN)
        gate = gates[rows, :]
        value = att_grad[rows, :]
        scale = lax.rsqrt(jnp.mean(value * value, axis=1, keepdims=True) + EPS)
        normed = value * scale
        weighted = grad * silu(gate)
        gate_term[rows, :] = bf(grad * normed * gain[...] * silu_slope(gate))
        gain_part[...] += jnp.sum(weighted * normed, axis=0, keepdims=True)
        c = weighted * gain[...]
        agrad = scale * c - value * (scale * scale * scale) * jnp.mean(c * value, axis=1, keepdims=True)
        att_grad[rows, :] = agrad
        here = keep[rows, :]
        ratios, (growth,) = powers_of(paths[: (levels + 1) * count, :], count, levels, decay[rows, :])
        ahalf = halves(agrad)
        values = qkv[rows, 2 * head :]
        pair = mm(ahalf[0], values, NT) + mm(ahalf[1], values, NT)
        state = states[3 * b + j]
        dprob = mix(pair, ratios, here, masks, jnp.sum(pair * diag, axis=1, keepdims=True))
        dprob += growth * dot3(ahalf, halves(state[:, head:]), NT)
        prob = probs[rows, :]
        dscore = prob * (dprob - jnp.sum(prob * dprob, axis=1, keepdims=True))
        query = halves(silu(qkv[rows, :head].astype(F32)) * head ** (-0.5))
        dprobs[rows, :] = dprob
        dscores[rows, :] = dscore
        unit_k = dot3(halves(growth * dscore), query, TN)
        unit_v = dot3(halves(growth * prob), ahalf, TN)
        units[b, j] = jnp.concatenate([unit_k, unit_v], axis=1)
        return nothing

    own[1].wait()
    own[2].wait()
    lax.fori_loop(0, 1, first, 0)
    for r in range(STRIPS):
        share.forward(r)
    share.wait_sibling(False)
    lax.fori_loop(1, 3, first, 0)
    weave.run(1)
    share.wait_sibling(True)
    lax.fori_loop(3, 4, first, 0)
    weave.run(1)
    for b in range(seqs):
        total[b] = spread(decs[b, 0], 2 * head) * units[b, 1] + units[b, 0]
    carry = Prefix(p, True, total, end_dec, ending, *prefix_refs[:4], prefix_refs[4:])
    carry.start()
    weave.run(1)
    carry.run()
    weave.run(1)
    for b in range(seqs):
        adjoints[b, 1] = ending[b]
        adjoints[b, 0] = spread(decs[b, 1], 2 * head) * ending[b] + units[b, 1]
    is_last = (lax.broadcasted_iota(jnp.int32, (count, 1), 0) == count - 1).astype(F32)

    def second(i, nothing):
        b, j = place(i)
        rows = pl.ds(pl.multiple_of((b * 2 + j) * count, count), count)
        here = keep[rows, :]
        ratios, (growth, rest) = powers_of(paths[...], count, levels, decay[rows, :])
        qraw = qkv[rows, :head].astype(F32)
        kraw = qkv[rows, head : 2 * head].astype(F32)
        query = halves(silu(qraw) * head ** (-0.5))
        keys = halves(silu(kraw))
        values = qkv[rows, 2 * head :]
        agrad = halves(att_grad[rows, :])
        prob, dscore = probs[rows, :], dscores[rows, :]
        state = halves(states[3 * b + j][:, :head])
        adj = adjoints[b, j]
        ahalf = halves(adj)
        adj_k, adj_v = (ahalf[0][:, :head], ahalf[1][:, :head]), (ahalf[0][:, head:], ahalf[1][:, head:])
        dweights = halves(unmix(dscore, ratios, here, masks, diag))
        dquery = dot3(dweights, keys, NN) + dot3(halves(dscore * growth), state, NN)
        term[rows, :head] = bf(silu_slope(qraw) * dquery * head ** (-0.5))
        left = halves(rest * here)
        dkey = dot3(dweights, query, TN) + dot3(left, adj_k, NN)
        term[rows, head : 2 * head] = bf(silu_slope(kraw) * dkey)
        dvalue = dot3(halves(weights[rows, :]), agrad, TN) + dot3(left, adj_v, NN)
        term[rows, 2 * head :] = bf(dvalue)
        pair_k = dot3(query, keys, NT)
        pair_v = mm(agrad[0], values, NT) + mm(agrad[1], values, NT)
        dkeep = jnp.sum(pair_k * diag, axis=1, keepdims=True) * dscore
        dkeep += jnp.sum(pair_v * diag, axis=1, keepdims=True) * prob
        dkeep += rest * (dot3(keys, adj_k, NT) + mm(values, adj_v[0], NT) + mm(values, adj_v[1], NT))
        for l, ratio in enumerate(ratios):
            mask = masks[l].astype(F32)
            more = dot3(halves(pair_k * mask), halves(dscore * ratio), TN)
            more += dot3(halves(pair_v * mask), halves(prob * ratio), TN)
            dkeep += ratio * more
        dsum = dscore * scores[rows, :] + prob * dprobs[rows, :] - here * dkeep
        at_end = jnp.sum(adj * states[3 * b + j + 1], axis=1, keepdims=True)
        at_end = jnp.sum(at_end * on_diagonal(adj.shape[0]), axis=0, keepdims=True)
        dsum += is_last * at_end
        decay_term[rows, :] = exact_sums(later[...], dsum) - (1.0 - here) * dkeep
        for k, jobs in SECOND_JOBS:
            pl.when(i == k)(functools.partial(weave.run, jobs))
        return nothing

    lax.fori_loop(0, 4, second, 0)
    weave.rest()
    share.finish(False)
    fold.finish()
    carry.finish()


def backward(size, number, slot, plan, hbm_ins, vmem_ins, grads):
    seqs, block, width = hbm_ins[0].shape
    h, m, n, rows = slot.head, slot.slots, slot.chunks, slot.seqs * slot.rows
    line = size // 4
    shape = jax.ShapeDtypeStruct
    outs = [
        shape((block, width), F32), shape((seqs, 2, block, width), BF16), shape((1, width), F32), shape((rows, h), BF16),
        shape((1, h), F32), shape((rows, 3 * h), BF16), shape((rows, m), F32),
    ]
    results, spaces, sems = [], [], []
    for i, unit, offset, columns, whole in plan:
        results.append(shape((2, unit, columns) if whole else (unit, 2 * columns), F32))
        spaces += [shape((line, 2 * unit, columns), BF16), shape((line + 1, 2 * unit, columns), BF16)]
        sems += scatter_sems(line)
    widest = max(entry[3] for entry in plan)
    scratch = [
        pltpu.VMEM((block, width), BF16), pltpu.VMEM((rows, h), F32),
        pltpu.VMEM((2, block, width), BF16), pltpu.SemaphoreType.DMA((4,)),
        pltpu.VMEM((rows, h), F32), pltpu.VMEM((rows, m), F32), pltpu.VMEM((rows, m), F32), pltpu.VMEM((seqs, n, m, 2 * h), F32),
        pltpu.VMEM((seqs, n, m, 2 * h), F32), pltpu.VMEM((seqs, m, 2 * h), F32),
    ]
    scratch += prefix_scratch(seqs, m, 2 * h) + fold_scratch(block, width) + SHARE_SEMS
    scratch += pool_scratch(2 * plan[0][1], widest) + sems
    later = slot.paths[-2 * slot.chunk : -slot.chunk].T
    result = pl.pallas_call(
        functools.partial(backward_kernel, size, plan, slot.levels),
        out_shape=outs + results + spaces,
        in_specs=[ANY] * 4 + [VM] * 16 + [ANY] * len(grads),
        out_specs=[VM] * 7 + [ANY] * (len(results) + len(spaces)),
        scratch_shapes=scratch,
        compiler_params=remote_params(number, 62),
        name="attend_backward",
    )(*hbm_ins, *vmem_ins, slot.paths, later, slot.masks, *grads)
    return result[: 7 + len(results)]


def last_kernel(size, plan, *refs):
    p = Place(size)
    (part, ff_part, tokens, residual, residual_grad, gain, pack), refs = take(refs, 7)
    grads = max(i for i, _, _, _, _ in plan) + 1
    grad_refs, refs = take(refs, grads)
    (input_grad, output, sums), refs = take(refs, 3)
    outs, refs = take(refs, len(plan))
    spaces, refs = take(refs, 2 * len(plan))
    fold_refs, refs = take(refs, 5)
    ff_refs, refs = take(refs, 5)
    (out_sem, mine, came, s_sem), refs = take(refs, 4)
    pool_refs, refs = take(refs, 5)
    greet_all(p)
    pool = Pool(pool_refs)
    work = []
    for n, (i, unit, offset, width, _) in enumerate(plan):
        work.append(
            Scatter(p, grad_refs[i], outs[n], spaces[2 * n], spaces[2 * n + 1], unit, offset, width, refs[3 * n : 3 * n + 3])
        )
    weave = Weave(scatter_ops(work, pool))
    fold = Fold(p, part, *fold_refs[:3], fold_refs[3:])
    ff = Fold(p, ff_part, *ff_refs[:3], ff_refs[3:])
    weave.run(2)
    fold.start()
    ff.start()
    for r in range(STRIPS):
        fold.cross(r)
    weave.run(1)
    gains = jnp.zeros((1, part.shape[3]), F32)

    def out_copy(ref, k, r):
        block = ref.at[p.c, fold.strip(r)]
        return remote(block, block, out_sem.at[0, k * STRIPS + r], out_sem.at[1, k * STRIPS + r], p.sibling())

    for r in range(STRIPS):
        ff.cross(r)
    weave.run(2)
    for r in range(STRIPS):
        down, more = norm_back(fold.total(r), tokens[p.c, fold.strip(r)].astype(F32), gain[...])
        gains += more
        input_grad[p.c, fold.strip(r)] = residual_grad[fold.strip(r)] + down
        out_copy(input_grad, 1, r).start()
        if r % 2 == 1:
            weave.run(1)
    unit = plan[0][1]
    mine[...] = pack[...]
    for s in range(size):
        mine[s, 0:1, pl.ds(0, unit)] = gains[:, s * unit : (s + 1) * unit]
    smalls = Smalls(p, mine, sums, came, s_sem)
    smalls.start()
    weave.run(2)
    for r in range(STRIPS):
        output[p.c, fold.strip(r)] = bf(residual[fold.strip(r)] + ff.total(r))
        out_copy(output, 0, r).start()
        if r % 2 == 1:
            weave.run(1)
    weave.rest()
    smalls.finish()
    for r in range(STRIPS):
        out_copy(output, 0, r).wait()
        out_copy(input_grad, 1, r).wait()
    ff.finish()
    fold.finish()


def last(size, number, plan, vmem_ins, grads):
    seqs, _, block, width = vmem_ins[0].shape
    pack = vmem_ins[-1]
    line = size // 4
    shape = jax.ShapeDtypeStruct
    outs = [shape((seqs, block, width), F32), shape((seqs, block, width), BF16), shape(pack.shape[1:], F32)]
    results, specs, spaces, sems = [], [], [], []
    for i, unit, offset, columns, whole in plan:
        results.append(shape((2, unit, columns) if whole else (unit, 2 * columns), F32))
        specs.append(VM if whole else ANY)
        spaces += [shape((line, 2 * unit, columns), BF16), shape((line + 1, 2 * unit, columns), BF16)]
        sems += scatter_sems(line)
    widest = max(entry[3] for entry in plan)
    scratch = fold_scratch(block, width) * 2 + [
        pltpu.SemaphoreType.DMA((2, 2 * STRIPS)), pltpu.VMEM(pack.shape, F32), pltpu.VMEM((2 * size,) + pack.shape[1:], F32),
        pltpu.SemaphoreType.DMA((2, 2 * size)),
    ]
    scratch += pool_scratch(2 * plan[0][1], widest) + sems
    result = pl.pallas_call(
        functools.partial(last_kernel, size, plan),
        out_shape=outs + results + spaces,
        in_specs=[VM] * 7 + [ANY] * len(grads),
        out_specs=[VM] * 3 + specs + [ANY] * len(spaces),
        scratch_shapes=scratch,
        compiler_params=remote_params(number, 60),
        name="last",
    )(*vmem_ins, *grads)
    return result[: 3 + len(results)]

def greet_all(place):
    barrier = pltpu.get_barrier_semaphore()

    def one(i, carry):
        signal(barrier, (lax.rem(place.s + i // 2, place.size), lax.rem(place.c + lax.rem(i, 2), 2)))
        return carry

    lax.fori_loop(1, 2 * place.size, one, 0)
    pl.semaphore_wait(barrier, 2 * place.size - 1)


class Smalls:
    def __init__(self, place, pack, out, came, sems):
        self.p, self.pack, self.out, self.came, self.sems = place, pack, out, came, sems

    def copy(self, i):
        p = self.p
        s = lax.rem(p.s + i // 2, p.size)
        return remote(
            self.pack.at[s], self.came.at[i], self.sems.at[0, i], self.sems.at[1, i], (s, lax.rem(p.c + lax.rem(i, 2), 2))
        )

    def start(self):
        lax.fori_loop(1, 2 * self.p.size, lambda i, c: (self.copy(i).start(), c)[1], 0)

    def finish(self):
        def one(i, total):
            self.copy(i).wait()
            return total + self.came[i]

        self.out[...] = lax.fori_loop(1, 2 * self.p.size, one, self.pack[self.p.s])


class Swap:
    def __init__(self, place, own, both, sems):
        p = self.p = place
        self.keep = pltpu.make_async_copy(own, both.at[:, p.x], sems.at[0])
        self.cross = remote(own.at[p.c], both.at[p.c, p.x], sems.at[1], sems.at[2], p.partner())
        came = both.at[p.c, 1 - p.x]
        self.hand = remote(came, came, sems.at[3], sems.at[4], p.sibling())

    def start(self):
        self.cross.start()
        self.keep.start()

    def forward(self):
        self.cross.wait_recv()
        self.hand.start()

    def finish(self):
        self.keep.wait()
        self.cross.wait_send()
        self.hand.wait()


def gather_kernel(size, plan, swaps, *refs):
    p = Place(size)
    shards = len(plan)
    fulls = max(i for i, _, _, _, _ in plan) + 1
    ins, refs = refs[: shards + swaps], refs[shards + swaps :]
    outs, refs = refs[: fulls + swaps], refs[fulls + swaps :]
    greet(p, sibling=True)
    work = []
    for n, (i, unit, offset, width, late) in enumerate(plan):
        work.append(Gather(p, ins[n], outs[i], unit, offset, width, refs[4 * n : 4 * n + 4], late))
    moves = [Swap(p, ins[shards + n], outs[fulls + n], refs[4 * shards + n]) for n in range(swaps)]
    weave = Weave(gather_ops(work, len(work)))
    weave.run(len(work))
    for move in moves:
        move.start()
    weave.run(len(weave.steps) - len(work))
    for move in moves:
        move.forward()
    weave.rest()
    for move in moves:
        move.finish()


def gather(size, number, plan, shards, fulls, tokens):
    line = size // 4
    scratch = []
    for _ in plan:
        scratch += gather_sems(line)
    shapes = [jax.ShapeDtypeStruct(shape, BF16) for shape in fulls]
    for array in tokens:
        shapes.append(jax.ShapeDtypeStruct((array.shape[0], 2) + array.shape[1:], BF16))
        scratch.append(pltpu.SemaphoreType.DMA((5,)))
    return pl.pallas_call(
        functools.partial(gather_kernel, size, plan, len(tokens)),
        out_shape=shapes,
        in_specs=[ANY] * (len(shards) + len(tokens)),
        out_specs=[ANY] * len(shapes),
        scratch_shapes=scratch,
        compiler_params=remote_params(number, 60),
        name="gather",
    )(*shards, *tokens)


def dot(left, right, dims, dtype=F32):
    return lax.dot_general(left, right, dims, preferred_element_type=F32).astype(dtype)


def lanes(row):
    return jnp.pad(row.reshape(-1), (0, 128 - row.size))


def shards(
    tokens, grad_out, query_weight, key_weight, value_weight, forget_weight, forget_bias, outgate_weight, output_weight,
    slot_gain, first_gain, second_gain, gate_weight, up_weight, down_weight,
):
    size = lax.axis_size("seq")
    x = lax.rem(lax.axis_index("seq"), 2)
    c = lax.axis_index("head")
    seqs, block, width = tokens.shape
    heads_here, slot_part = forget_bias.shape
    slots = slot_part * size
    head = slot_gain.shape[0] * size
    unit = first_gain.shape[0]
    hidden = gate_weight.shape[1] // 2
    rows = seqs * 2 * block
    pack = jnp.stack([lanes(first_gain), lanes(second_gain), lanes(slot_gain), lanes(forget_bias)] + [jnp.zeros(128, BF16)] * 12)
    plan = [
        (0, unit, 0, head, False), (0, unit, head, head, False), (0, unit, 2 * head, head, False),
        (1, unit, 0, head, False), (1, unit, head, 2 * slots, False), (2, unit, 0, head, False),
        (3, 16, 0, 128, False),
    ]
    fulls = [(width, 3 * head), (width, head + 2 * slots), (width, head), (16 * size, 128)]
    qkv_full, gate_full, out_full, small_full, tok, gout = gather(
        size, 0, plan,
        (query_weight, key_weight, value_weight, outgate_weight, forget_weight, output_weight.T, pack),
        fulls, (tokens, grad_out),
    )
    small = small_full.reshape(size, 16, 128).astype(F32)
    first_full = small[:, 0, :unit].reshape(1, width)
    second_full = small[:, 1, :unit].reshape(1, width)
    slot_full = small[:, 2, : head // size].reshape(1, head)
    bias_full = small[:, 3, : heads_here * slot_part].reshape(size, heads_here, slot_part)
    bias_full = jnp.moveaxis(bias_full, 1, 0).reshape(heads_here, slots)

    def own_head(array, axis):
        return jnp.where(x == 0, *jnp.split(array, 2, axis=axis))

    inputs = tok.reshape(rows, width).astype(F32)
    normed_one = (inputs * inverse_rms(inputs) * first_full).astype(BF16)
    qkv = dot(normed_one, qkv_full, NN, BF16)
    gates = dot(normed_one, gate_full, NN)
    logit = own_head(gates[:, head:], 1) + own_head(bias_full, 0)
    decay = -jax.nn.softplus(-logit) / TAU
    keep = -jnp.expm1(decay)
    slot = Slots(seqs, 2 * block, head, slots, block)
    ff_plan = [(0, unit, 0, hidden, False), (0, unit, hidden, hidden, False), (1, unit, 0, hidden, False)]
    (gated, attended, probs, scores, weights, states, decs, end_decs, residual, normed_two, ff_full, down_full) = forward(
        size, 1, slot, ff_plan, [(width, 2 * hidden), (width, hidden)], qkv, gates, decay, keep, slot_full, out_full, tokens,
        second_full, (gate_weight, up_weight, down_weight.T),
    )
    shape = (seqs, 2, block, width)
    normed_two = normed_two.reshape(rows, width)
    ff = dot(normed_two, ff_full, NN)
    ff_gate, ff_up = ff[:, :hidden], ff[:, hidden:]
    sig = jax.nn.sigmoid(ff_gate)
    activated = (ff_gate * sig * ff_up).astype(BF16)
    ff_part = dot(activated, down_full, NT, BF16).reshape(shape)
    gout = gout.reshape(rows, width)
    act_grad = dot(gout, down_full, NN)
    ff_term = jnp.concatenate(
        [act_grad * ff_up * (sig + ff_gate * sig * (1.0 - sig)), act_grad * ff_gate * sig], axis=1
    ).astype(BF16)
    down_grad = dot(gout, activated, TN, BF16)
    ff_grad = dot(normed_two, ff_term, TN, BF16)
    normed_two_grad = dot(ff_term, ff_full, NT, BF16).reshape(shape)
    ff_plan = [(0, unit, 0, hidden, False), (0, unit, hidden, hidden, False), (1, unit, 0, hidden, False)]
    residual_grad, low, second_part, gate_term, slot_part_grad, qkv_term, decay_term, gate_grad, up_grad, down_grad = backward(
        size, 2, slot, ff_plan,
        (grad_out, gates, attended, normed_two_grad),
        (residual, second_full, out_full, qkv, decay, keep, slot_full, probs, scores, weights, states, decs,
         end_decs),
        (ff_grad, down_grad),
    )
    low = low.reshape(rows, width)
    out_grad = dot(low, gated, TN, BF16)
    forget_term = (decay_term * jax.nn.sigmoid(-logit) / TAU).astype(BF16)
    none = jnp.zeros_like(forget_term)
    gates_term = jnp.concatenate(
        [gate_term, jnp.where(x == 0, forget_term, none), jnp.where(x == 0, none, forget_term)], axis=1
    )
    qkv_grad = dot(normed_one, qkv_term, TN, BF16)
    gates_grad = dot(normed_one, gates_term, TN, BF16)
    normed_one_grad = (dot(qkv_term, qkv_full, NT) + dot(gates_term, gate_full, NT)).astype(BF16).reshape(shape)
    bias_part = jnp.sum(forget_term.astype(F32), axis=0)
    which = jnp.arange(2 * heads_here) == heads_here * c + x
    bias_part = jnp.where(which[:, None], bias_part[None, :], 0.0).reshape(2 * heads_here, size, slot_part)

    def rows_of(array):
        array = array.reshape(size, -1)
        return jnp.pad(array, ((0, 0), (0, 128 - array.shape[1])))

    zero = jnp.zeros((size, 128), F32)
    packed = jnp.stack(
        [zero, rows_of(second_part), rows_of(slot_part_grad), rows_of(jnp.moveaxis(bias_part, 1, 0))] + [zero] * 4, axis=1
    )
    plan = [
        (0, unit, 0, head, False), (1, unit, 0, head, False), (1, unit, head, head, False), (1, unit, 2 * head, head, False),
        (2, unit, 0, head, False), (2, unit, head, 2 * slots, True),
    ]
    input_grad, output, sums, output_grad, query_grad, key_grad, value_grad, outgate_grad, forget_grad = last(
        size, 3, plan, (normed_one_grad, ff_part, tokens, residual, residual_grad, first_full, packed),
        (out_grad, qkv_grad, gates_grad),
    )
    bias_grad = sums[3, : 2 * heads_here * slot_part].reshape(2, heads_here, slot_part)
    bias_grad = jnp.where(c == 0, bias_grad[0], bias_grad[1])
    return (
        output, input_grad, query_grad, key_grad, value_grad, forget_grad[0], bias_grad, outgate_grad, output_grad.T,
        sums[2, : head // size], sums[0, :unit], sums[1, :unit], gate_grad, up_grad, down_grad.T,
    )


def solution(mesh):
    row, column, vector, token = P("seq", "head"), P("head", "seq"), P("seq"), P(None, "seq", None)
    return jax.shard_map(
        shards,
        mesh=mesh,
        in_specs=(token, token, row, row, row, row, column, row, column, vector, vector, vector, row, row, column),
        out_specs=(token, token, row, row, row, row, column, row, column, vector, vector, vector, row, row, column),
        check_vma=False,
    )
```

time: 1140 us -> 1000 us (0.88)
  Pallas kernels: 950 us -> 815 us
    pallas_call x6 -> x2, Pallas kernels: 571 us -> 438 us  [the longest x1 277 us: backward(): pl.pallas_call(functools.partial(backward_kernel, size, plan, slot.levels...]
    dot_general x14 -> x13, matrix products: 138 us -> 131 us  [dot(): lax.dot_general(left, right, dims, preferred_element_type=F32).astype(dtype)]
where the time goes in v3:
time: 1000 us; the launch traced here: 990 us
  Pallas kernels  815 us (82%)
  matrix products  131 us (13%)
  local copies, waits for them, and re-layouts  30.4 us (3%)
  other arithmetic  12.2 us (1%)
    pallas_call x1, Pallas kernels, backward(): pl.pallas_call(functools.partial(backward_kernel, size, plan, slot.levels...  277 us
    pallas_call x1, Pallas kernels, forward(): pl.pallas_call(functools.partial(forward_kernel, size, plan, slot.levels)...  223 us
    pallas_call x1, Pallas kernels, last(): pl.pallas_call(functools.partial(last_kernel, size, plan), out_shape=outs...  161 us
    pallas_call x1, Pallas kernels, gather(): pl.pallas_call(functools.partial(gather_kernel, size, plan, len(tokens)),...  154 us
    dot_general x13, matrix products, dot(): lax.dot_general(left, right, dims, preferred_element_type=F32).astype(dtype)  131 us

profile of v3, /device:TPU:0, one launch (start us, length us, event | category | flops | bytes accessed | tf_op | source)
XLA Modules:
  0.0 989.8 jit_solution(11682733791233595939)
XLA Ops:
  0.7 0.1 broadcast_in_dim.35
  0.7 0.1 broadcast_in_dim.36
  0.8 0.7 reshape.122
  1.6 0.7 pad_bitcast_fusion
  2.2 1.9 stack.42.refs_6_
  4.1 1.8 copy.45
  5.9 2.2 copy.53
  8.1 154.1 %gather.1 = (bf16[2048,1536]{1,0:T(8,128)(2,1)}, bf16[2048,640]{1,0:T(8,128)(2,1)}, bf16[2048,512]{1,0:T(8,128)(2,1)}, bf16[256,128]{1,0:T(8,128)(2,1)}, bf16[2,...) custom-call(bf16[128,1024]{1,0:T(8,128)(2,1)} %refs_0_.2, bf16[128,1024]{1,0:T(8,128)(2,1)} %refs_1_.1, ...), custom_call_target="tpu_custom_call" | custom-call | tf_op jit(solution)/shard_map/gather/pallas_call | solution.py:1315
  162.2 0.0 copy-start.11
  162.2 3.1 multiply_reduce_fusion
  165.3 0.0 copy-done.11
  165.4 0.7 reshape_squeeze.14.refs_4_.refs_10_
  166.0 0.1 copy.62
  166.1 0.1 copy.50
  166.2 0.1 select_n.60
  166.3 0.0 copy-start.16
  166.3 0.0 slice-start
  166.3 3.4 fusion.1
  169.7 0.0 copy-start.1
  169.7 0.7 slice_bitcast_fusion.5
  170.4 0.0 copy-done.16
  170.4 3.4 fusion.11.refs_1_
  173.8 0.0 copy-start
  173.8 1.8 exponential-minus-one_negate_fusion
  175.7 8.1 convolution_convert_fusion.4.refs_0_.refs_7_
  183.7 223.0 %attend_forward.1 = (bf16[1024,512]{1,0:T(8,128)(2,1)}, f32[1024,512]{1,0:T(8,128)}, f32[1024,64]{1,0:T(8,128)}, f32[1024,64]{1,0:T(8,128)}, f32[1024,256]{1,0:T...) custom-call(bf16[1024,1536]{1,0:T(8,128)(2,1)} %convolution_convert_, ...), custom_call_target="tpu_custom_call" | custom-call | tf_op jit(solution)/shard_map/attend_forward/pallas_call | solution.py:695
  406.8 19.0 %fusion.12 = f32[1024,2816]{1,0:T(8,128)} fusion(bf16[1024,2048]{1,0:T(8,128)(2,1)} %bitcast.103, bf16[2048,2816]{1,0:T(8,128)(2,1)} %get-tuple-element.61), kind=kOutput, calls=%fused_computation.49 | convolution fusion | flops 11811160064 | bytes 27262976 | tf_op jit(solution)/shard_map/dot_general | solution.py:1327
  425.8 0.0 copy-done.13
  425.8 12.8 %multiply_convert_fusion.2 = (bf16[1024,1408]{1,0:T(8,128)(2,1)}, bf16[1024,1408]{1,0:T(8,128)(2,1)}, bf16[1024,1408]{1,0:T(8,128)(2,1)S(1)}) fusion(f32[1024,2816]{1,0:T(8,128)} %fusion.12, bf16[1024,2048]{1,0:T(8,128)(2,1)S(1)} %bitcast.101, bf16[2048,1408]{1,0:T(8,128)(2,1)S(1)} %copy-done.12), kind=kOutput, calls=%fused_computation.11 | convolution fusion | flops 5927206912 | bytes 30146560 | tf_op jit(solution)/shard_map/dot_general | solution.py:1327
  438.7 8.3 convolution_convert_fusion.5
  446.9 18.1 %convolution_convert_fusion.3 = bf16[1024,2048]{1,0:T(8,128)(2,1)} fusion(bf16[2048,2816]{1,0:T(8,128)(2,1)} %get-tuple-element.61, bf16[1024,1408]{1,0:T(8,128)(2,1)} %get-tuple-element.124, bf16[1024,1408]{1,0:T(8,128)(2,1)} %get-tuple-element.123), kind=kOutput, calls=%fused_computation.14 | convolution fusion | flops 11824791552 | bytes 21495808 | tf_op jit(solution)/shard_map/dot_general | solution.py:1327
  465.0 17.7 %convolution_convert_fusion.refs_20_ = bf16[2048,2816]{1,0:T(8,128)(2,1)} fusion(bf16[1024,2048]{1,0:T(8,128)(2,1)S(1)} %bitcast.104, bf16[1024,1408]{1,0:T(8,128)(2,1)} %get-tuple-element.124, bf16[1024,1408]{1,0:T(8,128)(2,1)} %get-tuple-element.123), kind=kOutput, calls=%fused_computation | convolution fusion | flops 11828461568 | bytes 21495808 | tf_op jit(solution)/shard_map/dot_general | solution.py:1327
  482.8 8.6 convolution_convert_fusion.2.refs_21_
  491.4 277.1 %attend_backward.1 = (f32[256,2048]{1,0:T(8,128)}, bf16[2,2,256,2048]{3,2,1,0:T(8,128)(2,1)}, f32[1,2048]{1,0:T(1,128)}, bf16[1024,512]{1,0:T(8,128)(2,1)}, f32[...) custom-call(bf16[2,256,2048]{2,1,0:T(8,128)(2,1)} %refs_0_.3, ...), custom_call_target="tpu_custom_call" | custom-call | tf_op jit(solution)/shard_map/attend_backward/pallas_call | solution.py:1122
  768.5 1.7 convert_reduce_fusion
  770.1 0.5 broadcast.82
  770.6 1.3 reduce.8
  772.0 0.1 reshape.128
  772.1 0.1 broadcast_in_dim.38
  772.2 0.1 copy.56
  772.2 0.1 copy.57
  772.4 1.4 stack.47.refs_6_
  773.8 6.0 convolution_convert_fusion.7.refs_7_
  779.8 1.5 copy.59
  781.4 10.1 %fusion.13 = f32[1024,2048]{1,0:T(8,128)S(1)} fusion(bf16[1024,1536]{1,0:T(8,128)(2,1)} %get-tuple-element.69, bf16[2048,1536]{1,0:T(8,128)(2,1)} %get-tuple-element.55), kind=kOutput, calls=%fused_computation.50 | convolution fusion | flops 6442450944 | bytes 17825792 | tf_op jit(solution)/shard_map/dot_general | solution.py:1327
  791.5 5.0 add_convert_fusion
  796.5 5.1 convolution_convert_fusion.6.refs_9_
  801.7 8.7 convolution_convert_fusion.1.refs_8_
  810.4 160.6 %last.1 = (f32[2,256,2048]{2,1,0:T(8,128)}, bf16[2,256,2048]{2,1,0:T(8,128)(2,1)}, f32[8,128]{1,0:T(8,128)}, f32[128,1024]{1,0:T(8,128)}, f32[128,1024]{1,0:T(8,...) custom-call(bf16[2,2,256,2048]{3,2,1,0:T(8,128)(2,1)} %bitcast.79, ...), custom_call_target="tpu_custom_call" | custom-call | tf_op jit(solution)/shard_map/last/pallas_call | solution.py:1217
  971.1 0.8 fusion.5
  971.9 0.6 select_n.67
  972.6 1.2 slice_bitcast_fusion.4
  973.8 1.3 slice_bitcast_fusion.2
  975.0 1.5 slice_bitcast_fusion
  976.5 2.0 copy.58
  978.5 3.3 copy.74
  981.9 2.1 copy.75
  984.0 0.8 copy.76
  984.8 0.8 copy.77
  985.6 0.8 copy.78
  986.4 0.8 copy.79
  987.2 0.0 copy-done.5
  987.2 1.1 copy.80
  988.3 1.1 copy.81
  (57 shorter events, 0.2 us)
Async XLA Ops:
  162.2 3.1 copy-start.11
  166.3 4.1 copy-start.16
  166.3 9.4 slice-start
  169.7 6.0 copy-start.1
  170.4 5.3 slice-start.1
  173.8 9.9 %copy-start = (f32[1024,640]{1,0:T(8,128)}, f32[1024,640]{1,0:T(8,128)S(1)}, u32[]{:S(2)}) copy-start(f32[1024,640]{1,0:T(8,128)S(1)} %fusion.11.refs_1_) | copy-start | bytes 7864324
  406.8 19.0 %copy-start.12 = (bf16[2048,1408]{1,0:T(8,128)(2,1)S(1)}, bf16[2048,1408]{1,0:T(8,128)(2,1)}, u32[]{:S(2)}) copy-start(bf16[2048,1408]{1,0:T(8,128)(2,1)} %get-tuple-element.59) | copy-start | bytes 17301508
  406.8 19.0 %copy-start.13 = (bf16[2,2,256,2048]{3,2,1,0:T(8,128)(2,1)S(1)}, bf16[2,2,256,2048]{3,2,1,0:T(8,128)(2,1)}, u32[]{:S(2)}) copy-start(bf16[2,2,256,2048]{3,2,1,0:T(8,128)(2,1)} %get-tuple-element.58) | copy-start | bytes 12582916
  438.7 8.3 copy-start.20
  446.9 18.1 %copy-start.14 = (bf16[2,2,256,2048]{3,2,1,0:T(8,128)(2,1)S(1)}, bf16[2,2,256,2048]{3,2,1,0:T(8,128)(2,1)}, u32[]{:S(2)}) copy-start(bf16[2,2,256,2048]{3,2,1,0:T(8,128)(2,1)} %get-tuple-element.60) | copy-start | bytes 12582916
  465.0 17.7 %copy-start.21 = (bf16[1024,1408]{1,0:T(8,128)(2,1)S(1)}, bf16[1024,1408]{1,0:T(8,128)(2,1)}, u32[]{:S(2)}) copy-start(bf16[1024,1408]{1,0:T(8,128)(2,1)} %copy-done.20) | copy-start | bytes 8650756
  491.4 282.4 %copy-start.18 = (bf16[1024,512]{1,0:T(8,128)(2,1)S(1)}, bf16[1024,512]{1,0:T(8,128)(2,1)}, u32[]{:S(2)}) copy-start(bf16[1024,512]{1,0:T(8,128)(2,1)} %get-tuple-element.76) | copy-start | bytes 3145732
  773.8 6.0 copy-start.6
  781.4 10.1 %copy-start.17 = (bf16[2048,640]{1,0:T(8,128)(2,1)S(1)}, bf16[2048,640]{1,0:T(8,128)(2,1)}, u32[]{:S(2)}) copy-start(bf16[2048,640]{1,0:T(8,128)(2,1)} %get-tuple-element.54) | copy-start | bytes 7864324
  781.4 10.1 %copy-start.19 = (bf16[1024,512]{1,0:T(8,128)(2,1)S(1)}, bf16[1024,512]{1,0:T(8,128)(2,1)}, u32[]{:S(2)}) copy-start(bf16[1024,512]{1,0:T(8,128)(2,1)} %get-tuple-element.70) | copy-start | bytes 3145732
  791.5 5.0 copy-start.2
  796.5 5.2 copy-start.15
  978.5 3.3 copy-start.3
  981.8 2.1 copy-start.10
  981.9 2.9 copy-start.9
  981.9 3.7 copy-start.8
  981.9 4.5 copy-start.7
  984.0 3.2 copy-start.5
  984.0 4.3 copy-start.4

commit v4 on v3

--- a/solution.py
+++ b/solution.py
@@ -711,6 +711,8 @@
 
 
 POOL_SENDS = 2
+AHEAD = 3
+LAG = 1
 
 
 def pool_scratch(rows, width):
@@ -749,9 +751,8 @@
     def b_copy(self, a):
         return remote(self.block(a, 1 - self.p.b), self.peer.at[a], self.b_sem.at[0, a], self.b_sem.at[1, a], self.p.across())
 
-    def start(self):
-        for n in range(self.p.line):
-            self.b_copy(self.goal(n)).start()
+    def start(self, n):
+        self.b_copy(self.goal(n)).start()
 
     def cut(self, ref):
         return ref if self.width == ref.shape[1] else ref.at[:, pl.ds(0, self.width)]
@@ -886,19 +887,23 @@
 
 def scatter_ops(work, pool):
     lines = work[0].p.line
-    jobs = [(k, n) for k in range(len(work)) for n in range(lines)]
-    steps = [work[0].start]
-    if len(work) > 1:
-        steps.append(work[1].start)
+    jobs = [(k * (lines - 1) + n, k, n) for k in range(len(work)) for n in range(lines - 1)]
+    jobs += [((k + 1) * (lines - 1) - 0.5 + LAG, k, lines - 1) for k in range(len(work))]
+    jobs = [(k, n) for _, k, n in sorted(jobs)]
     sends, totals = [], []
+
+    def begin():
+        for k, n in jobs[:AHEAD]:
+            work[k].start(n)
+
 
     def job(i):
         k, n = jobs[i]
 
         def step():
             work[k].prepare(pool, i % 2, n)
-            if n == 0 and 0 < k < len(work) - 1:
-                work[k + 1].start()
+            if i + AHEAD < len(jobs):
+                work[jobs[i + AHEAD][0]].start(jobs[i + AHEAD][1])
             if n < lines - 1:
                 out = len(sends) % POOL_SENDS
                 if len(sends) >= POOL_SENDS:
@@ -914,7 +919,7 @@
 
         return step
 
-    steps += [job(i) for i in range(len(jobs))]
+    steps = [begin] + [job(i) for i in range(len(jobs))]
 
     def finish():
         for ok, on, oo in sends[-POOL_SENDS:]:
@@ -926,7 +931,7 @@
     steps.append(finish)
     return steps
 
-SECOND_JOBS = ((0, 1), (1, 1), (2, 1), (3, 1))
+BACK_STEPS = (0, 1, 1, 0, 1, 1, 0, 2, 3, 2, 0, 1)
 
 
 def backward_kernel(size, plan, levels, *refs):
@@ -966,10 +971,11 @@
     fold = Fold(p, grad_part, *fold_refs[:3], fold_refs[3:], own_part)
     share = Share(p, low, share_sems)
     fold.start()
-    weave.run(2)
+    weave.run(1 + BACK_STEPS[0])
     own[3].wait()
     for r in range(STRIPS):
         fold.cross(r)
+    weave.run(BACK_STEPS[1])
     own[0].wait()
     gains = jnp.zeros((1, grad_part.shape[3]), F32)
     for r in range(STRIPS):
@@ -979,9 +985,9 @@
         residual_grad[fold.strip(r)] = value
         share.put(r, bf(value))
         if r == 1:
-            weave.run(1)
+            weave.run(BACK_STEPS[2])
     second_part[...] = gains
-    weave.run(1)
+    weave.run(BACK_STEPS[3])
     diag = on_diagonal(count)
     gain_part[...] = jnp.zeros_like(gain_part)
 
@@ -1025,27 +1031,29 @@
     own[1].wait()
     own[2].wait()
     lax.fori_loop(0, 1, first, 0)
+    weave.run(BACK_STEPS[4])
     for r in range(STRIPS):
         share.forward(r)
     share.wait_sibling(False)
     lax.fori_loop(1, 3, first, 0)
-    weave.run(1)
+    weave.run(BACK_STEPS[5])
     share.wait_sibling(True)
     lax.fori_loop(3, 4, first, 0)
-    weave.run(1)
+    weave.run(BACK_STEPS[6])
     for b in range(seqs):
         total[b] = spread(decs[b, 0], 2 * head) * units[b, 1] + units[b, 0]
     carry = Prefix(p, True, total, end_dec, ending, *prefix_refs[:4], prefix_refs[4:])
     carry.start()
-    weave.run(1)
+    weave.run(BACK_STEPS[7])
     carry.run()
-    weave.run(1)
     for b in range(seqs):
         adjoints[b, 1] = ending[b]
         adjoints[b, 0] = spread(decs[b, 1], 2 * head) * ending[b] + units[b, 1]
     is_last = (lax.broadcasted_iota(jnp.int32, (count, 1), 0) == count - 1).astype(F32)
 
     def second(i, nothing):
+        for k in range(4):
+            pl.when(i == k)(functools.partial(weave.run, BACK_STEPS[8 + k]))
         b, j = place(i)
         rows = pl.ds(pl.multiple_of((b * 2 + j) * count, count), count)
         here = keep[rows, :]
@@ -1084,8 +1092,6 @@
         at_end = jnp.sum(at_end * on_diagonal(adj.shape[0]), axis=0, keepdims=True)
         dsum += is_last * at_end
         decay_term[rows, :] = exact_sums(later[...], dsum) - (1.0 - here) * dkeep
-        for k, jobs in SECOND_JOBS:
-            pl.when(i == k)(functools.partial(weave.run, jobs))
         return nothing
 
     lax.fori_loop(0, 4, second, 0)
@@ -1153,7 +1159,7 @@
     weave = Weave(scatter_ops(work, pool))
     fold = Fold(p, part, *fold_refs[:3], fold_refs[3:])
     ff = Fold(p, ff_part, *ff_refs[:3], ff_refs[3:])
-    weave.run(2)
+    weave.run(1)
     fold.start()
     ff.start()
     for r in range(STRIPS):

time: 1000 us -> 951 us (0.951)
  Pallas kernels: 815 us -> 766 us
    pallas_call x1, Pallas kernels: 277 us -> 235 us  [backward(): pl.pallas_call(functools.partial(backward_kernel, size, plan, slot.levels...]
where the time goes in v4:
time: 951 us; the launch traced here: 941 us
  Pallas kernels  766 us (81%)
  matrix products  131 us (14%)
  local copies, waits for them, and re-layouts  30.4 us (3%)
  other arithmetic  12.2 us (1%)
    pallas_call x1, Pallas kernels, backward(): pl.pallas_call(functools.partial(backward_kernel, size, plan, slot.levels...  235 us
    pallas_call x1, Pallas kernels, forward(): pl.pallas_call(functools.partial(forward_kernel, size, plan, slot.levels)...  223 us
    pallas_call x1, Pallas kernels, last(): pl.pallas_call(functools.partial(last_kernel, size, plan), out_shape=outs...  154 us
    pallas_call x1, Pallas kernels, gather(): pl.pallas_call(functools.partial(gather_kernel, size, plan, len(tokens)),...  154 us
    dot_general x13, matrix products, dot(): lax.dot_general(left, right, dims, preferred_element_type=F32).astype(dtype)  131 us

profile of v4, /device:TPU:0, one launch (start us, length us, event | category | flops | bytes accessed | tf_op | source)
XLA Modules:
  0.0 940.8 jit_solution(7694290323239060451)
XLA Ops:
  0.7 0.1 broadcast_in_dim.35
  0.7 0.1 broadcast_in_dim.36
  0.8 0.7 reshape.122
  1.6 0.7 pad_bitcast_fusion
  2.2 1.9 stack.42.refs_6_
  4.1 1.8 copy.45
  5.9 2.2 copy.53
  8.1 154.1 %gather.1 = (bf16[2048,1536]{1,0:T(8,128)(2,1)}, bf16[2048,640]{1,0:T(8,128)(2,1)}, bf16[2048,512]{1,0:T(8,128)(2,1)}, bf16[256,128]{1,0:T(8,128)(2,1)}, bf16[2,...) custom-call(bf16[128,1024]{1,0:T(8,128)(2,1)} %refs_0_.2, bf16[128,1024]{1,0:T(8,128)(2,1)} %refs_1_.1, ...), custom_call_target="tpu_custom_call" | custom-call | tf_op jit(solution)/shard_map/gather/pallas_call | solution.py:1321
  162.2 3.1 multiply_reduce_fusion
  165.3 0.0 copy-done.11
  165.4 0.7 reshape_squeeze.14.refs_4_.refs_10_
  166.0 0.1 copy.62
  166.1 0.1 copy.50
  166.2 0.1 select_n.60
  166.3 0.0 copy-start.16
  166.3 0.0 slice-start
  166.3 3.4 fusion.1
  169.7 0.0 copy-start.1
  169.7 0.7 slice_bitcast_fusion.5
  170.4 3.4 fusion.11.refs_1_
  173.8 1.8 exponential-minus-one_negate_fusion
  175.7 0.0 slice-done.1
  175.7 8.1 convolution_convert_fusion.4.refs_0_.refs_7_
  183.7 223.0 %attend_forward.1 = (bf16[1024,512]{1,0:T(8,128)(2,1)}, f32[1024,512]{1,0:T(8,128)}, f32[1024,64]{1,0:T(8,128)}, f32[1024,64]{1,0:T(8,128)}, f32[1024,256]{1,0:T...) custom-call(bf16[1024,1536]{1,0:T(8,128)(2,1)} %convolution_convert_, ...), custom_call_target="tpu_custom_call" | custom-call | tf_op jit(solution)/shard_map/attend_forward/pallas_call | solution.py:695
  406.8 19.0 %fusion.12 = f32[1024,2816]{1,0:T(8,128)} fusion(bf16[1024,2048]{1,0:T(8,128)(2,1)} %bitcast.103, bf16[2048,2816]{1,0:T(8,128)(2,1)} %get-tuple-element.61), kind=kOutput, calls=%fused_computation.49 | convolution fusion | flops 11811160064 | bytes 27262976 | tf_op jit(solution)/shard_map/dot_general | solution.py:1333
  425.8 12.8 %multiply_convert_fusion.2 = (bf16[1024,1408]{1,0:T(8,128)(2,1)}, bf16[1024,1408]{1,0:T(8,128)(2,1)}, bf16[1024,1408]{1,0:T(8,128)(2,1)S(1)}) fusion(f32[1024,2816]{1,0:T(8,128)} %fusion.12, bf16[1024,2048]{1,0:T(8,128)(2,1)S(1)} %bitcast.101, bf16[2048,1408]{1,0:T(8,128)(2,1)S(1)} %copy-done.12), kind=kOutput, calls=%fused_computation.11 | convolution fusion | flops 5927206912 | bytes 30146560 | tf_op jit(solution)/shard_map/dot_general | solution.py:1333
  438.7 8.3 convolution_convert_fusion.5
  446.9 18.1 %convolution_convert_fusion.3 = bf16[1024,2048]{1,0:T(8,128)(2,1)} fusion(bf16[2048,2816]{1,0:T(8,128)(2,1)} %get-tuple-element.61, bf16[1024,1408]{1,0:T(8,128)(2,1)} %get-tuple-element.124, bf16[1024,1408]{1,0:T(8,128)(2,1)} %get-tuple-element.123), kind=kOutput, calls=%fused_computation.14 | convolution fusion | flops 11824791552 | bytes 21495808 | tf_op jit(solution)/shard_map/dot_general | solution.py:1333
  465.0 0.0 copy-done.14
  465.0 17.7 %convolution_convert_fusion.refs_20_ = bf16[2048,2816]{1,0:T(8,128)(2,1)} fusion(bf16[1024,2048]{1,0:T(8,128)(2,1)S(1)} %bitcast.104, bf16[1024,1408]{1,0:T(8,128)(2,1)} %get-tuple-element.124, bf16[1024,1408]{1,0:T(8,128)(2,1)} %get-tuple-element.123), kind=kOutput, calls=%fused_computation | convolution fusion | flops 11828461568 | bytes 21495808 | tf_op jit(solution)/shard_map/dot_general | solution.py:1333
  482.8 8.6 convolution_convert_fusion.2.refs_21_
  491.4 234.6 %attend_backward.1 = (f32[256,2048]{1,0:T(8,128)}, bf16[2,2,256,2048]{3,2,1,0:T(8,128)(2,1)}, f32[1,2048]{1,0:T(1,128)}, bf16[1024,512]{1,0:T(8,128)(2,1)}, f32[...) custom-call(bf16[2,256,2048]{2,1,0:T(8,128)(2,1)} %refs_0_.3, ...), custom_call_target="tpu_custom_call" | custom-call | tf_op jit(solution)/shard_map/attend_backward/pallas_call | solution.py:1128
  726.0 1.7 convert_reduce_fusion
  727.7 0.5 broadcast.82
  728.2 1.3 reduce.8
  729.5 0.1 reshape.128
  729.6 0.1 broadcast_in_dim.38
  729.7 0.1 copy.56
  729.8 0.1 copy.57
  729.9 1.4 stack.47.refs_6_
  731.3 0.0 copy-done.18
  731.3 0.0 copy-start.6
  731.3 6.0 convolution_convert_fusion.7.refs_7_
  737.3 1.5 copy.59
  738.9 9.9 %fusion.13 = f32[1024,2048]{1,0:T(8,128)S(1)} fusion(bf16[1024,1536]{1,0:T(8,128)(2,1)} %get-tuple-element.69, bf16[2048,1536]{1,0:T(8,128)(2,1)} %get-tuple-element.55), kind=kOutput, calls=%fused_computation.50 | convolution fusion | flops 6442450944 | bytes 17825792 | tf_op jit(solution)/shard_map/dot_general | solution.py:1333
  748.8 0.0 copy-done.17
  748.8 5.2 add_convert_fusion
  754.1 5.1 convolution_convert_fusion.6.refs_9_
  759.2 8.7 convolution_convert_fusion.1.refs_8_
  768.0 154.1 %last.1 = (f32[2,256,2048]{2,1,0:T(8,128)}, bf16[2,256,2048]{2,1,0:T(8,128)(2,1)}, f32[8,128]{1,0:T(8,128)}, f32[128,1024]{1,0:T(8,128)}, f32[128,1024]{1,0:T(8,...) custom-call(bf16[2,2,256,2048]{3,2,1,0:T(8,128)(2,1)} %bitcast.79, ...), custom_call_target="tpu_custom_call" | custom-call | tf_op jit(solution)/shard_map/last/pallas_call | solution.py:1223
  922.1 0.8 fusion.5
  923.0 0.6 select_n.67
  923.6 1.2 slice_bitcast_fusion.4
  924.8 1.3 slice_bitcast_fusion.2
  926.1 1.5 slice_bitcast_fusion
  927.5 2.0 copy.58
  929.6 3.3 copy.74
  932.9 2.1 copy.75
  935.0 0.8 copy.76
  935.8 0.8 copy.77
  936.6 0.8 copy.78
  937.4 0.8 copy.79
  938.2 1.1 copy.80
  939.3 1.1 copy.81
  (57 shorter events, 0.2 us)
Async XLA Ops:
  162.2 3.1 copy-start.11
  166.3 4.1 copy-start.16
  166.3 9.4 slice-start
  169.7 6.0 copy-start.1
  170.4 5.3 slice-start.1
  173.8 9.9 %copy-start = (f32[1024,640]{1,0:T(8,128)}, f32[1024,640]{1,0:T(8,128)S(1)}, u32[]{:S(2)}) copy-start(f32[1024,640]{1,0:T(8,128)S(1)} %fusion.11.refs_1_) | copy-start | bytes 7864324
  406.8 19.0 %copy-start.12 = (bf16[2048,1408]{1,0:T(8,128)(2,1)S(1)}, bf16[2048,1408]{1,0:T(8,128)(2,1)}, u32[]{:S(2)}) copy-start(bf16[2048,1408]{1,0:T(8,128)(2,1)} %get-tuple-element.59) | copy-start | bytes 17301508
  406.8 19.0 %copy-start.13 = (bf16[2,2,256,2048]{3,2,1,0:T(8,128)(2,1)S(1)}, bf16[2,2,256,2048]{3,2,1,0:T(8,128)(2,1)}, u32[]{:S(2)}) copy-start(bf16[2,2,256,2048]{3,2,1,0:T(8,128)(2,1)} %get-tuple-element.58) | copy-start | bytes 12582916
  438.7 8.3 copy-start.20
  446.9 18.1 %copy-start.14 = (bf16[2,2,256,2048]{3,2,1,0:T(8,128)(2,1)S(1)}, bf16[2,2,256,2048]{3,2,1,0:T(8,128)(2,1)}, u32[]{:S(2)}) copy-start(bf16[2,2,256,2048]{3,2,1,0:T(8,128)(2,1)} %get-tuple-element.60) | copy-start | bytes 12582916
  465.0 17.7 %copy-start.21 = (bf16[1024,1408]{1,0:T(8,128)(2,1)S(1)}, bf16[1024,1408]{1,0:T(8,128)(2,1)}, u32[]{:S(2)}) copy-start(bf16[1024,1408]{1,0:T(8,128)(2,1)} %copy-done.20) | copy-start | bytes 8650756
  491.4 240.0 %copy-start.18 = (bf16[1024,512]{1,0:T(8,128)(2,1)S(1)}, bf16[1024,512]{1,0:T(8,128)(2,1)}, u32[]{:S(2)}) copy-start(bf16[1024,512]{1,0:T(8,128)(2,1)} %get-tuple-element.76) | copy-start | bytes 3145732
  731.3 6.0 copy-start.6
  738.9 9.9 %copy-start.17 = (bf16[2048,640]{1,0:T(8,128)(2,1)S(1)}, bf16[2048,640]{1,0:T(8,128)(2,1)}, u32[]{:S(2)}) copy-start(bf16[2048,640]{1,0:T(8,128)(2,1)} %get-tuple-element.54) | copy-start | bytes 7864324
  738.9 9.9 %copy-start.19 = (bf16[1024,512]{1,0:T(8,128)(2,1)S(1)}, bf16[1024,512]{1,0:T(8,128)(2,1)}, u32[]{:S(2)}) copy-start(bf16[1024,512]{1,0:T(8,128)(2,1)} %get-tuple-element.70) | copy-start | bytes 3145732
  748.8 5.2 copy-start.2
  754.1 5.2 copy-start.15
  929.6 3.3 copy-start.3
  932.9 2.1 copy-start.10
  932.9 2.9 copy-start.9
  932.9 3.7 copy-start.8
  932.9 4.5 copy-start.7
  935.0 3.2 copy-start.5
  935.0 4.3 copy-start.4

commit v5 on v4

--- a/solution.py
+++ b/solution.py
@@ -185,28 +185,34 @@
 
 
 class Gather:
-    def __init__(self, place, shard, full, unit, offset, width, sems, late):
-        self.pl, self.shard, self.full = place, shard, full
-        self.unit, self.offset, self.width, self.late = unit, offset, width, late
+    def __init__(self, place, full, unit, pieces, sems, late=False):
+        self.pl, self.full, self.unit, self.pieces, self.late = place, full, unit, pieces, late
+        self.offset = min(offset for _, offset, _ in pieces)
+        self.width = sum(width for _, _, width in pieces)
         self.x_sem, self.b_sem, self.up_sem, self.down_sem = sems
 
-    def part(self, start, count):
+    def part(self, start, count, offset=None, width=None):
+        offset, width = (self.offset, self.width) if width is None else (offset, width)
         rows = pl.ds(start * self.unit, count * self.unit)
-        if self.width == self.full.shape[1]:
+        if width == self.full.shape[1]:
             return self.full.at[rows]
-        return self.full.at[rows, pl.ds(self.offset, self.width)]
-
-    def mine(self, x):
-        if self.shard.shape[1] == self.width:
-            return self.shard
-        return self.shard.at[:, pl.ds(x * self.width, self.width)]
-
-    def x_copy(self):
+        return self.full.at[rows, pl.ds(offset, width)]
+
+    def mine(self, i, x):
+        shard, _, width = self.pieces[i]
+        if shard.shape[1] == width:
+            return shard
+        return shard.at[:, pl.ds(x * width, width)]
+
+    def x_copy(self, i):
         p = self.pl
-        return remote(self.mine(1 - p.x), self.part(p.s, 1), self.x_sem.at[0], self.x_sem.at[1], p.partner())
-
-    def own_copy(self):
-        return pltpu.make_async_copy(self.mine(self.pl.x), self.part(self.pl.s, 1), self.x_sem.at[2])
+        _, offset, width = self.pieces[i]
+        here = self.part(p.s, 1, offset, width)
+        return remote(self.mine(i, 1 - p.x), here, self.x_sem.at[0, i], self.x_sem.at[1, i], p.partner())
+
+    def own_copy(self, i):
+        _, offset, width = self.pieces[i]
+        return pltpu.make_async_copy(self.mine(i, self.pl.x), self.part(self.pl.s, 1, offset, width), self.x_sem.at[2, i])
 
     def block(self, a):
         p = self.pl
@@ -251,14 +257,16 @@
         return h if way == "up" else self.pl.line - 1 + h
 
     def start_x(self):
-        self.x_copy().start()
-        self.own_copy().start()
+        for i in range(len(self.pieces)):
+            self.x_copy(i).start()
+            self.own_copy(i).start()
 
     def stage(self, h):
         p = self.pl
         if h == 0:
-            self.own_copy().wait()
-            self.x_copy().wait_recv()
+            for i in range(len(self.pieces)):
+                self.own_copy(i).wait()
+                self.x_copy(i).wait_recv()
             if self.late:
                 self.b_copy(0, p.a).start()
             else:
@@ -292,7 +300,8 @@
 
     def finish(self):
         p = self.pl
-        self.x_copy().wait_send()
+        for i in range(len(self.pieces)):
+            self.x_copy(i).wait_send()
         self.b_copy(0, p.a).wait_send()
         if not self.late:
             self.b_copy(0, p.a).wait_recv()
@@ -309,31 +318,28 @@
                     pl.when(self.gets(way, h))(both)
 
 
-def gather_sems(line):
+def gather_sems(line, pieces):
     return [
-        pltpu.SemaphoreType.DMA((3,)),
+        pltpu.SemaphoreType.DMA((3, pieces)),
         pltpu.SemaphoreType.DMA((2, 2 * line - 1)),
         pltpu.SemaphoreType.DMA((2, line - 1)),
         pltpu.SemaphoreType.DMA((2, line - 1)),
     ]
 
 
-def gather_ops(gathers, ahead):
-    steps = []
-    n = len(gathers)
-    for k in range(min(ahead, n)):
-        steps.append(gathers[k].start_x)
-    steps.append(functools.partial(gathers[0].stage, 0))
-    for k in range(n):
-        if k + ahead < n:
-            steps.append(gathers[k + ahead].start_x)
-        if k + 1 < n:
-            steps.append(functools.partial(gathers[k + 1].stage, 0))
-        for h in range(1, gathers[k].stages()):
-            steps.append(functools.partial(gathers[k].stage, h))
-    for g in gathers:
-        steps.append(g.finish)
-    return steps
+def gathers_of(place, plan, shards, fulls, sems):
+    work, at = [], 0
+    for n, (i, unit, columns) in enumerate(plan):
+        pieces = [(shards[at + m], offset, width) for m, (offset, width) in enumerate(columns)]
+        at += len(columns)
+        work.append(Gather(place, fulls[i], unit, pieces, sems[4 * n : 4 * n + 4]))
+    return work
+
+
+def gather_ops(gathers, pace):
+    order = sorted((k * pace + h, k, h) for k, g in enumerate(gathers) for h in range(g.stages()))
+    steps = [functools.partial(gathers[k].stage, h) for _, k, h in order]
+    return steps + [g.finish for g in gathers]
 
 VM = pl.BlockSpec(memory_space=pltpu.VMEM)
 ANY = pl.BlockSpec(memory_space=HBM)
@@ -578,26 +584,31 @@
     return block
 
 
+PACE = 1.5
+FORE_STEPS = (0, 6, 0, 4, 0, 2, 0, 0)
+
+
 def forward_kernel(size, plan, levels, *refs):
     p = Place(size)
-    (qkv, gates, decay, keep, gain, out_w, tokens, gain2, paths, masks), refs = take(refs, 10)
-    shard_refs, refs = take(refs, len(plan))
-    (gated, attended, probs, scores, weights, states, decs, end_dec, residual, normed), refs = take(refs, 10)
-    fulls, refs = take(refs, max(i for i, _, _, _, _ in plan) + 1)
+    (qkv, gates, decay, keep, gain, out_w, tokens, gain2, paths, masks, grad_out), refs = take(refs, 11)
+    shard_refs, refs = take(refs, sum(len(columns) for _, _, columns in plan))
+    (gated, attended, probs, scores, weights, states, decs, end_dec, residual, normed, grads), refs = take(refs, 11)
+    fulls, refs = take(refs, max(i for i, _, _ in plan) + 1)
     (units, part, total), refs = take(refs, 3)
     (start, *prefix_refs), refs = take(refs, 8)
     fold_refs, refs = take(refs, 5)
     share_sems, refs = take(refs, 2)
+    (swap_sem,), refs = take(refs, 1)
     count = paths.shape[1]
     head = gated.shape[1]
     seqs = tokens.shape[0]
     slots = keep.shape[1]
     greet(p, sibling=True)
-    work = []
-    for n, (i, unit, offset, width, late) in enumerate(plan):
-        work.append(Gather(p, shard_refs[n], fulls[i], unit, offset, width, refs[4 * n : 4 * n + 4], late))
-    weave = Weave(gather_ops(work, 3))
-    weave.run(3)
+    work = gathers_of(p, plan, shard_refs, fulls, refs)
+    for gathered in work:
+        gathered.start_x()
+    weave = Weave(gather_ops(work, PACE))
+    weave.run(FORE_STEPS[0])
     tail = paths[(levels + 1) * count :, :]
 
     def ends(b):
@@ -615,13 +626,15 @@
         ends(b)
     carry = Prefix(p, False, total, end_dec, start, *prefix_refs[:4], prefix_refs[4:])
     carry.start()
-    weave.run(1)
+    weave.run(FORE_STEPS[1])
+    move = Swap(p, grad_out, grads, swap_sem)
+    move.start()
     carry.run()
     for b in range(seqs):
         states[3 * b] = start[b]
         for j in range(2):
             states[3 * b + j + 1] = spread(decs[b, j], 2 * head) * states[3 * b + j] + units[b, j]
-    weave.run(1)
+    weave.run(FORE_STEPS[2])
     diag = on_diagonal(count)
     order = blocks_in_order(p, seqs)
     fold = Fold(p, part, *fold_refs[:3], fold_refs[3:])
@@ -658,49 +671,54 @@
         return nothing
 
     lax.fori_loop(0, 2, attend, 0)
-    weave.run(1)
+    weave.run(FORE_STEPS[3])
     lax.fori_loop(2, 3, attend, 0)
     for r in range(STRIPS):
         fold.cross(r)
+    weave.run(FORE_STEPS[4])
+    move.forward()
     lax.fori_loop(3, 4, attend, 0)
-    weave.run(1)
+    weave.run(FORE_STEPS[5])
     for r in range(STRIPS):
         value = tokens[p.c, fold.strip(r)].astype(F32) + fold.total(r)
         residual[fold.strip(r)] = value
         share.put(r, bf(value * inverse_rms(value) * gain2[...]))
-    weave.run(2)
+        if r == 1:
+            weave.run(FORE_STEPS[6])
+    weave.run(FORE_STEPS[7])
     for r in range(STRIPS):
         share.forward(r)
     weave.rest()
     share.finish()
     fold.finish()
     carry.finish()
-
-
-def forward(size, number, slot, plan, fulls, qkv, gates, decay, keep, gain, out_w, tokens, gain2, shards):
+    move.finish()
+
+
+def forward(size, number, slot, plan, fulls, qkv, gates, decay, keep, gain, out_w, tokens, gain2, grad_out, shards):
     seqs, block, width = tokens.shape
     h, m, n, rows = slot.head, slot.slots, slot.chunks, slot.seqs * slot.rows
     shape = jax.ShapeDtypeStruct
     outs = [
         shape((rows, h), BF16), shape((rows, h), F32), shape((rows, m), F32), shape((rows, m), F32), shape((rows, slot.chunk), F32),
         shape((seqs * (n + 1), m, 2 * h), F32), shape((seqs, n, m, 128), F32), shape((seqs, m, 128), F32),
-        shape((block, width), F32), shape((seqs, 2, block, width), BF16),
+        shape((block, width), F32), shape((seqs, 2, block, width), BF16), shape((seqs, 2, block, width), BF16),
     ]
     scratch = [
         pltpu.VMEM((seqs, n, m, 2 * h), F32), pltpu.VMEM((seqs, 2, block, width), BF16), pltpu.VMEM((seqs, m, 2 * h), F32),
     ]
-    scratch += prefix_scratch(seqs, m, 2 * h) + fold_scratch(block, width) + SHARE_SEMS
-    for _ in plan:
-        scratch += gather_sems(size // 4)
+    scratch += prefix_scratch(seqs, m, 2 * h) + fold_scratch(block, width) + SHARE_SEMS + [pltpu.SemaphoreType.DMA((5,))]
+    for _, _, columns in plan:
+        scratch += gather_sems(size // 4, len(columns))
     return pl.pallas_call(
         functools.partial(forward_kernel, size, plan, slot.levels),
         out_shape=outs + [shape(full, BF16) for full in fulls],
-        in_specs=[VM] * 10 + [ANY] * len(shards),
-        out_specs=[VM] * 10 + [ANY] * len(fulls),
+        in_specs=[VM] * 10 + [ANY] * (1 + len(shards)),
+        out_specs=[VM] * 10 + [ANY] * (1 + len(fulls)),
         scratch_shapes=scratch,
         compiler_params=remote_params(number, 60),
         name="attend_forward",
-    )(qkv, gates, decay, keep, gain, out_w, tokens, gain2, slot.paths, slot.masks, *shards)
+    )(qkv, gates, decay, keep, gain, out_w, tokens, gain2, slot.paths, slot.masks, grad_out, *shards)
 
 class Pool:
     def __init__(self, refs):
@@ -1137,18 +1155,49 @@
     return result[: 7 + len(results)]
 
 
+def products(p, part, fold, terms, i):
+    count, width = part.shape[2], part.shape[3]
+    stripe = min(512, width)
+    b, x = blocks_in_order(p, part.shape[0])(i)
+    rows = pl.ds(pl.multiple_of((b * 2 + x) * count, count), count)
+
+    def one(t, nothing):
+        columns = pl.ds(pl.multiple_of(t * stripe, stripe), stripe)
+        value = None
+        for left, right in terms:
+            more = mm(left[rows, :], right[columns, :], NT)
+            value = more if value is None else value + more
+        part[b, x, :, columns] = bf(value)
+        return nothing
+
+    lax.fori_loop(0, width // stripe, one, 0)
+    if i < 2:
+        fold.sib_all(i == 0)
+
+
+LAST_STEPS = (0, 1, 1, 1, 1, 1, 1, 2, 1)
+
+
 def last_kernel(size, plan, *refs):
     p = Place(size)
-    (part, ff_part, tokens, residual, residual_grad, gain, pack), refs = take(refs, 7)
+    (qkv_full, gate_full, down_full), refs = take(refs, 3)
+    (qkv_term, gates_term, activated, tokens, residual, residual_grad, gain, pack), refs = take(refs, 8)
     grads = max(i for i, _, _, _, _ in plan) + 1
     grad_refs, refs = take(refs, grads)
     (input_grad, output, sums), refs = take(refs, 3)
     outs, refs = take(refs, len(plan))
     spaces, refs = take(refs, 2 * len(plan))
+    (part, ff_part, qkv_w, gate_w, down_w, load_sem), refs = take(refs, 6)
     fold_refs, refs = take(refs, 5)
     ff_refs, refs = take(refs, 5)
     (out_sem, mine, came, s_sem), refs = take(refs, 4)
     pool_refs, refs = take(refs, 5)
+    loads = [
+        pltpu.make_async_copy(source, to, load_sem.at[n])
+        for n, (source, to) in enumerate(((qkv_full, qkv_w), (gate_full, gate_w), (down_full, down_w)))
+    ]
+    for load in loads:
+        load.start()
     greet_all(p)
     pool = Pool(pool_refs)
     work = []
@@ -1159,40 +1208,51 @@
     weave = Weave(scatter_ops(work, pool))
     fold = Fold(p, part, *fold_refs[:3], fold_refs[3:])
     ff = Fold(p, ff_part, *ff_refs[:3], ff_refs[3:])
-    weave.run(1)
-    fold.start()
-    ff.start()
+    weave.run(1 + LAST_STEPS[0])
+    loads[0].wait()
+    loads[1].wait()
+    terms = [(qkv_term, qkv_w), (gates_term, gate_w)]
+    for i in range(3):
+        products(p, part, fold, terms, i)
     for r in range(STRIPS):
         fold.cross(r)
-    weave.run(1)
+    weave.run(LAST_STEPS[1])
+    products(p, part, fold, terms, 3)
+    loads[2].wait()
+    products(p, ff_part, ff, [(activated, down_w)], 0)
+    weave.run(LAST_STEPS[2])
+    products(p, ff_part, ff, [(activated, down_w)], 1)
+    products(p, ff_part, ff, [(activated, down_w)], 2)
+    weave.run(LAST_STEPS[3])
+    for r in range(STRIPS):
+        ff.cross(r)
+    products(p, ff_part, ff, [(activated, down_w)], 3)
+    weave.run(LAST_STEPS[4])
     gains = jnp.zeros((1, part.shape[3]), F32)
 
     def out_copy(ref, k, r):
         block = ref.at[p.c, fold.strip(r)]
         return remote(block, block, out_sem.at[0, k * STRIPS + r], out_sem.at[1, k * STRIPS + r], p.sibling())
 
-    for r in range(STRIPS):
-        ff.cross(r)
-    weave.run(2)
     for r in range(STRIPS):
         down, more = norm_back(fold.total(r), tokens[p.c, fold.strip(r)].astype(F32), gain[...])
         gains += more
         input_grad[p.c, fold.strip(r)] = residual_grad[fold.strip(r)] + down
         out_copy(input_grad, 1, r).start()
         if r % 2 == 1:
-            weave.run(1)
+            weave.run(LAST_STEPS[5 + r // 2])
     unit = plan[0][1]
     mine[...] = pack[...]
     for s in range(size):
         mine[s, 0:1, pl.ds(0, unit)] = gains[:, s * unit : (s + 1) * unit]
     smalls = Smalls(p, mine, sums, came, s_sem)
     smalls.start()
-    weave.run(2)
+    weave.run(LAST_STEPS[7])
     for r in range(STRIPS):
         output[p.c, fold.strip(r)] = bf(residual[fold.strip(r)] + ff.total(r))
         out_copy(output, 0, r).start()
         if r % 2 == 1:
-            weave.run(1)
+            weave.run(LAST_STEPS[8])
     weave.rest()
     smalls.finish()
     for r in range(STRIPS):
@@ -1202,8 +1262,9 @@
     fold.finish()
 
 
-def last(size, number, plan, vmem_ins, grads):
-    seqs, _, block, width = vmem_ins[0].shape
+def last(size, number, plan, hbm_ins, vmem_ins, grads):
+    qkv_term, _, _, tokens = vmem_ins[:4]
+    seqs, block, width = tokens.shape
     pack = vmem_ins[-1]
     line = size // 4
     shape = jax.ShapeDtypeStruct
@@ -1215,7 +1276,8 @@
         spaces += [shape((line, 2 * unit, columns), BF16), shape((line + 1, 2 * unit, columns), BF16)]
         sems += scatter_sems(line)
     widest = max(entry[3] for entry in plan)
-    scratch = fold_scratch(block, width) * 2 + [
+    scratch = [pltpu.VMEM((seqs, 2, block, width), BF16)] * 2 + [pltpu.VMEM(w.shape, BF16) for w in hbm_ins]
+    scratch += [pltpu.SemaphoreType.DMA((3,))] + fold_scratch(block, width) * 2 + [
         pltpu.SemaphoreType.DMA((2, 2 * STRIPS)), pltpu.VMEM(pack.shape, F32), pltpu.VMEM((2 * size,) + pack.shape[1:], F32),
         pltpu.SemaphoreType.DMA((2, 2 * size)),
     ]
@@ -1223,12 +1285,12 @@
     result = pl.pallas_call(
         functools.partial(last_kernel, size, plan),
         out_shape=outs + results + spaces,
-        in_specs=[VM] * 7 + [ANY] * len(grads),
+        in_specs=[ANY] * 3 + [VM] * 8 + [ANY] * len(grads),
         out_specs=[VM] * 3 + specs + [ANY] * len(spaces),
         scratch_shapes=scratch,
-        compiler_params=remote_params(number, 60),
+        compiler_params=remote_params(number, 62),
         name="last",
-    )(*vmem_ins, *grads)
+    )(*hbm_ins, *vmem_ins, *grads)
     return result[: 3 + len(results)]
 
 def greet_all(place):
@@ -1288,20 +1350,20 @@
 
 def gather_kernel(size, plan, swaps, *refs):
     p = Place(size)
-    shards = len(plan)
-    fulls = max(i for i, _, _, _, _ in plan) + 1
-    ins, refs = refs[: shards + swaps], refs[shards + swaps :]
-    outs, refs = refs[: fulls + swaps], refs[fulls + swaps :]
+    shards = sum(len(columns) for _, _, columns in plan)
+    fulls = max(i for i, _, _ in plan) + 1
+    ins, refs = take(refs, shards + swaps)
+    outs, refs = take(refs, fulls + swaps)
     greet(p, sibling=True)
-    work = []
-    for n, (i, unit, offset, width, late) in enumerate(plan):
-        work.append(Gather(p, ins[n], outs[i], unit, offset, width, refs[4 * n : 4 * n + 4], late))
-    moves = [Swap(p, ins[shards + n], outs[fulls + n], refs[4 * shards + n]) for n in range(swaps)]
-    weave = Weave(gather_ops(work, len(work)))
-    weave.run(len(work))
+    work = gathers_of(p, plan, ins, outs, refs)
+    moves = [Swap(p, ins[shards + n], outs[fulls + n], refs[4 * len(plan) + n]) for n in range(swaps)]
+    for gathered in work:
+        gathered.start_x()
+    weave = Weave(gather_ops(work, 1))
+    weave.run(4)
     for move in moves:
         move.start()
-    weave.run(len(weave.steps) - len(work))
+    weave.run(len(weave.steps) - len(work) - 4)
     for move in moves:
         move.forward()
     weave.rest()
@@ -1312,8 +1374,8 @@
 def gather(size, number, plan, shards, fulls, tokens):
     line = size // 4
     scratch = []
-    for _ in plan:
-        scratch += gather_sems(line)
+    for _, _, columns in plan:
+        scratch += gather_sems(line, len(columns))
     shapes = [jax.ShapeDtypeStruct(shape, BF16) for shape in fulls]
     for array in tokens:
         shapes.append(jax.ShapeDtypeStruct((array.shape[0], 2) + array.shape[1:], BF16))
@@ -1353,15 +1415,14 @@
     rows = seqs * 2 * block
     pack = jnp.stack([lanes(first_gain), lanes(second_gain), lanes(slot_gain), lanes(forget_bias)] + [jnp.zeros(128, BF16)] * 12)
     plan = [
-        (0, unit, 0, head, False), (0, unit, head, head, False), (0, unit, 2 * head, head, False),
-        (1, unit, 0, head, False), (1, unit, head, 2 * slots, False), (2, unit, 0, head, False),
-        (3, 16, 0, 128, False),
+        (0, unit, [(0, head), (head, head), (2 * head, head)]), (1, unit, [(0, head), (head, 2 * slots)]), (2, unit, [(0, head)]),
+        (3, 16, [(0, 128)]),
     ]
     fulls = [(width, 3 * head), (width, head + 2 * slots), (width, head), (16 * size, 128)]
-    qkv_full, gate_full, out_full, small_full, tok, gout = gather(
+    qkv_full, gate_full, out_full, small_full, tok = gather(
         size, 0, plan,
         (query_weight, key_weight, value_weight, outgate_weight, forget_weight, output_weight.T, pack),
-        fulls, (tokens, grad_out),
+        fulls, (tokens,),
     )
     small = small_full.reshape(size, 16, 128).astype(F32)
     first_full = small[:, 0, :unit].reshape(1, width)
@@ -1381,10 +1442,10 @@
     decay = -jax.nn.softplus(-logit) / TAU
     keep = -jnp.expm1(decay)
     slot = Slots(seqs, 2 * block, head, slots, block)
-    ff_plan = [(0, unit, 0, hidden, False), (0, unit, hidden, hidden, False), (1, unit, 0, hidden, False)]
-    (gated, attended, probs, scores, weights, states, decs, end_decs, residual, normed_two, ff_full, down_full) = forward(
+    ff_plan = [(0, unit, [(0, hidden)]), (0, unit, [(hidden, hidden)]), (1, unit, [(0, hidden)])]
+    (gated, attended, probs, scores, weights, states, decs, end_decs, residual, normed_two, gout, ff_full, down_full) = forward(
         size, 1, slot, ff_plan, [(width, 2 * hidden), (width, hidden)], qkv, gates, decay, keep, slot_full, out_full, tokens,
-        second_full, (gate_weight, up_weight, down_weight.T),
+        second_full, grad_out, (gate_weight, up_weight, down_weight.T),
     )
     shape = (seqs, 2, block, width)
     normed_two = normed_two.reshape(rows, width)
@@ -1392,7 +1453,6 @@
     ff_gate, ff_up = ff[:, :hidden], ff[:, hidden:]
     sig = jax.nn.sigmoid(ff_gate)
     activated = (ff_gate * sig * ff_up).astype(BF16)
-    ff_part = dot(activated, down_full, NT, BF16).reshape(shape)
     gout = gout.reshape(rows, width)
     act_grad = dot(gout, down_full, NN)
     ff_term = jnp.concatenate(
@@ -1418,7 +1478,6 @@
     )
     qkv_grad = dot(normed_one, qkv_term, TN, BF16)
     gates_grad = dot(normed_one, gates_term, TN, BF16)
-    normed_one_grad = (dot(qkv_term, qkv_full, NT) + dot(gates_term, gate_full, NT)).astype(BF16).reshape(shape)
     bias_part = jnp.sum(forget_term.astype(F32), axis=0)
     which = jnp.arange(2 * heads_here) == heads_here * c + x
     bias_part = jnp.where(which[:, None], bias_part[None, :], 0.0).reshape(2 * heads_here, size, slot_part)
@@ -1436,7 +1495,8 @@
         (2, unit, 0, head, False), (2, unit, head, 2 * slots, True),
     ]
     input_grad, output, sums, output_grad, query_grad, key_grad, value_grad, outgate_grad, forget_grad = last(
-        size, 3, plan, (normed_one_grad, ff_part, tokens, residual, residual_grad, first_full, packed),
+        size, 3, plan, (qkv_full, gate_full, down_full),
+        (qkv_term, gates_term, activated, tokens, residual, residual_grad, first_full, packed),
         (out_grad, qkv_grad, gates_grad),
     )
     bias_grad = sums[3, : 2 * heads_here * slot_part].reshape(2, heads_here, slot_part)

time: 951 us -> 896 us (0.942)
  matrix products: 131 us -> 104 us
  Pallas kernels: 766 us -> 739 us
    dot_general x13 -> x10, matrix products: 131 us -> 104 us  [dot(): lax.dot_general(left, right, dims, preferred_element_type=F32).astype(dtype)]
    pallas_call x1, Pallas kernels: 154 us -> 140 us  [gather(): pl.pallas_call(functools.partial(gather_kernel, size, plan, len(tokens)),...]
where the time goes in v5:
time: 896 us; the launch traced here: 885 us
  Pallas kernels  739 us (82%)
  matrix products  104 us (12%)
  local copies, waits for them, and re-layouts  30.7 us (3%)
  other arithmetic  10.9 us (1%)
    pallas_call x1, Pallas kernels, backward(): pl.pallas_call(functools.partial(backward_kernel, size, plan, slot.levels...  237 us
    pallas_call x1, Pallas kernels, forward(): pl.pallas_call(functools.partial(forward_kernel, size, plan, slot.levels)...  214 us
    pallas_call x1, Pallas kernels, last(): pl.pallas_call(functools.partial(last_kernel, size, plan), out_shape=outs...  148 us
    pallas_call x1, Pallas kernels, gather(): pl.pallas_call(functools.partial(gather_kernel, size, plan, len(tokens)),...  140 us
    dot_general x10, matrix products, dot(): lax.dot_general(left, right, dims, preferred_element_type=F32).astype(dtype)  104 us
    unnamed x74, local copies, waits for them, and re-layouts  18 us

profile of v5, /device:TPU:0, one launch (start us, length us, event | category | flops | bytes accessed | tf_op | source)
XLA Modules:
  0.0 885.5 jit_solution(9018231306468977867)
XLA Ops:
  0.7 0.7 reshape.116
  1.4 0.7 pad_bitcast_fusion
  2.1 1.9 stack.42.refs_6_
  3.9 1.8 copy.45
  5.7 139.9 %gather.1 = (bf16[2048,1536]{1,0:T(8,128)(2,1)}, bf16[2048,640]{1,0:T(8,128)(2,1)}, bf16[2048,512]{1,0:T(8,128)(2,1)}, bf16[256,128]{1,0:T(8,128)(2,1)}, bf16[2,2,256,2048]{3,2,1,0:T(8,128)(2,1)}) custom-call(bf16[128,1024]{1,0:T(8,128)(2,1)} %refs_0_.2, bf16[128,1024]{1,0:T(8,128)(2,1)} %refs_1_.1, bf16[128,1024]{1,0:T(8,128)(2,1)} %refs_2_.1, ...), custom_call_target="tpu_custom_call" | custom-call | tf_op jit(solution)/shard_map/gather/pallas_call | solution.py:1383
  145.6 0.8 slice.63
  146.3 0.1 copy.62
  146.4 0.1 copy.50
  146.5 0.1 select_n.60
  146.6 0.0 copy-start.1
  146.6 0.9 slice.62
  147.5 3.3 multiply_reduce_fusion
  150.8 0.0 copy-done.1
  150.9 0.0 copy-start.9
  150.9 0.0 slice-start
  150.9 1.0 fusion.1
  151.9 0.7 copy-done.9
  152.6 3.4 fusion.9.refs_1_
  156.0 0.0 copy-start
  156.0 1.8 exponential-minus-one_negate_fusion
  157.9 0.0 copy-start.14
  157.9 8.1 convolution_convert_fusion.4.refs_0_.refs_7_
  166.0 0.6 slice_bitcast_fusion.5
  166.6 0.7 reshape_squeeze.14.refs_4_.refs_10_
  167.3 1.1 copy.53
  168.4 214.1 %attend_forward.1 = (bf16[1024,512]{1,0:T(8,128)(2,1)}, f32[1024,512]{1,0:T(8,128)}, f32[1024,64]{1,0:T(8,128)}, f32[1024,64]{1,0:T(8,128)}, f32[1024,256]{1,0:T...) custom-call(bf16[1024,1536]{1,0:T(8,128)(2,1)} %convolution_convert_, ...), custom_call_target="tpu_custom_call" | custom-call | tf_op jit(solution)/shard_map/attend_forward/pallas_call | solution.py:713
  382.5 19.0 %fusion.10 = f32[1024,2816]{1,0:T(8,128)} fusion(bf16[1024,2048]{1,0:T(8,128)(2,1)} %bitcast.93, bf16[2048,2816]{1,0:T(8,128)(2,1)} %get-tuple-element.61), kind=kOutput, calls=%fused_computation.45 | convolution fusion | flops 11811160064 | bytes 27262976 | tf_op jit(solution)/shard_map/dot_general | solution.py:1395
  401.5 12.8 %multiply_convert_fusion.2 = (bf16[1024,1408]{1,0:T(8,128)(2,1)}, bf16[1024,1408]{1,0:T(8,128)(2,1)}, bf16[1024,1408]{1,0:T(8,128)(2,1)S(1)}) fusion(f32[1024,2816]{1,0:T(8,128)} %fusion.10, bf16[1024,2048]{1,0:T(8,128)(2,1)S(1)} %bitcast.95, bf16[2048,1408]{1,0:T(8,128)(2,1)S(1)} %copy-done.2), kind=kOutput, calls=%fused_computation.10 | convolution fusion | flops 5927206912 | bytes 30146560 | tf_op jit(solution)/shard_map/dot_general | solution.py:1395
  414.3 8.7 convolution_convert_fusion.2.refs_21_
  423.0 17.7 %convolution_convert_fusion.refs_20_ = bf16[2048,2816]{1,0:T(8,128)(2,1)} fusion(bf16[1024,2048]{1,0:T(8,128)(2,1)S(1)} %bitcast.94, bf16[1024,1408]{1,0:T(8,128)(2,1)} %get-tuple-element.124, bf16[1024,1408]{1,0:T(8,128)(2,1)} %get-tuple-element.123), kind=kOutput, calls=%fused_computation | convolution fusion | flops 11828461568 | bytes 21495808 | tf_op jit(solution)/shard_map/dot_general | solution.py:1395
  440.7 16.3 %convolution_convert_fusion.3 = bf16[1024,2048]{1,0:T(8,128)(2,1)} fusion(bf16[2048,2816]{1,0:T(8,128)(2,1)} %get-tuple-element.61, bf16[1024,1408]{1,0:T(8,128)(2,1)S(1)} %copy-done.27, bf16[1024,1408]{1,0:T(8,128)(2,1)S(1)} %copy-done.26), kind=kOutput, calls=%fused_computation.13 | convolution fusion | flops 11824791552 | bytes 21495808 | tf_op jit(solution)/shard_map/dot_general | solution.py:1395
  457.0 236.7 %attend_backward.1 = (f32[256,2048]{1,0:T(8,128)}, bf16[2,2,256,2048]{3,2,1,0:T(8,128)(2,1)}, f32[1,2048]{1,0:T(1,128)}, bf16[1024,512]{1,0:T(8,128)(2,1)}, f32[...) custom-call(bf16[2,256,2048]{2,1,0:T(8,128)(2,1)} %refs_0_.3, ...), custom_call_target="tpu_custom_call" | custom-call | tf_op jit(solution)/shard_map/attend_backward/pallas_call | solution.py:1146
  693.7 1.8 convert_reduce_fusion
  695.5 1.4 pad_maximum_fusion.3.refs_4_
  696.9 0.0 copy-start.3
  696.9 4.9 convolution_convert_fusion.5.refs_13_
  701.8 9.1 %convolution_convert_fusion.1.refs_12_ = bf16[2048,1536]{1,0:T(8,128)(2,1)} fusion(bf16[1024,2048]{1,0:T(8,128)(2,1)S(1)} %copy-done.5, bf16[1024,1536]{1,0:T(8,128)(2,1)S(1)} %copy-done.7), kind=kOutput, calls=%fused_computation.5 | convolution fusion | flops 6445596672 | bytes 13631488 | tf_op jit(solution)/shard_map/dot_general | solution.py:1395
  711.0 3.8 convolution_convert_fusion.6.refs_11_
  714.8 0.1 broadcast_in_dim.38
  714.8 0.1 copy.56
  714.9 0.1 copy.57
  715.0 0.1 broadcast_in_dim.35
  715.1 0.1 broadcast_in_dim.36
  715.2 0.5 broadcast.82
  715.7 0.7 reduce.8
  716.4 0.1 reshape.120
  716.5 0.7 stack.47.refs_10_
  717.2 148.2 %last.1 = (f32[2,256,2048]{2,1,0:T(8,128)}, bf16[2,256,2048]{2,1,0:T(8,128)(2,1)}, f32[8,128]{1,0:T(8,128)}, f32[128,1024]{1,0:T(8,128)}, f32[128,1024]{1,0:T(8,...) custom-call(bf16[2048,1536]{1,0:T(8,128)(2,1)} %get-tuple-element.52, ...), custom_call_target="tpu_custom_call" | custom-call | tf_op jit(solution)/shard_map/last/pallas_call | solution.py:1285
  865.4 2.2 copy.58
  867.6 1.5 slice_bitcast_fusion
  869.1 0.8 fusion.5
  869.9 0.6 select_n.67
  870.6 1.3 slice_bitcast_fusion.2
  871.8 1.2 slice_bitcast_fusion.4
  873.0 1.5 copy.59
  874.6 1.3 copy.74
  875.9 1.6 copy-done.6
  877.5 2.1 copy.75
  879.6 0.8 copy.76
  880.4 0.8 copy.77
  881.2 0.8 copy.78
  882.0 0.8 copy.79
  882.8 1.1 copy.80
  883.9 1.1 copy.81
  (67 shorter events, 0.2 us)
Async XLA Ops:
  146.6 4.3 copy-start.1
  150.9 1.7 copy-start.9
  150.9 7.0 slice-start
  151.9 6.0 copy-start.4
  152.6 5.3 slice-start.1
  156.0 10.0 %copy-start = (f32[1024,640]{1,0:T(8,128)}, f32[1024,640]{1,0:T(8,128)S(1)}, u32[]{:S(2)}) copy-start(f32[1024,640]{1,0:T(8,128)S(1)} %fusion.9.refs_1_) | copy-start | bytes 7864324
  157.9 8.1 copy-start.19
  157.9 9.4 %copy-start.14 = (bf16[2816,128]{1,0:T(8,128)(2,1)S(1)}, bf16[2816,128]{1,0:T(8,128)(2,1)}, u32[]{:S(2)}) copy-start(bf16[2816,128]{1,0:T(8,128)(2,1)} %param.31) | copy-start | bytes 2162692
  382.5 19.0 %copy-start.2 = (bf16[2048,1408]{1,0:T(8,128)(2,1)S(1)}, bf16[2048,1408]{1,0:T(8,128)(2,1)}, u32[]{:S(2)}) copy-start(bf16[2048,1408]{1,0:T(8,128)(2,1)} %get-tuple-element.57.refs_2_) | copy-start | bytes 17301508
  382.5 19.0 %copy-start.24 = (bf16[2,2,256,2048]{3,2,1,0:T(8,128)(2,1)S(1)}, bf16[2,2,256,2048]{3,2,1,0:T(8,128)(2,1)}, u32[]{:S(2)}) copy-start(bf16[2,2,256,2048]{3,2,1,0:T(8,128)(2,1)} %get-tuple-element.59) | copy-start | bytes 12582916
  414.3 8.7 copy-start.8
  414.3 8.7 copy-start.23
  423.0 17.7 %copy-start.26 = (bf16[1024,1408]{1,0:T(8,128)(2,1)S(1)}, bf16[1024,1408]{1,0:T(8,128)(2,1)}, u32[]{:S(2)}) copy-start(bf16[1024,1408]{1,0:T(8,128)(2,1)} %get-tuple-element.123) | copy-start | bytes 8650756
  423.0 17.7 %copy-start.27 = (bf16[1024,1408]{1,0:T(8,128)(2,1)S(1)}, bf16[1024,1408]{1,0:T(8,128)(2,1)}, u32[]{:S(2)}) copy-start(bf16[1024,1408]{1,0:T(8,128)(2,1)} %get-tuple-element.124) | copy-start | bytes 8650756
  693.6 3.3 copy-start.5
  696.9 4.9 copy-start.3
  696.9 4.9 copy-start.7
  701.8 9.1 %copy-start.22 = (bf16[2,2,256,2048]{3,2,1,0:T(8,128)(2,1)S(1)}, bf16[2,2,256,2048]{3,2,1,0:T(8,128)(2,1)}, u32[]{:S(2)}) copy-start(bf16[2,2,256,2048]{3,2,1,0:T(8,128)(2,1)} %get-tuple-element.75) | copy-start | bytes 12582916
  701.8 9.1 %copy-start.25 = (bf16[1024,512]{1,0:T(8,128)(2,1)S(1)}, bf16[1024,512]{1,0:T(8,128)(2,1)}, u32[]{:S(2)}) copy-start(bf16[1024,512]{1,0:T(8,128)(2,1)} %get-tuple-element.76) | copy-start | bytes 3145732
  711.0 4.7 copy-start.21
  711.0 5.5 copy-start.20
  717.2 155.8 %copy-start.13 = (f32[128,2816]{1,0:T(8,128)S(1)}, f32[128,2816]{1,0:T(8,128)}, u32[]{:S(2)}) copy-start(f32[128,2816]{1,0:T(8,128)} %get-tuple-element.88) | copy-start | bytes 4325380
  865.4 9.1 %copy-start.10 = (bf16[2,256,2048]{2,1,0:T(8,128)(2,1)S(1)}, bf16[2,256,2048]{2,1,0:T(8,128)(2,1)}, u32[]{:S(2)}) copy-start(bf16[2,256,2048]{2,1,0:T(8,128)(2,1)} %get-tuple-element.149) | copy-start | bytes 6291460
  874.5 2.9 copy-start.6
  877.5 2.1 copy-start.18
  877.5 2.9 copy-start.17
  877.5 3.7 copy-start.16
  877.5 4.5 copy-start.15
  879.6 3.2 copy-start.12
  879.6 4.3 copy-start.11

commit v6 on v5

--- a/solution.py
+++ b/solution.py
@@ -730,7 +730,7 @@
 
 POOL_SENDS = 2
 AHEAD = 3
-LAG = 1
+LAG = 3
 
 
 def pool_scratch(rows, width):
@@ -949,7 +949,7 @@
     steps.append(finish)
     return steps
 
-BACK_STEPS = (0, 1, 1, 0, 1, 1, 0, 2, 3, 2, 0, 1)
+BACK_STEPS = (0, 0, 1, 0, 2, 0, 0, 2, 2, 1, 4, 0)
 
 
 def backward_kernel(size, plan, levels, *refs):
@@ -1348,47 +1348,103 @@
         self.hand.wait()
 
 
-def gather_kernel(size, plan, swaps, *refs):
+def gather_kernel(size, plan, *refs):
     p = Place(size)
     shards = sum(len(columns) for _, _, columns in plan)
     fulls = max(i for i, _, _ in plan) + 1
-    ins, refs = take(refs, shards + swaps)
-    outs, refs = take(refs, fulls + swaps)
+    ins, refs = take(refs, shards)
+    (own_tokens,), refs = take(refs, 1)
+    outs, refs = take(refs, fulls)
+    (tokens, normed, qkv, gates), refs = take(refs, 4)
+    (swap_sem, tok, qkv_w, gate_w, small, load_sem), refs = take(refs, 6)
     greet(p, sibling=True)
     work = gathers_of(p, plan, ins, outs, refs)
-    moves = [Swap(p, ins[shards + n], outs[fulls + n], refs[4 * len(plan) + n]) for n in range(swaps)]
+    smalls, qkv_gather, gate_gather, out_gather = work
+    move = Swap(p, own_tokens, tokens, swap_sem)
     for gathered in work:
         gathered.start_x()
-    weave = Weave(gather_ops(work, 1))
+    weave = Weave(gather_ops(work, 1)[: -len(work)])
+    weave.run(6)
+    move.start()
     weave.run(4)
-    for move in moves:
-        move.start()
-    weave.run(len(weave.steps) - len(work) - 4)
-    for move in moves:
-        move.forward()
+    move.forward()
+    weave.run(2)
+    move.finish()
+    smalls.finish()
+    loads = [
+        pltpu.make_async_copy(source, to, load_sem.at[n])
+        for n, (source, to) in enumerate(((tokens, tok), (outs[3], small), (outs[0], qkv_w), (outs[1], gate_w)))
+    ]
+    loads[0].start()
+    loads[1].start()
+    loads[0].wait()
+    loads[1].wait()
+    seqs, pair, block, width = tok.shape
+    unit = plan[1][1]
+    gain = jnp.concatenate([small[16 * s : 16 * s + 1, :unit].astype(F32) for s in range(size)], axis=1)
+    step = 32
+
+    def norm(i, nothing):
+        b, x, r = i // (pair * (block // step)), lax.rem(i // (block // step), pair), lax.rem(i, block // step)
+        rows = pl.ds(pl.multiple_of(r * step, step), step)
+        value = tok[b, x, rows, :].astype(F32)
+        where = pl.ds(pl.multiple_of(i * step, step), step)
+        normed[where, :] = bf(value * inverse_rms(value) * gain)
+        return nothing
+
+    lax.fori_loop(0, seqs * pair * (block // step), norm, 0)
     weave.rest()
-    for move in moves:
-        move.finish()
+    qkv_gather.finish()
+    loads[2].start()
+    gate_gather.finish()
+    loads[3].start()
+    loads[2].wait()
+
+    def rows_of(i):
+        return pl.ds(pl.multiple_of(i * block, block), block)
+
+    third = qkv.shape[1] // 3
+
+    def project(i, nothing):
+        for t in range(3):
+            columns = pl.ds(t * third, third)
+            qkv[rows_of(i), columns] = bf(mm(normed[rows_of(i), :], qkv_w[:, columns], NN))
+        return nothing
+
+    lax.fori_loop(0, seqs * pair, project, 0)
+    loads[3].wait()
+
+    def gate(i, nothing):
+        gates[rows_of(i), :] = mm(normed[rows_of(i), :], gate_w[...], NN)
+        return nothing
+
+    lax.fori_loop(0, seqs * pair, gate, 0)
+    out_gather.finish()
 
 
 def gather(size, number, plan, shards, fulls, tokens):
     line = size // 4
-    scratch = []
+    seqs, block, width = tokens.shape
+    rows = 2 * seqs * block
+    shape = jax.ShapeDtypeStruct
+    sems = []
     for _, _, columns in plan:
-        scratch += gather_sems(line, len(columns))
-    shapes = [jax.ShapeDtypeStruct(shape, BF16) for shape in fulls]
-    for array in tokens:
-        shapes.append(jax.ShapeDtypeStruct((array.shape[0], 2) + array.shape[1:], BF16))
-        scratch.append(pltpu.SemaphoreType.DMA((5,)))
+        sems += gather_sems(line, len(columns))
     return pl.pallas_call(
-        functools.partial(gather_kernel, size, plan, len(tokens)),
-        out_shape=shapes,
-        in_specs=[ANY] * (len(shards) + len(tokens)),
-        out_specs=[ANY] * len(shapes),
-        scratch_shapes=scratch,
+        functools.partial(gather_kernel, size, plan),
+        out_shape=[shape(full, BF16) for full in fulls] + [
+            shape((seqs, 2, block, width), BF16), shape((rows, width), BF16), shape((rows, fulls[0][1]), BF16),
+            shape((rows, fulls[1][1]), F32),
+        ],
+        in_specs=[ANY] * (len(shards) + 1),
+        out_specs=[ANY] * (len(fulls) + 1) + [VM] * 3,
+        scratch_shapes=[
+            pltpu.SemaphoreType.DMA((5,)), pltpu.VMEM((seqs, 2, block, width), BF16), pltpu.VMEM(fulls[0], BF16),
+            pltpu.VMEM(fulls[1], BF16), pltpu.VMEM(fulls[3], BF16), pltpu.SemaphoreType.DMA((4,)),
+        ] + sems,
         compiler_params=remote_params(number, 60),
         name="gather",
-    )(*shards, *tokens)
+    )(*shards, tokens)
 
 
 def dot(left, right, dims, dtype=F32):
@@ -1415,14 +1471,13 @@
     rows = seqs * 2 * block
     pack = jnp.stack([lanes(first_gain), lanes(second_gain), lanes(slot_gain), lanes(forget_bias)] + [jnp.zeros(128, BF16)] * 12)
     plan = [
-        (0, unit, [(0, head), (head, head), (2 * head, head)]), (1, unit, [(0, head), (head, 2 * slots)]), (2, unit, [(0, head)]),
-        (3, 16, [(0, 128)]),
+        (3, 16, [(0, 128)]), (0, unit, [(0, head), (head, head), (2 * head, head)]), (1, unit, [(0, head), (head, 2 * slots)]),
+        (2, unit, [(0, head)]),
     ]
     fulls = [(width, 3 * head), (width, head + 2 * slots), (width, head), (16 * size, 128)]
-    qkv_full, gate_full, out_full, small_full, tok = gather(
+    qkv_full, gate_full, out_full, small_full, _, normed_one, qkv, gates = gather(
         size, 0, plan,
-        (query_weight, key_weight, value_weight, outgate_weight, forget_weight, output_weight.T, pack),
-        fulls, (tokens,),
+        (pack, query_weight, key_weight, value_weight, outgate_weight, forget_weight, output_weight.T), fulls, tokens,
     )
     small = small_full.reshape(size, 16, 128).astype(F32)
     first_full = small[:, 0, :unit].reshape(1, width)
@@ -1434,10 +1489,6 @@
     def own_head(array, axis):
         return jnp.where(x == 0, *jnp.split(array, 2, axis=axis))
 
-    inputs = tok.reshape(rows, width).astype(F32)
-    normed_one = (inputs * inverse_rms(inputs) * first_full).astype(BF16)
-    qkv = dot(normed_one, qkv_full, NN, BF16)
-    gates = dot(normed_one, gate_full, NN)
     logit = own_head(gates[:, head:], 1) + own_head(bias_full, 0)
     decay = -jax.nn.softplus(-logit) / TAU
     keep = -jnp.expm1(decay)
@@ -1461,14 +1512,19 @@
     down_grad = dot(gout, activated, TN, BF16)
     ff_grad = dot(normed_two, ff_term, TN, BF16)
     normed_two_grad = dot(ff_term, ff_full, NT, BF16).reshape(shape)
-    ff_plan = [(0, unit, 0, hidden, False), (0, unit, hidden, hidden, False), (1, unit, 0, hidden, False)]
-    residual_grad, low, second_part, gate_term, slot_part_grad, qkv_term, decay_term, gate_grad, up_grad, down_grad = backward(
+    front = (hidden // 128 + 1) // 2 * 128
+    back = hidden - front
+    ff_plan = [
+        (0, unit, 0, hidden, False), (0, unit, hidden, hidden, False), (1, unit, 0, front, False), (1, unit, front, back, False),
+    ]
+    residual_grad, low, second_part, gate_term, slot_part_grad, qkv_term, decay_term, gate_grad, up_grad, down_front, down_back = backward(
         size, 2, slot, ff_plan,
         (grad_out, gates, attended, normed_two_grad),
         (residual, second_full, out_full, qkv, decay, keep, slot_full, probs, scores, weights, states, decs,
          end_decs),
         (ff_grad, down_grad),
     )
+    down_grad = jnp.concatenate([down_front[:, :front], down_back[:, :back], down_front[:, front:], down_back[:, back:]], axis=1)
     low = low.reshape(rows, width)
     out_grad = dot(low, gated, TN, BF16)
     forget_term = (decay_term * jax.nn.sigmoid(-logit) / TAU).astype(BF16)

time: 896 us -> 874 us (0.975)
  matrix products: 104 us -> 90.7 us
    dot_general x10 -> x8, matrix products: 104 us -> 90.7 us  [dot(): lax.dot_general(left, right, dims, preferred_element_type=F32).astype(dtype)]
    pallas_call x1, Pallas kernels: 237 us -> 225 us  [backward(): pl.pallas_call(functools.partial(backward_kernel, size, plan, slot.levels...]
    unnamed x74 -> x57, local copies, waits for them, and re-layouts: 18 us -> 17.9 us
where the time goes in v6:
time: 874 us; the launch traced here: 863 us
  Pallas kernels  731 us (84%)
  matrix products  90.7 us (10%)
  local copies, waits for them, and re-layouts  32.9 us (4%)
    pallas_call x1, Pallas kernels, backward(): pl.pallas_call(functools.partial(backward_kernel, size, plan, slot.levels...  225 us
    pallas_call x1, Pallas kernels, forward(): pl.pallas_call(functools.partial(forward_kernel, size, plan, slot.levels)...  214 us
    pallas_call x1, Pallas kernels, last(): pl.pallas_call(functools.partial(last_kernel, size, plan), out_shape=outs...  148 us
    pallas_call x1, Pallas kernels, gather(): pl.pallas_call(functools.partial(gather_kernel, size, plan), out_shape=[s...  145 us
    dot_general x8, matrix products, dot(): lax.dot_general(left, right, dims, preferred_element_type=F32).astype(dtype)  90.7 us
    unnamed x57, local copies, waits for them, and re-layouts  17.9 us

profile of v6, /device:TPU:0, one launch (start us, length us, event | category | flops | bytes accessed | tf_op | source)
XLA Modules:
  0.0 863.1 jit_solution(9240254507780167831)
XLA Ops:
  0.7 0.8 reshape.95
  1.5 0.7 pad_bitcast_fusion
  2.1 1.9 stack.42.refs_0_
  4.0 1.8 copy.41
  5.8 145.1 %gather.1 = (bf16[2048,1536]{1,0:T(8,128)(2,1)}, bf16[2048,640]{1,0:T(8,128)(2,1)}, bf16[2048,512]{1,0:T(8,128)(2,1)}, bf16[256,128]{1,0:T(8,128)(2,1)}, bf16[2,...) custom-call(bf16[16,128]{1,0:T(8,128)(2,1)} %stack.42.refs_0_, ...), custom_call_target="tpu_custom_call" | custom-call | tf_op jit(solution)/shard_map/gather/pallas_call | solution.py:1433
  150.9 0.8 slice.78
  151.7 0.1 copy.52
  151.7 0.1 copy.43
  151.8 0.1 select_n.60
  151.9 2.9 exponential-minus-one_negate_fusion
  154.8 0.8 convert.9
  155.7 0.6 slice_bitcast_fusion.1
  156.3 0.8 slice.79
  157.0 0.7 reshape_squeeze.14.refs_4_.refs_10_
  157.7 0.0 copy-done.8
  157.7 1.1 copy.46
  158.8 213.9 %attend_forward.1 = (bf16[1024,512]{1,0:T(8,128)(2,1)}, f32[1024,512]{1,0:T(8,128)}, f32[1024,64]{1,0:T(8,128)}, f32[1024,64]{1,0:T(8,128)}, f32[1024,256]{1,0:T...) custom-call(bf16[1024,1536]{1,0:T(8,128)(2,1)} %get-tuple-element.57, ...), custom_call_target="tpu_custom_call" | custom-call | tf_op jit(solution)/shard_map/attend_forward/pallas_call | solution.py:713
  372.7 19.0 %fusion.8 = f32[1024,2816]{1,0:T(8,128)} fusion(bf16[1024,2048]{1,0:T(8,128)(2,1)} %bitcast.73, bf16[2048,2816]{1,0:T(8,128)(2,1)} %get-tuple-element.65), kind=kOutput, calls=%fused_computation.40 | convolution fusion | flops 11811160064 | bytes 27262976 | tf_op jit(solution)/shard_map/dot_general | solution.py:1451
  391.8 0.0 copy-done
  391.8 12.3 %multiply_convert_fusion.2 = (bf16[1024,1408]{1,0:T(8,128)(2,1)S(1)}, bf16[1024,1408]{1,0:T(8,128)(2,1)}, bf16[1024,1408]{1,0:T(8,128)(2,1)S(1)}) fusion(f32[1024,2816]{1,0:T(8,128)} %fusion.8, bf16[1024,2048]{1,0:T(8,128)(2,1)S(1)} %bitcast.75, bf16[2048,1408]{1,0:T(8,128)(2,1)S(1)} %copy-done), kind=kOutput, calls=%fused_computation.6 | convolution fusion | flops 5927206912 | bytes 30146560 | tf_op jit(solution)/shard_map/dot_general | solution.py:1451
  404.1 8.6 %convolution_convert_fusion.2.refs_21_ = bf16[2048,1408]{1,0:T(8,128)(2,1)} fusion(bf16[1024,2048]{1,0:T(8,128)(2,1)S(1)} %bitcast.76, bf16[1024,1408]{1,0:T(8,128)(2,1)S(1)} %get-tuple-element.131.refs_5_), kind=kOutput, calls=%fused_computation.2 | convolution fusion | flops 5908463616 | bytes 12845056 | tf_op jit(solution)/shard_map/dot_general | solution.py:1451
  412.7 0.0 copy-done.4
  412.7 17.1 %convolution_convert_fusion.refs_20_ = bf16[2048,2816]{1,0:T(8,128)(2,1)} fusion(bf16[1024,2048]{1,0:T(8,128)(2,1)S(1)} %bitcast.74, bf16[1024,1408]{1,0:T(8,128)(2,1)} %get-tuple-element.130, bf16[1024,1408]{1,0:T(8,128)(2,1)S(1)} %get-tuple-element.129), kind=kOutput, calls=%fused_computation | convolution fusion | flops 11828461568 | bytes 21495808 | tf_op jit(solution)/shard_map/dot_general | solution.py:1451
  429.8 0.0 copy-done.21
  429.8 16.3 %convolution_convert_fusion.3 = bf16[1024,2048]{1,0:T(8,128)(2,1)} fusion(bf16[2048,2816]{1,0:T(8,128)(2,1)} %get-tuple-element.65, bf16[1024,1408]{1,0:T(8,128)(2,1)S(1)} %copy-done.21, bf16[1024,1408]{1,0:T(8,128)(2,1)S(1)} %get-tuple-element.129), kind=kOutput, calls=%fused_computation.9 | convolution fusion | flops 11824791552 | bytes 21495808 | tf_op jit(solution)/shard_map/dot_general | solution.py:1451
  446.0 224.6 %attend_backward.1 = (f32[256,2048]{1,0:T(8,128)}, bf16[2,2,256,2048]{3,2,1,0:T(8,128)(2,1)}, f32[1,2048]{1,0:T(1,128)}, bf16[1024,512]{1,0:T(8,128)(2,1)}, f32[...) custom-call(bf16[2,256,2048]{2,1,0:T(8,128)(2,1)} %refs_0_.1, ...), custom_call_target="tpu_custom_call" | custom-call | tf_op jit(solution)/shard_map/attend_backward/pallas_call | solution.py:1146
  670.7 1.2 fusion.6
  671.9 1.1 fusion.7
  673.1 0.1 maximum_bitcast_fusion
  673.2 1.5 copy.51
  674.7 1.6 convert_reduce_fusion
  676.4 0.2 pad_maximum_fusion.3.refs_4_
  676.6 0.0 copy-start.1
  676.6 0.6 copy-done.16
  677.2 4.8 convolution_convert_fusion.4.refs_13_
  682.1 0.0 copy-done.3
  682.1 8.8 %convolution_convert_fusion.1.refs_12_ = bf16[2048,1536]{1,0:T(8,128)(2,1)} fusion(bf16[1024,2048]{1,0:T(8,128)(2,1)S(1)} %copy-done.16, bf16[1024,1536]{1,0:T(8,128)(2,1)S(1)} %copy-done.3), kind=kOutput, calls=%fused_computation.1 | convolution fusion | flops 6445596672 | bytes 13631488 | tf_op jit(solution)/shard_map/dot_general | solution.py:1451
  690.9 3.8 convolution_convert_fusion.5.refs_11_
  694.6 0.1 broadcast_in_dim.37
  694.7 0.1 copy.48
  694.8 0.1 copy.49
  694.9 0.1 broadcast_in_dim.34
  695.0 0.1 broadcast_in_dim.35
  695.1 0.5 broadcast.67
  695.6 0.0 copy-done.15
  695.6 0.7 reduce.7
  696.3 0.1 reshape.99
  696.4 0.7 stack.47.refs_10_
  697.1 147.6 %last.1 = (f32[2,256,2048]{2,1,0:T(8,128)}, bf16[2,256,2048]{2,1,0:T(8,128)(2,1)}, f32[8,128]{1,0:T(8,128)}, f32[128,1024]{1,0:T(8,128)}, f32[128,1024]{1,0:T(8,...) custom-call(bf16[2048,1536]{1,0:T(8,128)(2,1)} %get-tuple-element.55, ...), custom_call_target="tpu_custom_call" | custom-call | tf_op jit(solution)/shard_map/last/pallas_call | solution.py:1285
  844.7 2.0 copy.50
  846.7 1.5 slice_bitcast_fusion
  848.2 0.8 fusion.2
  849.0 0.6 select_n.67
  849.7 1.3 slice_bitcast_fusion.3
  851.0 1.2 slice_bitcast_fusion.5
  852.2 3.2 copy.64
  855.4 2.1 copy.65
  857.5 0.8 copy.66
  858.3 0.8 copy.67
  859.1 0.8 copy.68
  859.9 0.8 copy.69
  860.7 0.0 copy-done.6
  860.7 1.1 copy.70
  861.8 1.1 copy.71
  (46 shorter events, 0.2 us)
Async XLA Ops:
  0.6 157.1 %copy-start.8 = (bf16[2816,128]{1,0:T(8,128)(2,1)S(1)}, bf16[2816,128]{1,0:T(8,128)(2,1)}, u32[]{:S(2)}) copy-start(bf16[2816,128]{1,0:T(8,128)(2,1)} %param.31) | copy-start | bytes 2162692
  372.7 19.1 %copy-start = (bf16[2048,1408]{1,0:T(8,128)(2,1)S(1)}, bf16[2048,1408]{1,0:T(8,128)(2,1)}, u32[]{:S(2)}) copy-start(bf16[2048,1408]{1,0:T(8,128)(2,1)} %get-tuple-element.61.refs_2_) | copy-start | bytes 17301508
  372.7 19.1 %copy-start.19 = (bf16[2,2,256,2048]{3,2,1,0:T(8,128)(2,1)S(1)}, bf16[2,2,256,2048]{3,2,1,0:T(8,128)(2,1)}, u32[]{:S(2)}) copy-start(bf16[2,2,256,2048]{3,2,1,0:T(8,128)(2,1)} %get-tuple-element.63) | copy-start | bytes 12582916
  404.1 8.6 %copy-start.4 = (bf16[1024,1408]{1,0:T(8,128)(2,1)}, bf16[1024,1408]{1,0:T(8,128)(2,1)S(1)}, u32[]{:S(2)}) copy-start(bf16[1024,1408]{1,0:T(8,128)(2,1)S(1)} %get-tuple-element.131.refs_5_) | copy-start | bytes 8650756
  404.1 8.6 %copy-start.18 = (bf16[2,2,256,2048]{3,2,1,0:T(8,128)(2,1)S(1)}, bf16[2,2,256,2048]{3,2,1,0:T(8,128)(2,1)}, u32[]{:S(2)}) copy-start(bf16[2,2,256,2048]{3,2,1,0:T(8,128)(2,1)} %get-tuple-element.64) | copy-start | bytes 12582916
  412.7 17.1 %copy-start.21 = (bf16[1024,1408]{1,0:T(8,128)(2,1)S(1)}, bf16[1024,1408]{1,0:T(8,128)(2,1)}, u32[]{:S(2)}) copy-start(bf16[1024,1408]{1,0:T(8,128)(2,1)} %get-tuple-element.130) | copy-start | bytes 8650756
  670.7 4.0 copy-start.13
  673.0 3.3 copy-start.7
  674.7 2.5 copy-start.16
  676.6 5.5 copy-start.1
  677.2 4.9 copy-start.3
  682.1 8.8 %copy-start.17 = (bf16[2,2,256,2048]{3,2,1,0:T(8,128)(2,1)S(1)}, bf16[2,2,256,2048]{3,2,1,0:T(8,128)(2,1)}, u32[]{:S(2)}) copy-start(bf16[2,2,256,2048]{3,2,1,0:T(8,128)(2,1)} %get-tuple-element.79) | copy-start | bytes 12582916
  682.1 8.8 %copy-start.20 = (bf16[1024,512]{1,0:T(8,128)(2,1)S(1)}, bf16[1024,512]{1,0:T(8,128)(2,1)}, u32[]{:S(2)}) copy-start(bf16[1024,512]{1,0:T(8,128)(2,1)} %get-tuple-element.80) | copy-start | bytes 3145732
  690.9 4.7 copy-start.15
  690.9 5.5 copy-start.14
  849.7 5.7 copy-start.2
  855.4 2.1 copy-start.12
  855.4 2.9 copy-start.11
  855.4 3.7 copy-start.10
  855.4 4.5 copy-start.9
  857.5 3.2 copy-start.6
  857.5 4.3 copy-start.5

commit v7 on v6

--- a/solution.py
+++ b/solution.py
@@ -585,20 +585,20 @@
 
 
 PACE = 1.5
-FORE_STEPS = (0, 6, 0, 4, 0, 2, 0, 0)
+FORE_STEPS = (0, 6, 1, 1, 0, 2, 0, 2)
 
 
 def forward_kernel(size, plan, levels, *refs):
     p = Place(size)
     (qkv, gates, decay, keep, gain, out_w, tokens, gain2, paths, masks, grad_out), refs = take(refs, 11)
     shard_refs, refs = take(refs, sum(len(columns) for _, _, columns in plan))
-    (gated, attended, probs, scores, weights, states, decs, end_dec, residual, normed, grads), refs = take(refs, 11)
+    (gated, attended, probs, scores, weights, states, decs, end_dec, residual, normed, grads, ff), refs = take(refs, 12)
     fulls, refs = take(refs, max(i for i, _, _ in plan) + 1)
     (units, part, total), refs = take(refs, 3)
     (start, *prefix_refs), refs = take(refs, 8)
     fold_refs, refs = take(refs, 5)
     share_sems, refs = take(refs, 2)
-    (swap_sem,), refs = take(refs, 1)
+    (swap_sem, ff_w, ff_tile, ff_sem), refs = take(refs, 4)
     count = paths.shape[1]
     head = gated.shape[1]
     seqs = tokens.shape[0]
@@ -607,7 +607,7 @@
     work = gathers_of(p, plan, shard_refs, fulls, refs)
     for gathered in work:
         gathered.start_x()
-    weave = Weave(gather_ops(work, PACE))
+    weave = Weave(gather_ops(work, PACE)[: -len(work)])
     weave.run(FORE_STEPS[0])
     tail = paths[(levels + 1) * count :, :]
 
@@ -688,8 +688,46 @@
     weave.run(FORE_STEPS[7])
     for r in range(STRIPS):
         share.forward(r)
+    share.finish()
+
+    def complete(gathered):
+        while any(step.func.__self__ is gathered for step in weave.steps):
+            weave.run(1)
+        gathered.finish()
+
+    columns = ff_w.shape[2]
+    tiles = ff.shape[1] // columns
+    up_from = (ff.shape[1] // 2) // columns
+
+    def load(t):
+        return pltpu.make_async_copy(fulls[0].at[:, pl.ds(t * columns, columns)], ff_w.at[t % 2], ff_sem.at[0, t % 2])
+
+    def store(t):
+        return pltpu.make_async_copy(ff_tile.at[t % 2], ff.at[:, pl.ds(t * columns, columns)], ff_sem.at[1, t % 2])
+
+    complete(work[0])
+    load(0).start()
+    for t in range(tiles):
+        load(t).wait()
+        if t + 1 == up_from:
+            complete(work[1])
+        if t + 1 < tiles:
+            load(t + 1).start()
+        if t >= 2:
+            store(t - 2).wait()
+
+        def product(i, nothing, t=t):
+            b, x = i // 2, lax.rem(i, 2)
+            rows = pl.ds(pl.multiple_of(i * count, count), count)
+            ff_tile[t % 2, rows, :] = mm(normed[b, x], ff_w[t % 2], NN)
+            return nothing
+
+        lax.fori_loop(0, 2 * seqs, product, 0)
+        store(t).start()
     weave.rest()
-    share.finish()
+    work[2].finish()
+    store(tiles - 2).wait()
+    store(tiles - 1).wait()
     fold.finish()
     carry.finish()
     move.finish()
@@ -703,18 +741,21 @@
         shape((rows, h), BF16), shape((rows, h), F32), shape((rows, m), F32), shape((rows, m), F32), shape((rows, slot.chunk), F32),
         shape((seqs * (n + 1), m, 2 * h), F32), shape((seqs, n, m, 128), F32), shape((seqs, m, 128), F32),
         shape((block, width), F32), shape((seqs, 2, block, width), BF16), shape((seqs, 2, block, width), BF16),
+        shape((rows, fulls[0][1]), F32),
     ]
+    tile = 256
     scratch = [
         pltpu.VMEM((seqs, n, m, 2 * h), F32), pltpu.VMEM((seqs, 2, block, width), BF16), pltpu.VMEM((seqs, m, 2 * h), F32),
     ]
     scratch += prefix_scratch(seqs, m, 2 * h) + fold_scratch(block, width) + SHARE_SEMS + [pltpu.SemaphoreType.DMA((5,))]
+    scratch += [pltpu.VMEM((2, width, tile), BF16), pltpu.VMEM((2, rows, tile), F32), pltpu.SemaphoreType.DMA((2, 2))]
     for _, _, columns in plan:
         scratch += gather_sems(size // 4, len(columns))
     return pl.pallas_call(
         functools.partial(forward_kernel, size, plan, slot.levels),
         out_shape=outs + [shape(full, BF16) for full in fulls],
         in_specs=[VM] * 10 + [ANY] * (1 + len(shards)),
-        out_specs=[VM] * 10 + [ANY] * (1 + len(fulls)),
+        out_specs=[VM] * 10 + [ANY] * (2 + len(fulls)),
         scratch_shapes=scratch,
         compiler_params=remote_params(number, 60),
         name="attend_forward",
@@ -1494,13 +1535,12 @@
     keep = -jnp.expm1(decay)
     slot = Slots(seqs, 2 * block, head, slots, block)
     ff_plan = [(0, unit, [(0, hidden)]), (0, unit, [(hidden, hidden)]), (1, unit, [(0, hidden)])]
-    (gated, attended, probs, scores, weights, states, decs, end_decs, residual, normed_two, gout, ff_full, down_full) = forward(
+    (gated, attended, probs, scores, weights, states, decs, end_decs, residual, normed_two, gout, ff, ff_full, down_full) = forward(
         size, 1, slot, ff_plan, [(width, 2 * hidden), (width, hidden)], qkv, gates, decay, keep, slot_full, out_full, tokens,
         second_full, grad_out, (gate_weight, up_weight, down_weight.T),
     )
     shape = (seqs, 2, block, width)
     normed_two = normed_two.reshape(rows, width)
-    ff = dot(normed_two, ff_full, NN)
     ff_gate, ff_up = ff[:, :hidden], ff[:, hidden:]
     sig = jax.nn.sigmoid(ff_gate)
     activated = (ff_gate * sig * ff_up).astype(BF16)

time: 874 us -> 858 us (0.982)
  matrix products: 90.7 us -> 74.6 us
    dot_general x8 -> x7, matrix products: 90.7 us -> 74.6 us  [dot(): lax.dot_general(left, right, dims, preferred_element_type=F32).astype(dtype)]
    unnamed x57 -> x55, local copies, waits for them, and re-layouts: 17.9 us -> 17.9 us
where the time goes in v7:
time: 858 us; the launch traced here: 847 us
  Pallas kernels  731 us (85%)
  matrix products  74.6 us (9%)
  local copies, waits for them, and re-layouts  32.9 us (4%)
    pallas_call x1, Pallas kernels, backward(): pl.pallas_call(functools.partial(backward_kernel, size, plan, slot.levels...  225 us
    pallas_call x1, Pallas kernels, forward(): pl.pallas_call(functools.partial(forward_kernel, size, plan, slot.levels)...  214 us
    pallas_call x1, Pallas kernels, last(): pl.pallas_call(functools.partial(last_kernel, size, plan), out_shape=outs...  148 us
    pallas_call x1, Pallas kernels, gather(): pl.pallas_call(functools.partial(gather_kernel, size, plan), out_shape=[s...  145 us
    dot_general x7, matrix products, dot(): lax.dot_general(left, right, dims, preferred_element_type=F32).astype(dtype)  74.6 us
    unnamed x55, local copies, waits for them, and re-layouts  17.9 us

profile of v7, /device:TPU:0, one launch (start us, length us, event | category | flops | bytes accessed | tf_op | source)
XLA Modules:
  0.0 846.8 jit_solution(17079416517726613875)
XLA Ops:
  0.6 0.0 copy-start.7
  0.7 0.8 reshape.95
  1.5 0.7 pad_bitcast_fusion
  2.1 1.9 stack.42.refs_0_
  4.0 1.8 copy.41
  5.8 145.1 %gather.1 = (bf16[2048,1536]{1,0:T(8,128)(2,1)}, bf16[2048,640]{1,0:T(8,128)(2,1)}, bf16[2048,512]{1,0:T(8,128)(2,1)}, bf16[256,128]{1,0:T(8,128)(2,1)}, bf16[2,...) custom-call(bf16[16,128]{1,0:T(8,128)(2,1)} %stack.42.refs_0_, ...), custom_call_target="tpu_custom_call" | custom-call | tf_op jit(solution)/shard_map/gather/pallas_call | solution.py:1474
  150.9 0.8 slice.78
  151.6 0.1 copy.52
  151.7 0.1 copy.43
  151.8 0.1 select_n.60
  151.9 2.8 exponential-minus-one_negate_fusion
  154.6 0.8 convert.9
  155.5 0.6 slice_bitcast_fusion.1
  156.1 0.8 slice.79
  156.9 0.7 reshape_squeeze.14.refs_4_.refs_10_
  157.5 0.0 copy-done.7
  157.5 1.1 copy.46
  158.7 213.9 %attend_forward.1 = (bf16[1024,512]{1,0:T(8,128)(2,1)}, f32[1024,512]{1,0:T(8,128)}, f32[1024,64]{1,0:T(8,128)}, f32[1024,64]{1,0:T(8,128)}, f32[1024,256]{1,0:T...) custom-call(bf16[1024,1536]{1,0:T(8,128)(2,1)} %get-tuple-element.58, ...), custom_call_target="tpu_custom_call" | custom-call | tf_op jit(solution)/shard_map/attend_forward/pallas_call | solution.py:754
  372.6 0.0 copy-start.18
  372.6 15.5 %multiply_convert_fusion.2 = (bf16[1024,1408]{1,0:T(8,128)(2,1)S(1)}, bf16[1024,1408]{1,0:T(8,128)(2,1)}, bf16[1024,1408]{1,0:T(8,128)(2,1)S(1)}) fusion(f32[1024,2816]{1,0:T(8,128)} %get-tuple-element.65, bf16[1024,2048]{1,0:T(8,128)(2,1)} %bitcast.72, bf16[2048,1408]{1,0:T(8,128)(2,1)} %get-tuple-element.62.refs_2_), kind=kOutput, calls=%fused_computation.6 | convolution fusion | flops 5927206912 | bytes 30146560 | tf_op jit(solution)/shard_map/dot_general | solution.py:1492
  388.0 0.0 copy-done.18
  388.1 8.6 %convolution_convert_fusion.2.refs_21_ = bf16[2048,1408]{1,0:T(8,128)(2,1)} fusion(bf16[1024,2048]{1,0:T(8,128)(2,1)S(1)} %bitcast.73, bf16[1024,1408]{1,0:T(8,128)(2,1)S(1)} %get-tuple-element.133.refs_5_), kind=kOutput, calls=%fused_computation.2 | convolution fusion | flops 5908463616 | bytes 12845056 | tf_op jit(solution)/shard_map/dot_general | solution.py:1492
  396.7 0.0 copy-done.3
  396.7 16.6 %convolution_convert_fusion.refs_20_ = bf16[2048,2816]{1,0:T(8,128)(2,1)} fusion(bf16[1024,2048]{1,0:T(8,128)(2,1)S(1)} %bitcast.71, bf16[1024,1408]{1,0:T(8,128)(2,1)} %get-tuple-element.132, bf16[1024,1408]{1,0:T(8,128)(2,1)S(1)} %get-tuple-element.131), kind=kOutput, calls=%fused_computation | convolution fusion | flops 11828461568 | bytes 21495808 | tf_op jit(solution)/shard_map/dot_general | solution.py:1492
  413.2 16.4 %convolution_convert_fusion.3 = bf16[1024,2048]{1,0:T(8,128)(2,1)} fusion(bf16[2048,2816]{1,0:T(8,128)(2,1)} %get-tuple-element.66, bf16[1024,1408]{1,0:T(8,128)(2,1)S(1)} %copy-done.20, bf16[1024,1408]{1,0:T(8,128)(2,1)S(1)} %get-tuple-element.131), kind=kOutput, calls=%fused_computation.9 | convolution fusion | flops 11824791552 | bytes 21495808 | tf_op jit(solution)/shard_map/dot_general | solution.py:1492
  429.6 224.5 %attend_backward.1 = (f32[256,2048]{1,0:T(8,128)}, bf16[2,2,256,2048]{3,2,1,0:T(8,128)(2,1)}, f32[1,2048]{1,0:T(1,128)}, bf16[1024,512]{1,0:T(8,128)(2,1)}, f32[...) custom-call(bf16[2,256,2048]{2,1,0:T(8,128)(2,1)} %refs_0_.1, ...), custom_call_target="tpu_custom_call" | custom-call | tf_op jit(solution)/shard_map/attend_backward/pallas_call | solution.py:1187
  654.2 1.2 fusion.6
  655.4 1.1 fusion.7
  656.5 0.1 maximum_bitcast_fusion
  656.6 1.5 copy.51
  658.2 1.6 convert_reduce_fusion
  659.9 0.2 pad_maximum_fusion.3.refs_4_
  660.1 0.0 copy-start
  660.1 0.6 copy-done.15
  660.7 5.0 convolution_convert_fusion.4.refs_13_
  665.7 8.8 %convolution_convert_fusion.1.refs_12_ = bf16[2048,1536]{1,0:T(8,128)(2,1)} fusion(bf16[1024,2048]{1,0:T(8,128)(2,1)S(1)} %copy-done.15, bf16[1024,1536]{1,0:T(8,128)(2,1)S(1)} %copy-done.2), kind=kOutput, calls=%fused_computation.1 | convolution fusion | flops 6445596672 | bytes 13631488 | tf_op jit(solution)/shard_map/dot_general | solution.py:1492
  674.5 3.8 convolution_convert_fusion.5.refs_11_
  678.3 0.1 broadcast_in_dim.37
  678.4 0.1 copy.48
  678.4 0.1 copy.49
  678.5 0.1 broadcast_in_dim.34
  678.6 0.1 broadcast_in_dim.35
  678.7 0.5 broadcast.67
  679.2 0.7 reduce.7
  679.9 0.1 reshape.99
  680.0 0.7 stack.47.refs_10_
  680.7 147.6 %last.1 = (f32[2,256,2048]{2,1,0:T(8,128)}, bf16[2,256,2048]{2,1,0:T(8,128)(2,1)}, f32[8,128]{1,0:T(8,128)}, f32[128,1024]{1,0:T(8,128)}, f32[128,1024]{1,0:T(8,...) custom-call(bf16[2048,1536]{1,0:T(8,128)(2,1)} %get-tuple-element.56, ...), custom_call_target="tpu_custom_call" | custom-call | tf_op jit(solution)/shard_map/last/pallas_call | solution.py:1326
  828.4 2.0 copy.50
  830.4 1.5 slice_bitcast_fusion
  831.9 0.8 fusion.2
  832.7 0.6 select_n.67
  833.4 1.3 slice_bitcast_fusion.3
  834.7 1.2 slice_bitcast_fusion.5
  835.9 3.2 copy.64
  839.1 0.0 copy-start.8
  839.1 2.1 copy.65
  841.2 0.8 copy.66
  842.0 0.8 copy.67
  842.8 0.0 copy-done.9
  842.8 0.8 copy.68
  843.6 0.8 copy.69
  844.4 1.1 copy.70
  845.5 0.0 copy-done.4
  845.5 1.1 copy.71
  (43 shorter events, 0.2 us)
Async XLA Ops:
  0.6 156.9 %copy-start.7 = (bf16[2816,128]{1,0:T(8,128)(2,1)S(1)}, bf16[2816,128]{1,0:T(8,128)(2,1)}, u32[]{:S(2)}) copy-start(bf16[2816,128]{1,0:T(8,128)(2,1)} %param.31) | copy-start | bytes 2162692
  372.6 15.5 %copy-start.18 = (bf16[2,2,256,2048]{3,2,1,0:T(8,128)(2,1)S(1)}, bf16[2,2,256,2048]{3,2,1,0:T(8,128)(2,1)}, u32[]{:S(2)}) copy-start(bf16[2,2,256,2048]{3,2,1,0:T(8,128)(2,1)} %get-tuple-element.64) | copy-start | bytes 12582916
  388.0 8.6 %copy-start.3 = (bf16[1024,1408]{1,0:T(8,128)(2,1)}, bf16[1024,1408]{1,0:T(8,128)(2,1)S(1)}, u32[]{:S(2)}) copy-start(bf16[1024,1408]{1,0:T(8,128)(2,1)S(1)} %get-tuple-element.133.refs_5_) | copy-start | bytes 8650756
  388.0 8.6 %copy-start.17 = (bf16[2,2,256,2048]{3,2,1,0:T(8,128)(2,1)S(1)}, bf16[2,2,256,2048]{3,2,1,0:T(8,128)(2,1)}, u32[]{:S(2)}) copy-start(bf16[2,2,256,2048]{3,2,1,0:T(8,128)(2,1)} %get-tuple-element.74) | copy-start | bytes 12582916
  396.7 16.6 %copy-start.20 = (bf16[1024,1408]{1,0:T(8,128)(2,1)S(1)}, bf16[1024,1408]{1,0:T(8,128)(2,1)}, u32[]{:S(2)}) copy-start(bf16[1024,1408]{1,0:T(8,128)(2,1)} %get-tuple-element.132) | copy-start | bytes 8650756
  654.2 4.0 copy-start.12
  656.5 3.3 copy-start.6
  658.2 2.5 copy-start.15
  660.1 5.6 copy-start
  660.7 5.0 copy-start.2
  665.7 8.8 %copy-start.16 = (bf16[2,2,256,2048]{3,2,1,0:T(8,128)(2,1)S(1)}, bf16[2,2,256,2048]{3,2,1,0:T(8,128)(2,1)}, u32[]{:S(2)}) copy-start(bf16[2,2,256,2048]{3,2,1,0:T(8,128)(2,1)} %get-tuple-element.81) | copy-start | bytes 12582916
  665.7 8.8 %copy-start.19 = (bf16[1024,512]{1,0:T(8,128)(2,1)S(1)}, bf16[1024,512]{1,0:T(8,128)(2,1)}, u32[]{:S(2)}) copy-start(bf16[1024,512]{1,0:T(8,128)(2,1)} %get-tuple-element.82) | copy-start | bytes 3145732
  674.5 4.7 copy-start.14
  674.5 5.5 copy-start.13
  833.4 5.7 copy-start.1
  839.0 2.1 copy-start.11
  839.1 2.9 copy-start.10
  839.1 3.7 copy-start.9
  839.1 4.5 copy-start.8
  841.2 3.2 copy-start.5
  841.2 4.3 copy-start.4
